TPU v7x, 32 devices: a whole 2x2x4 slice. The times are simulated.
32 devices in a mesh: ta: 2 (over x), tp: 16 (over z, y, core).
Axes of the slice: x: 2, y: 2, z: 4, core: 2. Of those that a mesh axis runs over, the one named last changes fastest.
Arguments:
- green: float32 [2, 2, 16, 16, 512], P(None, None, 'tp', None, 'ta'), may hold values from -5 to 5
- hamiltonian: float32 [32, 32], replicated, may hold values from -1 to 1
- interaction: float32 [32, 32], replicated, may hold values from 0.4 to 1.2
Outputs:
- green_next: float32 [2, 2, 16, 16, 512], P(None, None, 'tp', None, 'ta')
All inputs are finite; a program needn't handle non-finite values.
Results may differ from a plain program's by a relative error of at most 0.0091.
Values may be sent and summed in bfloat16 or wider, within the bound.
No kernel may reach another device: no remote copies, remote signals or barrier semaphores. Data moves between devices by JAX's collectives and lax.ppermute only.
A program may use at most 64 MiB of HBM per device.

v0:
```python
import math

import jax
import jax.numpy as jnp
from jax import lax
from jax.sharding import PartitionSpec as P

NO = 32
ITERS = 2


highest = lax.Precision.HIGHEST


def shifted(block, axis, distance):
    devices = range(lax.axis_size(axis))
    route = [(i - distance, i) for i in devices if i - distance in devices]
    return lax.ppermute(block, axis, route)


def half_dot(left_side, right_side):
    return jnp.dot(left_side, right_side, preferred_element_type=jnp.float32)


def accumulate(left_side, right_side):
    product_real = half_dot(left_side[0], right_side[0]) - half_dot(left_side[1], right_side[1])
    product_imag = half_dot(left_side[0], right_side[1]) + half_dot(left_side[1], right_side[0])
    return (product_real, product_imag)


def self_energy(values, mirror_part, weights):
    real_square = values[0] * values[0] - values[1] * values[1]
    imag_square = 2.0 * values[0] * values[1]
    sigma_real = weights * (real_square * mirror_part[0] - imag_square * mirror_part[1])
    sigma_imag = weights * (real_square * mirror_part[1] + imag_square * mirror_part[0])
    return jnp.stack([sigma_real, sigma_imag])


def shards(green, hamiltonian, interaction):
    tp_count = lax.axis_size("tp")
    ta_place = lax.axis_index("ta")
    tp_place = lax.axis_index("tp")
    groups = green.shape[1]
    stripe = green.shape[3]
    block_rows = green.shape[4]
    columns = groups * stripe
    factor = 1.0 / math.sqrt(2 * block_rows)
    current = green[:, :, 0].reshape(2, columns, block_rows)
    squared = interaction * interaction
    column_global = (
        jnp.arange(groups, dtype=jnp.int32)[:, None] * tp_count + tp_place
    ) * stripe + jnp.arange(stripe, dtype=jnp.int32)[None, :]
    column_orbital = (column_global % NO).reshape(columns)
    onehot = (column_orbital[:, None] == jnp.arange(NO, dtype=jnp.int32)[None, :]).astype(
        jnp.float32
    )
    lookup_table = jnp.dot(onehot, squared.T, precision=highest)
    coupling = jnp.tile(lookup_table, (1, block_rows // NO))
    row_time = jnp.arange(block_rows, dtype=jnp.int32) // NO
    column_time = (tp_place * stripe + jnp.arange(stripe, dtype=jnp.int32)) // NO
    is_later = column_time[:, None] > row_time[None, :]
    block_width = math.gcd(block_rows, 128)
    blocked = jnp.kron(jnp.eye(block_width // NO, dtype=jnp.float32), hamiltonian.T)
    zero_half = jnp.zeros((), jnp.bfloat16)
    for iteration in range(ITERS):
        rounded = current.astype(jnp.bfloat16)
        outgoing = rounded.reshape(2, groups, stripe, tp_count, stripe)
        previous = shifted(rounded, "ta", 1)
        earliest = shifted(rounded, "ta", 2)
        hamilton_term = jnp.dot(
            current.reshape(-1, block_width), blocked, precision=highest
        ).reshape(2, columns, block_rows)
        selected = []
        nearby = jnp.stack(
            [
                lax.dynamic_index_in_dim(
                    outgoing, jnp.minimum(ta_place + step_ahead, groups - 1), 1, keepdims=False
                )
                for step_ahead in range(3)
            ],
            1,
        )
        spread = lax.all_to_all(nearby, "tp", split_axis=3, concat_axis=3, tiled=True)
        from_one = shifted(spread[:, 1], "ta", 1)
        from_two = shifted(spread[:, 2], "ta", 2)
        received = (from_two, from_one, spread[:, 0])
        by_current = current.reshape(2, groups, stripe, block_rows)
        for window_index in range(3):
            group_pick = jnp.maximum(ta_place - 2 + window_index, 0)
            own_part = lax.dynamic_index_in_dim(by_current, group_pick, 1, keepdims=False)
            flipped = (
                jnp.transpose(received[window_index], (0, 3, 2, 1))
                .reshape(2, stripe, block_rows)
                .astype(jnp.float32)
            )
            selected.append(self_energy(own_part, flipped, coupling[:stripe]))
        oldest = jnp.where(is_later[None], selected[0], 0.0)
        middle = selected[1]
        newest = jnp.where(is_later[None], 0.0, selected[2])
        sending = jnp.stack([oldest + newest, middle], 1).astype(jnp.bfloat16)[:, :, None]
        portion = lax.all_gather(sending, "tp", axis=2, tiled=True)
        row_count = portion.shape[2] * stripe
        arriving_time = jnp.arange(row_count, dtype=jnp.int32) // NO
        later_here = (arriving_time[:, None] > row_time[None, :])[None]
        merged = portion[:, 0].reshape(2, row_count, block_rows)
        recent = portion[:, 1].reshape(2, row_count, block_rows)
        right_side = jnp.concatenate(
            [
                jnp.where(later_here, merged, zero_half),
                recent,
                jnp.where(later_here, zero_half, merged),
            ],
            1,
        )
        memory = accumulate(
            jnp.concatenate([source for source in (earliest, previous, rounded)], 2), right_side
        )
        next_real = current[0] + 0.5 * (hamilton_term[1] + factor * memory[1])
        next_imag = current[1] - 0.5 * (hamilton_term[0] + factor * memory[0])
        current = jnp.stack([next_real, next_imag])
    return current.reshape(2, groups, 1, stripe, block_rows)


def solution(mesh):
    in_specs = (P(None, None, "tp", None, "ta"), P(), P())
    out_specs = P(None, None, "tp", None, "ta")
    return jax.shard_map(shards, mesh=mesh, in_specs=in_specs, out_specs=out_specs, check_vma=False)
```

profile of v0, /device:TPU:0, one launch (start us, length us, event | category | flops | bytes accessed | tf_op | source)
XLA Modules:
  0.0 90.4 jit_solution(7145150270465288988)
XLA Ops:
  0.0 0.8 convert_element_type.87
  0.8 0.6 collective-permute-start
  1.5 4.9 %collective-permute-start.1 = (bf16[2,32,256]{2,1,0:T(8,128)(2,1)S(1)}, bf16[2,32,256]{2,1,0:T(8,128)(2,1)S(1)}, u32[]{:S(2)}, u32[]{:S(2)}) collective-permute-start(bf16[2,32,256]{2,1,0:T(8,128)(2,1)S(1)} %bitcast.318), channel_id=1, source_target_pairs={{0,16},{1,17},{2,18},{3,19},{4,20},{5,21},{6,22},{7,23},{8,24},{9,... | collective-permute-start | bytes 98312 | tf_op jit(solution)/shard_map/ppermute | solution.py:18
  6.4 0.2 convert_element_type.89
  6.7 0.1 pad_maximum_fusion.2
  6.8 0.4 copy.64
  7.2 1.0 %reshape.876 = bf16[16,2,768]{2,1,0:T(2,128)(2,1)} reshape(bf16[16,3,2,16,16]{4,3,2,1,0:T(8,128)(2,1)S(1)} %bitcast.300) | data formatting | bytes 98304
  8.2 6.1 %all-to-all-start = ((bf16[16,2,768]{2,1,0:T(2,128)(2,1)}), bf16[16,2,768]{2,1,0:T(2,128)(2,1)S(1)}, u32[]{:S(2)}, u32[]{:S(2)}) async-start(bf16[16,2,768]{2,1,0:T(2,128)(2,1)} %reshape.876), calls=%async_computation | async-start | bytes 98304 | tf_op jit(solution)/shard_map/all_to_all | solution.py:83
  14.5 0.1 broadcast_compare_fusion
  14.7 0.1 broadcast_multiply_fusion
  14.8 0.2 mul.527
  15.0 0.2 convolution_bitcast_fusion
  15.2 0.2 fusion.64
  15.7 5.4 %all-to-all-done = bf16[16,2,768]{2,1,0:T(2,128)(2,1)S(1)} async-done(((bf16[16,2,768]{2,1,0:T(2,128)(2,1)}), bf16[16,2,768]{2,1,0:T(2,128)(2,1)S(1)}, u32[]{:S(2)}, u32[]{:S(2)}) %all-to-all-start) | async-done | bytes 49184 | tf_op jit(solution)/shard_map/all_to_all | solution.py:83
  21.0 0.3 reshape.877
  21.4 0.7 collective-permute-start.2
  22.1 1.3 %collective-permute-start.3 = (bf16[2,16,16,16]{1,3,0,2:T(8,128)(2,1)S(1)}, bf16[2,16,16,16]{1,3,0,2:T(8,128)(2,1)S(1)}, u32[]{:S(2)}, u32[]{:S(2)}) collective-permute-start(bf16[2,16,16,16]{1,3,0,2:T(8,128)(2,1)S(1)} %get-tuple-element.13), channel_id=1, source_target_pairs={{0,16},{1,17},{2,18},{3,19},{4,20},{5,21},{6,22},{7,23},{8,24},{9,... | collective-permute-start | bytes 49160 | tf_op jit(solution)/shard_map/ppermute | solution.py:18
  23.5 0.1 slice.268
  23.6 0.1 slice.270
  23.8 0.1 slice.261
  24.0 0.1 slice.263
  24.1 2.1 %collective-permute-done.3 = bf16[2,16,16,16]{1,3,0,2:T(8,128)(2,1)S(1)} collective-permute-done((bf16[2,16,16,16]{1,3,0,2:T(8,128)(2,1)S(1)}, bf16[2,16,16,16]{1,3,0,2:T(8,128)(2,1)S(1)}, u32[]{:S(2)}, u32[]{:S(2)}) %collective-permute-start.3) | collective-permute-done | bytes 16416 | tf_op jit(solution)/shard_map/ppermute | solution.py:18
  26.3 0.1 slice.275
  26.4 0.1 slice.277
  26.6 19.4 %all_gather.6 = bf16[2,2,16,16,256]{4,3,2,0,1:T(8,128)(2,1)S(1)} all-gather(bf16[2,2,1,16,256]{4,3,2,0,1:T(8,128)(2,1)S(1)} %pad_maximum_fusion.8), channel_id=1, replica_groups=mesh['ta'=2,'tp'=16] {'tp'}, dimensions={2}, use_global_device_ids=true | all-gather | bytes 557056 | tf_op jit(solution)/shard_map/all_gather | solution.py:101
  46.2 0.1 fusion.16
  46.4 0.2 fusion.17
  46.6 0.2 fusion.83
  46.8 0.2 fusion.84
  47.0 0.7 collective-permute-start.4
  47.7 4.4 %collective-permute-start.5 = (bf16[2,32,256]{2,1,0:T(8,128)(2,1)S(1)}, bf16[2,32,256]{2,1,0:T(8,128)(2,1)S(1)}, u32[]{:S(2)}, u32[]{:S(2)}) collective-permute-start(bf16[2,32,256]{2,1,0:T(8,128)(2,1)S(1)} %fusion.71), channel_id=1, source_target_pairs={{0,16},{1,17},{2,18},{3,19},{4,20},{5,21},{6,22},{7,23},{8,24},{9,... | collective-permute-start | bytes 98312 | tf_op jit(solution)/shard_map/ppermute | solution.py:18
  52.1 0.1 stack.125
  52.3 0.1 stack.126
  52.5 0.1 fusion.85
  52.6 1.0 %reshape.878 = bf16[16,2,768]{2,1,0:T(2,128)(2,1)} reshape(bf16[16,2,3,16,16]{4,3,2,1,0:T(8,128)(2,1)S(1)} %fusion.85) | data formatting | bytes 98304
  53.6 3.5 %all-to-all-start.1 = ((bf16[16,2,768]{2,1,0:T(2,128)(2,1)}), bf16[16,2,768]{2,1,0:T(2,128)(2,1)S(1)}, u32[]{:S(2)}, u32[]{:S(2)}) async-start(bf16[16,2,768]{2,1,0:T(2,128)(2,1)} %reshape.878), calls=%async_computation.1 | async-start | bytes 98304 | tf_op jit(solution)/shard_map/all_to_all | solution.py:83
  57.1 0.2 fusion.86
  57.5 6.4 %all-to-all-done.1 = bf16[16,2,768]{2,1,0:T(2,128)(2,1)S(1)} async-done(((bf16[16,2,768]{2,1,0:T(2,128)(2,1)}), bf16[16,2,768]{2,1,0:T(2,128)(2,1)S(1)}, u32[]{:S(2)}, u32[]{:S(2)}) %all-to-all-start.1) | async-done | bytes 49184 | tf_op jit(solution)/shard_map/all_to_all | solution.py:83
  63.8 0.3 reshape.879
  64.2 0.7 collective-permute-start.6
  64.9 1.3 %collective-permute-start.7 = (bf16[2,16,16,16]{3,1,0,2:T(8,128)(2,1)S(1)}, bf16[2,16,16,16]{3,1,0,2:T(8,128)(2,1)S(1)}, u32[]{:S(2)}, u32[]{:S(2)}) collective-permute-start(bf16[2,16,16,16]{3,1,0,2:T(8,128)(2,1)S(1)} %get-tuple-element.10), channel_id=1, source_target_pairs={{0,16},{1,17},{2,18},{3,19},{4,20},{5,21},{6,22},{7,23},{8,24},{9,... | collective-permute-start | bytes 49160 | tf_op jit(solution)/shard_map/ppermute | solution.py:18
  66.6 2.4 %collective-permute-done.7 = bf16[2,16,16,16]{3,1,0,2:T(8,128)(2,1)S(1)} collective-permute-done((bf16[2,16,16,16]{3,1,0,2:T(8,128)(2,1)S(1)}, bf16[2,16,16,16]{3,1,0,2:T(8,128)(2,1)S(1)}, u32[]{:S(2)}, u32[]{:S(2)}) %collective-permute-start.7) | collective-permute-done | bytes 16416 | tf_op jit(solution)/shard_map/ppermute | solution.py:18
  69.3 19.5 %all_gather.7 = bf16[2,2,16,16,256]{4,3,0,2,1:T(8,128)(2,1)S(1)} all-gather(bf16[2,2,1,16,256]{4,3,0,2,1:T(8,128)(2,1)S(1)} %pad_maximum_fusion.9), channel_id=1, replica_groups=mesh['ta'=2,'tp'=16] {'tp'}, dimensions={2}, use_global_device_ids=true | all-gather | bytes 557056 | tf_op jit(solution)/shard_map/all_gather | solution.py:101
  89.0 0.1 fusion.18
  89.1 0.2 fusion.19
  89.3 0.2 fusion.7
  89.6 0.2 fusion.3
  89.8 0.6 pad_maximum_fusion.7
  (81 shorter events, 2.1 us)
Async XLA Ops:
  0.8 14.8 %collective-permute-start = (bf16[2,32,256]{2,1,0:T(8,128)(2,1)S(1)}, bf16[2,32,256]{2,1,0:T(8,128)(2,1)S(1)}, u32[]{:S(2)}, u32[]{:S(2)}) collective-permute-start(bf16[2,32,256]{2,1,0:T(8,128)(2,1)S(1)} %bitcast.317), channel_id=1, source_target_pairs={} | collective-permute-start | bytes 98312 | tf_op jit(solution)/shard_map/ppermute | solution.py:18
  1.5 14.1 %collective-permute-start.1 = (bf16[2,32,256]{2,1,0:T(8,128)(2,1)S(1)}, bf16[2,32,256]{2,1,0:T(8,128)(2,1)S(1)}, u32[]{:S(2)}, u32[]{:S(2)}) collective-permute-start(bf16[2,32,256]{2,1,0:T(8,128)(2,1)S(1)} %bitcast.318), channel_id=1, source_target_pairs={{0,16},{1,17},{2,18},{3,19},{4,20},{5,21},{6,22},{7,23},{8,24},{9,... | collective-permute-start | bytes 98312 | tf_op jit(solution)/shard_map/ppermute | solution.py:18
  6.8 7.5 %copy-start = (f32[2,2,1,16,256]{4,3,2,1,0:T(8,128)S(1)}, f32[2,2,1,16,256]{4,3,2,1,0:T(8,128)}, u32[]{:S(2)}) copy-start(f32[2,2,1,16,256]{4,3,2,1,0:T(8,128)} %param.3) | copy-start | bytes 196612
  6.8 7.9 %copy-start.1 = (f32[32,32]{1,0:T(8,128)S(1)}, f32[32,32]{1,0:T(8,128)}, u32[]{:S(2)}) copy-start(f32[32,32]{1,0:T(8,128)} %param.4) | copy-start | bytes 12292
  8.2 7.0 %copy-start.2 = (f32[32,32]{1,0:T(8,128)S(1)}, f32[32,32]{1,0:T(8,128)}, u32[]{:S(2)}) copy-start(f32[32,32]{1,0:T(8,128)} %param.5) | copy-start | bytes 12292
  8.2 12.8 %all-to-all-start = ((bf16[16,2,768]{2,1,0:T(2,128)(2,1)}), bf16[16,2,768]{2,1,0:T(2,128)(2,1)S(1)}, u32[]{:S(2)}, u32[]{:S(2)}) async-start(bf16[16,2,768]{2,1,0:T(2,128)(2,1)} %reshape.876), calls=%async_computation | async-start | bytes 98304 | tf_op jit(solution)/shard_map/all_to_all | solution.py:83
  21.4 2.3 %collective-permute-start.2 = (bf16[2,16,16,16]{1,3,0,2:T(8,128)(2,1)S(1)}, bf16[2,16,16,16]{1,3,0,2:T(8,128)(2,1)S(1)}, u32[]{:S(2)}, u32[]{:S(2)}) collective-permute-start(bf16[2,16,16,16]{1,3,0,2:T(8,128)(2,1)S(1)} %get-tuple-element.12), channel_id=1, source_target_pairs={} | collective-permute-start | bytes 49160 | tf_op jit(solution)/shard_map/ppermute | solution.py:18
  22.1 4.1 %collective-permute-start.3 = (bf16[2,16,16,16]{1,3,0,2:T(8,128)(2,1)S(1)}, bf16[2,16,16,16]{1,3,0,2:T(8,128)(2,1)S(1)}, u32[]{:S(2)}, u32[]{:S(2)}) collective-permute-start(bf16[2,16,16,16]{1,3,0,2:T(8,128)(2,1)S(1)} %get-tuple-element.13), channel_id=1, source_target_pairs={{0,16},{1,17},{2,18},{3,19},{4,20},{5,21},{6,22},{7,23},{8,24},{9,... | collective-permute-start | bytes 49160 | tf_op jit(solution)/shard_map/ppermute | solution.py:18
  47.0 10.4 %collective-permute-start.4 = (bf16[2,32,256]{2,1,0:T(8,128)(2,1)S(1)}, bf16[2,32,256]{2,1,0:T(8,128)(2,1)S(1)}, u32[]{:S(2)}, u32[]{:S(2)}) collective-permute-start(bf16[2,32,256]{2,1,0:T(8,128)(2,1)S(1)} %fusion.71), channel_id=1, source_target_pairs={} | collective-permute-start | bytes 98312 | tf_op jit(solution)/shard_map/ppermute | solution.py:18
  47.7 9.7 %collective-permute-start.5 = (bf16[2,32,256]{2,1,0:T(8,128)(2,1)S(1)}, bf16[2,32,256]{2,1,0:T(8,128)(2,1)S(1)}, u32[]{:S(2)}, u32[]{:S(2)}) collective-permute-start(bf16[2,32,256]{2,1,0:T(8,128)(2,1)S(1)} %fusion.71), channel_id=1, source_target_pairs={{0,16},{1,17},{2,18},{3,19},{4,20},{5,21},{6,22},{7,23},{8,24},{9,... | collective-permute-start | bytes 98312 | tf_op jit(solution)/shard_map/ppermute | solution.py:18
  53.6 10.2 %all-to-all-start.1 = ((bf16[16,2,768]{2,1,0:T(2,128)(2,1)}), bf16[16,2,768]{2,1,0:T(2,128)(2,1)S(1)}, u32[]{:S(2)}, u32[]{:S(2)}) async-start(bf16[16,2,768]{2,1,0:T(2,128)(2,1)} %reshape.878), calls=%async_computation.1 | async-start | bytes 98304 | tf_op jit(solution)/shard_map/all_to_all | solution.py:83
  64.2 2.1 %collective-permute-start.6 = (bf16[2,16,16,16]{3,1,0,2:T(8,128)(2,1)S(1)}, bf16[2,16,16,16]{3,1,0,2:T(8,128)(2,1)S(1)}, u32[]{:S(2)}, u32[]{:S(2)}) collective-permute-start(bf16[2,16,16,16]{3,1,0,2:T(8,128)(2,1)S(1)} %get-tuple-element.9), channel_id=1, source_target_pairs={} | collective-permute-start | bytes 49160 | tf_op jit(solution)/shard_map/ppermute | solution.py:18
  64.9 4.1 %collective-permute-start.7 = (bf16[2,16,16,16]{3,1,0,2:T(8,128)(2,1)S(1)}, bf16[2,16,16,16]{3,1,0,2:T(8,128)(2,1)S(1)}, u32[]{:S(2)}, u32[]{:S(2)}) collective-permute-start(bf16[2,16,16,16]{3,1,0,2:T(8,128)(2,1)S(1)} %get-tuple-element.10), channel_id=1, source_target_pairs={{0,16},{1,17},{2,18},{3,19},{4,20},{5,21},{6,22},{7,23},{8,24},{9,... | collective-permute-start | bytes 49160 | tf_op jit(solution)/shard_map/ppermute | solution.py:18
where the time goes:
time: 90.9 us; the launch traced here: 90.4 us
  blocking collectives  38.9 us (43%)
  starting transfers between devices  24 us (26%)
  waiting for transfers between devices  16.3 us (18%)
  local copies, waits for them, and re-layouts  5.72 us (6%)
  other arithmetic  2.58 us (3%)
  matrix products  2.07 us (2%)
    all_gather x2, blocking collectives, shards(): portion = lax.all_gather(sending, 'tp', axis=2, tiled=True)  38.9 us
    ppermute x8, starting transfers between devices, shifted(): return lax.ppermute(block, axis, route)  14.5 us
    all_to_all x2, waiting for transfers between devices, shards(): lax.all_to_all(nearby, 'tp', split_axis=3, concat_axis=3, tiled=True)  11.7 us
    all_to_all x2, starting transfers between devices, shards(): lax.all_to_all(nearby, 'tp', split_axis=3, concat_axis=3, tiled=True)  9.57 us
    ppermute x8, waiting for transfers between devices, shifted(): return lax.ppermute(block, axis, route)  4.51 us
    unnamed x11, local copies, waits for them, and re-layouts  2.65 us
  transfers between devices with their start and end apart: 10, of which 4 were waited for; matrix products, arithmetic and copies ran while one was open for 6% of the time, Pallas kernels for 0%

commit v1 on v0

--- a/solution.py
+++ b/solution.py
@@ -3,6 +3,8 @@
 import jax
 import jax.numpy as jnp
 from jax import lax
+from jax.experimental import pallas as pl
+from jax.experimental.pallas import tpu as pltpu
 from jax.sharding import PartitionSpec as P
 
 NO = 32
@@ -36,7 +38,7 @@
     return jnp.stack([sigma_real, sigma_imag])
 
 
-def shards(green, hamiltonian, interaction):
+def windowed(green, hamiltonian, interaction):
     tp_count = lax.axis_size("tp")
     ta_place = lax.axis_index("ta")
     tp_place = lax.axis_index("tp")
@@ -121,7 +123,183 @@
     return current.reshape(2, groups, 1, stripe, block_rows)
 
 
+def exchange_orders(ta_count, tp_count):
+    tp_bits = [1 << bit for bit in reversed(range(1, tp_count.bit_length() - 1))]
+    even = tp_bits + [tp_count]
+    odd = tp_bits[:1] + tp_bits[2:] + [tp_count] + tp_bits[1:2]
+    return even, odd
+
+
+def gathered(own, orders, count):
+    held = own[None]
+    for masks in zip(*orders):
+        route = [(i, i ^ masks[i % 2]) for i in range(count)]
+        held = jnp.concatenate([held, lax.ppermute(held, ("ta", "tp"), route)])
+    return held
+
+
+def offsets_of(order):
+    offsets = [0]
+    for mask in order:
+        offsets = offsets + [known ^ mask for known in offsets]
+    return offsets
+
+
+def bf16_dot(left_side, right_side):
+    return lax.dot_general(
+        left_side, right_side, (((1,), (0,)), ((), ())), preferred_element_type=jnp.float32
+    )
+
+
+def make_iterations(orders, ta_count, tp_count, stripe, block_rows, factor):
+    order_size = ta_count * block_rows
+    offsets = [offsets_of(order) for order in orders]
+    half = jnp.bfloat16
+
+    def square_of(values):
+        real, imag = values
+        return real * real - imag * imag, 2.0 * real * imag
+
+    def window_of(values, mirror, weights, first_time):
+        rows, width = values[0].shape
+        real_square, imag_square = square_of(values)
+        mirror_real = mirror[0].astype(jnp.float32)
+        mirror_imag = mirror[1].astype(jnp.float32)
+        real = real_square * mirror_real - imag_square * mirror_imag
+        imag = real_square * mirror_imag + imag_square * mirror_real
+        source_time = lax.broadcasted_iota(jnp.int32, (rows, width), 0) // NO
+        target_time = lax.broadcasted_iota(jnp.int32, (rows, width), 1) // NO + first_time
+        inside = source_time <= target_time
+
+        def weighted(part):
+            part = (part.reshape(rows // NO, NO, width) * weights[None]).reshape(rows, width)
+            return jnp.where(inside, part, 0.0).astype(half)
+
+        return weighted(real), weighted(imag)
+
+    def products(left_side, right_side):
+        real = bf16_dot(left_side[0], right_side[0]) - bf16_dot(left_side[1], right_side[1])
+        imag = bf16_dot(left_side[0], right_side[1]) + bf16_dot(left_side[1], right_side[0])
+        return real, imag
+
+    def rotated(values, high_table, low_table):
+        high = values.astype(half)
+        low = (values - high.astype(jnp.float32)).astype(half)
+        return (
+            bf16_dot(high, high_table) + bf16_dot(low, high_table) + bf16_dot(high, low_table)
+        )
+
+    def kernel(place, near, far, weights_ref, high_ref, low_ref, out, values, lows, nexts, low_next):
+        ta_place = place[0]
+        tp_place = place[1]
+        me = ta_place * tp_count + tp_place
+        odd = me % 2
+        for source, flip in ((near, 0), (far, 1)):
+            for index in range(len(offsets[0])):
+                mask = jnp.where(odd == flip, offsets[0][index], offsets[1][index])
+                device = (me ^ flip) ^ mask
+                row = pl.multiple_of((device % tp_count) * stripe, stripe)
+                block = device // tp_count
+                for part in range(2):
+                    for group in range(ta_count):
+                        values[part, block, group, pl.ds(row, stripe), :] = source[
+                            index, part, group
+                        ]
+        weights = weights_ref[...]
+        high_table = high_ref[...]
+        low_table = low_ref[...]
+        for block in range(ta_count):
+            for part in range(2):
+                for group in range(ta_count):
+                    lows[part, group, :, block * block_rows : (block + 1) * block_rows] = values[
+                        part, block, group
+                    ].astype(half)
+        rounded = [lows[part].reshape(order_size, order_size) for part in range(2)]
+        for block in range(ta_count):
+            current = [values[part, block].reshape(order_size, block_rows) for part in range(2)]
+            mirror = [
+                jnp.transpose(lows[part, block].astype(jnp.float32)) for part in range(2)
+            ]
+            window = window_of(current, mirror, weights, block * (block_rows // NO))
+            memory = products(rounded, window)
+            hamilton = [rotated(current[part], high_table, low_table) for part in range(2)]
+            shape = (ta_count, block_rows, block_rows)
+            next_real = current[0] + 0.5 * (hamilton[1] + factor * memory[1])
+            next_imag = current[1] - 0.5 * (hamilton[0] + factor * memory[0])
+            for part, result in ((0, next_real), (1, next_imag)):
+                nexts[part, block] = result.reshape(shape)
+                low_next[part, :, :, block * block_rows : (block + 1) * block_rows] = (
+                    result.reshape(shape).astype(half)
+                )
+        current = [nexts[part, ta_place].reshape(order_size, block_rows) for part in range(2)]
+        mirror = [
+            jnp.transpose(low_next[part, ta_place].astype(jnp.float32)) for part in range(2)
+        ]
+        window = window_of(current, mirror, weights, ta_place * (block_rows // NO))
+        row = pl.multiple_of(tp_place * stripe, stripe)
+        own = [
+            nexts[part, ta_place, :, pl.ds(row, stripe), :].reshape(ta_count * stripe, block_rows)
+            for part in range(2)
+        ]
+        own_rounded = [
+            low_next[part, :, pl.ds(row, stripe), :].reshape(ta_count * stripe, order_size)
+            for part in range(2)
+        ]
+        memory = products(own_rounded, window)
+        hamilton = [rotated(own[part], high_table, low_table) for part in range(2)]
+        shape = (ta_count, stripe, block_rows)
+        out[0] = (own[0] + 0.5 * (hamilton[1] + factor * memory[1])).reshape(shape)
+        out[1] = (own[1] - 0.5 * (hamilton[0] + factor * memory[0])).reshape(shape)
+
+    big = (2, ta_count, ta_count, block_rows, block_rows)
+    flat = (2, ta_count, block_rows, order_size)
+    return pl.pallas_call(
+        kernel,
+        out_shape=jax.ShapeDtypeStruct((2, ta_count, stripe, block_rows), jnp.float32),
+        in_specs=[pl.BlockSpec(memory_space=pltpu.SMEM)]
+        + [pl.BlockSpec(memory_space=pltpu.VMEM)] * 5,
+        out_specs=pl.BlockSpec(memory_space=pltpu.VMEM),
+        scratch_shapes=[
+            pltpu.VMEM(big, jnp.float32),
+            pltpu.VMEM(flat, half),
+            pltpu.VMEM(big, jnp.float32),
+            pltpu.VMEM(flat, half),
+        ],
+        name="iterations",
+    )
+
+
+def replicated(green, hamiltonian, interaction):
+    ta_count = lax.axis_size("ta")
+    tp_count = lax.axis_size("tp")
+    stripe = green.shape[3]
+    block_rows = green.shape[4]
+    factor = 1.0 / math.sqrt(2 * block_rows)
+    orders = exchange_orders(ta_count, tp_count)
+    count = ta_count * tp_count
+    near = gathered(green[:, :, 0], orders, count)
+    far = lax.ppermute(near, ("ta", "tp"), [(i, i ^ 1) for i in range(count)])
+    place = jnp.stack([lax.axis_index("ta"), lax.axis_index("tp")]).astype(jnp.int32)
+    weights = jnp.tile((interaction * interaction).T, (1, block_rows // NO))
+    table = jnp.kron(jnp.eye(block_rows // NO, dtype=jnp.float32), hamiltonian.T)
+    high_table = table.astype(jnp.bfloat16)
+    low_table = (table - high_table.astype(jnp.float32)).astype(jnp.bfloat16)
+    step = make_iterations(orders, ta_count, tp_count, stripe, block_rows, factor)
+    result = step(place, near, far, weights, high_table, low_table)
+    return result[:, :, None]
+
+
 def solution(mesh):
     in_specs = (P(None, None, "tp", None, "ta"), P(), P())
     out_specs = P(None, None, "tp", None, "ta")
+    ta_count = mesh.shape["ta"]
+    tp_count = mesh.shape["tp"]
+
+    def shards(green, hamiltonian, interaction):
+        whole_bytes = green.size * green.dtype.itemsize * ta_count * tp_count
+        covered = ta_count == 2 and green.shape[1] == 2 and tp_count >= 4
+        if covered and tp_count & (tp_count - 1) == 0 and whole_bytes <= 1 << 22:
+            return replicated(green, hamiltonian, interaction)
+        return windowed(green, hamiltonian, interaction)
+
     return jax.shard_map(shards, mesh=mesh, in_specs=in_specs, out_specs=out_specs, check_vma=False)

time: 90.9 us -> 41 us (0.45)
  blocking collectives: 38.9 us -> 0 us
  starting transfers between devices: 24 us -> 8.26 us
  Pallas kernels: 0 us -> 5.94 us
  waiting for transfers between devices: 16.3 us -> 20.5 us
  local copies, waits for them, and re-layouts: 5.72 us -> 3.51 us
  matrix products: 2.07 us -> 0 us
    all_gather x2 -> x0, blocking collectives: 38.9 us -> none  [shards(): portion = lax.all_gather(sending, 'tp', axis=2, tiled=True)]
    ppermute x8 -> x5, waiting for transfers between devices: 4.51 us -> 20.5 us  [the longest x4 20.5 us: gathered(): held = jnp.concatenate([held, lax.ppermute(held, ('ta', 'tp'), route)])]
    all_to_all x2 -> x0, waiting for transfers between devices: 11.7 us -> none  [shards(): lax.all_to_all(nearby, 'tp', split_axis=3, concat_axis=3, tiled=True)]
    all_to_all x2 -> x0, starting transfers between devices: 9.57 us -> none  [shards(): lax.all_to_all(nearby, 'tp', split_axis=3, concat_axis=3, tiled=True)]
    ppermute x8 -> x5, starting transfers between devices: 14.5 us -> 8.26 us  [the longest x4 8.19 us: gathered(): held = jnp.concatenate([held, lax.ppermute(held, ('ta', 'tp'), route)])]
    pallas_call x0 -> x1, Pallas kernels: none -> 5.94 us  [replicated(): result = step(place, near, far, weights, high_table, low_table)]
    dot_general x11 -> x0, matrix products: 2.07 us -> none  [the longest x8 1.48 us: half_dot(): return jnp.dot(left_side, right_side, preferred_element_type=jnp.float32)]
    slice x31 -> x0, local copies, waits for them, and re-layouts: 1.56 us -> none  [the longest x15 0.79 us: self_energy(): mirror_part[1]]
  transfers between devices with their start and end apart: 10 -> 5, of which waited for: 4 -> 4; matrix products, arithmetic and copies ran while one was open for 6% -> 7% of each run, Pallas kernels for 0% -> 0%
where the time goes in v1:
time: 41 us; the launch traced here: 40.7 us
  waiting for transfers between devices  20.5 us (50%)
  starting transfers between devices  8.26 us (20%)
  Pallas kernels  5.94 us (14%)
  local copies, waits for them, and re-layouts  3.51 us (9%)
  other arithmetic  2.37 us (6%)
    ppermute x4, waiting for transfers between devices, gathered(): held = jnp.concatenate([held, lax.ppermute(held, ('ta', 'tp'), route)])  20.5 us
    ppermute x4, starting transfers between devices, gathered(): held = jnp.concatenate([held, lax.ppermute(held, ('ta', 'tp'), route)])  8.19 us
    pallas_call x1, Pallas kernels, replicated(): result = step(place, near, far, weights, high_table, low_table)  5.94 us
    unnamed x14, local copies, waits for them, and re-layouts  2.3 us
    concatenate x3, other arithmetic, gathered(): held = jnp.concatenate([held, lax.ppermute(held, ('ta', 'tp'), route)])  0.91 us
  transfers between devices with their start and end apart: 5, of which 4 were waited for; matrix products, arithmetic and copies ran while one was open for 7% of the time, Pallas kernels for 0%

profile of v1, /device:TPU:0, one launch (start us, length us, event | category | flops | bytes accessed | tf_op | source)
XLA Modules:
  0.0 40.7 jit_solution(5686341455887094518)
XLA Ops:
  0.0 0.0 copy-start.2
  0.0 4.1 %collective-permute-start = (f32[1,2,2,16,256]{4,3,2,1,0:T(8,128)}, f32[1,2,2,16,256]{4,3,2,1,0:T(8,128)S(1)}, u32[]{:S(2)}, u32[]{:S(2)}) collective-permute-start(f32[1,2,2,16,256]{4,3,2,1,0:T(8,128)} %bitcast.12), channel_id=1, source_target_pairs={{0,8},{1,9},{2,10},{3,11},{4,12},{5,13},{6,14},{7,15},{8,0},{9,1},... | collective-permute-start | bytes 196616 | tf_op jit(solution)/shard_map/ppermute | solution.py:137
  4.1 3.9 %collective-permute-done = f32[1,2,2,16,256]{4,3,2,1,0:T(8,128)S(1)} collective-permute-done((f32[1,2,2,16,256]{4,3,2,1,0:T(8,128)}, f32[1,2,2,16,256]{4,3,2,1,0:T(8,128)S(1)}, u32[]{:S(2)}, u32[]{:S(2)}) %collective-permute-start) | collective-permute-done | bytes 65568 | tf_op jit(solution)/shard_map/ppermute | solution.py:137
  8.0 0.8 %pad_maximum_fusion.2 = f32[2,2,2,16,256]{4,3,2,1,0:T(8,128)S(1)} fusion(f32[1,2,2,16,256]{4,3,2,1,0:T(8,128)S(1)} %collective-permute-done, f32[1,2,2,16,256]{4,3,2,1,0:T(8,128)} %bitcast.13), kind=kLoop, calls=%fused_computation.4 | loop fusion | flops 32768 | bytes 262144 | tf_op jit(solution)/shard_map/concatenate | solution.py:137
  8.8 0.7 %collective-permute-start.1 = (f32[2,2,2,16,256]{4,3,2,1,0:T(8,128)S(1)}, f32[2,2,2,16,256]{4,3,2,1,0:T(8,128)S(1)}, u32[]{:S(2)}, u32[]{:S(2)}) collective-permute-start(f32[2,2,2,16,256]{4,3,2,1,0:T(8,128)S(1)} %pad_maximum_fusion.2), channel_id=1, source_target_pairs={{0,4},{1,3},{2,6},{3,1},{4,0},{5,7},{6,2},{7,5},{8,12},{9,11},{10,... | collective-permute-start | bytes 393224 | tf_op jit(solution)/shard_map/ppermute | solution.py:137
  9.5 4.4 %collective-permute-done.1 = f32[2,2,2,16,256]{4,3,2,1,0:T(8,128)S(1)} collective-permute-done((f32[2,2,2,16,256]{4,3,2,1,0:T(8,128)S(1)}, f32[2,2,2,16,256]{4,3,2,1,0:T(8,128)S(1)}, u32[]{:S(2)}, u32[]{:S(2)}) %collective-permute-start.1) | collective-permute-done | bytes 131104 | tf_op jit(solution)/shard_map/ppermute | solution.py:137
  13.9 0.0 copy-done.2
  13.9 1.7 %collective-permute-start.2 = (f32[4,2,2,16,256]{4,3,2,1,0:T(8,128)S(1)}, f32[4,2,2,16,256]{4,3,2,1,0:T(8,128)S(1)}, u32[]{:S(2)}, u32[]{:S(2)}) collective-permute-start(f32[4,2,2,16,256]{4,3,2,1,0:T(8,128)S(1)} %pad_maximum_fusion.1), channel_id=1, source_target_pairs={{0,2},{1,17},{2,0},{3,19},{4,6},{5,21},{6,4},{7,23},{8,10},{9,25},... | collective-permute-start | bytes 786440 | tf_op jit(solution)/shard_map/ppermute | solution.py:137
  15.7 4.7 %collective-permute-done.2 = f32[4,2,2,16,256]{4,3,2,1,0:T(8,128)S(1)} collective-permute-done((f32[4,2,2,16,256]{4,3,2,1,0:T(8,128)S(1)}, f32[4,2,2,16,256]{4,3,2,1,0:T(8,128)S(1)}, u32[]{:S(2)}, u32[]{:S(2)}) %collective-permute-start.2) | collective-permute-done | bytes 262176 | tf_op jit(solution)/shard_map/ppermute | solution.py:137
  20.4 1.7 %collective-permute-start.3 = (f32[8,2,2,16,256]{4,3,2,1,0:T(8,128)S(1)}, f32[8,2,2,16,256]{4,3,2,1,0:T(8,128)S(1)}, u32[]{:S(2)}, u32[]{:S(2)}) collective-permute-start(f32[8,2,2,16,256]{4,3,2,1,0:T(8,128)S(1)} %pad_maximum_fusion), channel_id=1, source_target_pairs={{0,16},{1,5},{2,18},{3,7},{4,20},{5,1},{6,22},{7,3},{8,24},{9,13},... | collective-permute-start | bytes 1572872 | tf_op jit(solution)/shard_map/ppermute | solution.py:137
  22.2 7.5 %collective-permute-done.3 = f32[8,2,2,16,256]{4,3,2,1,0:T(8,128)S(1)} collective-permute-done((f32[8,2,2,16,256]{4,3,2,1,0:T(8,128)S(1)}, f32[8,2,2,16,256]{4,3,2,1,0:T(8,128)S(1)}, u32[]{:S(2)}, u32[]{:S(2)}) %collective-permute-start.3) | collective-permute-done | bytes 524320 | tf_op jit(solution)/shard_map/ppermute | solution.py:137
  29.6 0.0 copy-start.3
  29.7 0.0 copy-start
  29.7 0.1 collective-permute-start.4
  29.8 0.6 %copy-done.3 = f32[32,32]{1,0:T(8,128)S(1)} copy-done((f32[32,32]{1,0:T(8,128)S(1)}, f32[32,32]{1,0:T(8,128)}, u32[]{:S(2)}) %copy-start.3) | copy-done | bytes 4120
  30.4 0.0 copy-start.4
  30.4 0.1 copy.5
  30.4 0.6 %copy-done.4 = f32[32,32]{1,0:T(8,128)S(1)} copy-done((f32[32,32]{1,0:T(8,128)S(1)}, f32[32,32]{1,0:T(8,128)}, u32[]{:S(2)}) %copy-start.4) | copy-done | bytes 4120
  31.1 0.1 copy.4
  31.2 0.7 %tile.10.weights_ref = f32[32,256]{1,0:T(8,128)} reshape(f32[32,8,32]{2,1,0:T(8,128)S(1)} %tile.4) | data formatting | bytes 65536 | tf_op jit(solution)/shard_map/tile | solution.py:283
  31.9 0.1 broadcast_multiply_fusion
  32.0 0.3 mul.31
  32.4 0.0 copy-done
  32.4 0.6 %pad_add_fusion.place = s32[2]{0:T(128)} fusion(s32[1]{0:T(128)} %bitcast.1, s32[1]{0:T(128)} %bitcast), kind=kLoop, calls=%fused_computation.13 | loop fusion | flops 2 | bytes 16 | tf_op jit(solution)/shard_map/stack | solution.py:282
  33.0 0.7 %subtract_convert_fusion = (bf16[256,256]{1,0:T(8,128)(2,1)}, bf16[256,256]{1,0:T(8,128)(2,1)}) fusion(f32[256,256]{1,0:T(8,128)S(1)} %mul.31), kind=kLoop, calls=%fused_computation.3 | loop fusion | flops 262144 | bytes 524288 | tf_op jit(solution)/shard_map/convert_element_type | solution.py:286
  33.7 0.0 collective-permute-done.4.far
  33.7 0.0 copy-start.1
  33.7 1.0 %copy-done.1 = f32[16,2,2,16,256]{4,3,2,1,0:T(8,128)} copy-done((f32[16,2,2,16,256]{4,3,2,1,0:T(8,128)}, f32[16,2,2,16,256]{4,3,2,1,0:T(8,128)S(1)}, u32[]{:S(2)}) %copy-start.1) | copy-done | bytes 1048600
  34.7 5.9 %iterations.1 = f32[2,2,16,256]{3,2,1,0:T(8,128)} custom-call(s32[2]{0:T(128)} %pad_add_fusion.place, f32[16,2,2,16,256]{4,3,2,1,0:T(8,128)} %copy-done, f32[16,2,2,16,256]{4,3,2,1,0:T(8,128)} %copy-done.1, f32[32,256]{1,0:T(8,128)} %tile.10.weights_ref, bf16[256,256]{1,0:T(8,128)(2,1)} %get-tuple-element.6.high_ref, bf16[256,256]{1,0:T(8,128)(2,1)} %get-tuple-element.5.low_ref), custom_call_target="tpu_custom_call" | custom-call | tf_op jit(solution)/shard_map/iterations/pallas_call | solution.py:288
  (10 shorter events, 0.2 us)
Async XLA Ops:
  0.0 13.9 %copy-start.2 = (f32[2,2,1,16,256]{4,3,2,1,0:T(8,128)S(1)}, f32[2,2,1,16,256]{4,3,2,1,0:T(8,128)}, u32[]{:S(2)}) copy-start(f32[2,2,1,16,256]{4,3,2,1,0:T(8,128)} %param.3) | copy-start | bytes 196612
  0.0 8.0 %collective-permute-start = (f32[1,2,2,16,256]{4,3,2,1,0:T(8,128)}, f32[1,2,2,16,256]{4,3,2,1,0:T(8,128)S(1)}, u32[]{:S(2)}, u32[]{:S(2)}) collective-permute-start(f32[1,2,2,16,256]{4,3,2,1,0:T(8,128)} %bitcast.12), channel_id=1, source_target_pairs={{0,8},{1,9},{2,10},{3,11},{4,12},{5,13},{6,14},{7,15},{8,0},{9,1},... | collective-permute-start | bytes 196616 | tf_op jit(solution)/shard_map/ppermute | solution.py:137
  8.8 5.0 %collective-permute-start.1 = (f32[2,2,2,16,256]{4,3,2,1,0:T(8,128)S(1)}, f32[2,2,2,16,256]{4,3,2,1,0:T(8,128)S(1)}, u32[]{:S(2)}, u32[]{:S(2)}) collective-permute-start(f32[2,2,2,16,256]{4,3,2,1,0:T(8,128)S(1)} %pad_maximum_fusion.2), channel_id=1, source_target_pairs={{0,4},{1,3},{2,6},{3,1},{4,0},{5,7},{6,2},{7,5},{8,12},{9,11},{10,... | collective-permute-start | bytes 393224 | tf_op jit(solution)/shard_map/ppermute | solution.py:137
  13.9 6.4 %collective-permute-start.2 = (f32[4,2,2,16,256]{4,3,2,1,0:T(8,128)S(1)}, f32[4,2,2,16,256]{4,3,2,1,0:T(8,128)S(1)}, u32[]{:S(2)}, u32[]{:S(2)}) collective-permute-start(f32[4,2,2,16,256]{4,3,2,1,0:T(8,128)S(1)} %pad_maximum_fusion.1), channel_id=1, source_target_pairs={{0,2},{1,17},{2,0},{3,19},{4,6},{5,21},{6,4},{7,23},{8,10},{9,25},... | collective-permute-start | bytes 786440 | tf_op jit(solution)/shard_map/ppermute | solution.py:137
  20.4 9.2 %collective-permute-start.3 = (f32[8,2,2,16,256]{4,3,2,1,0:T(8,128)S(1)}, f32[8,2,2,16,256]{4,3,2,1,0:T(8,128)S(1)}, u32[]{:S(2)}, u32[]{:S(2)}) collective-permute-start(f32[8,2,2,16,256]{4,3,2,1,0:T(8,128)S(1)} %pad_maximum_fusion), channel_id=1, source_target_pairs={{0,16},{1,5},{2,18},{3,7},{4,20},{5,1},{6,22},{7,3},{8,24},{9,13},... | collective-permute-start | bytes 1572872 | tf_op jit(solution)/shard_map/ppermute | solution.py:137
  29.6 0.7 %copy-start.3 = (f32[32,32]{1,0:T(8,128)S(1)}, f32[32,32]{1,0:T(8,128)}, u32[]{:S(2)}) copy-start(f32[32,32]{1,0:T(8,128)} %param.4) | copy-start | bytes 12292
  29.7 2.7 %copy-start = (f32[16,2,2,16,256]{4,3,2,1,0:T(8,128)}, f32[16,2,2,16,256]{4,3,2,1,0:T(8,128)S(1)}, u32[]{:S(2)}) copy-start(f32[16,2,2,16,256]{4,3,2,1,0:T(8,128)S(1)} %constant_dynamic-update-slice_fusion.near) | copy-start | bytes 3145732
  29.7 4.0 %collective-permute-start.4 = (f32[16,2,2,16,256]{4,3,2,1,0:T(8,128)S(1)}, f32[16,2,2,16,256]{4,3,2,1,0:T(8,128)S(1)}, u32[]{:S(2)}, u32[]{:S(2)}) collective-permute-start(f32[16,2,2,16,256]{4,3,2,1,0:T(8,128)S(1)} %constant_dynamic-update-slice_fusion.near), channel_id=1, source_target_pairs={{0,1},{1,0},{2,3},{3,2},{4,5},{5,4},{6,7},{7,6},{8,9},{9,8},{10,11... | collective-permute-start | bytes 3145736 | tf_op jit(solution)/shard_map/ppermute | solution.py:281
  30.4 0.7 %copy-start.4 = (f32[32,32]{1,0:T(8,128)S(1)}, f32[32,32]{1,0:T(8,128)}, u32[]{:S(2)}) copy-start(f32[32,32]{1,0:T(8,128)} %param.5) | copy-start | bytes 12292
  33.7 1.0 %copy-start.1 = (f32[16,2,2,16,256]{4,3,2,1,0:T(8,128)}, f32[16,2,2,16,256]{4,3,2,1,0:T(8,128)S(1)}, u32[]{:S(2)}) copy-start(f32[16,2,2,16,256]{4,3,2,1,0:T(8,128)S(1)} %collective-permute-done.4.far) | copy-start | bytes 3145732

commit v2 on v1

--- a/solution.py
+++ b/solution.py
@@ -125,16 +125,22 @@
 
 def exchange_orders(ta_count, tp_count):
     tp_bits = [1 << bit for bit in reversed(range(1, tp_count.bit_length() - 1))]
-    even = tp_bits + [tp_count]
-    odd = tp_bits[:1] + tp_bits[2:] + [tp_count] + tp_bits[1:2]
-    return even, odd
-
-
-def gathered(own, orders, count):
-    held = own[None]
-    for masks in zip(*orders):
-        route = [(i, i ^ masks[i % 2]) for i in range(count)]
-        held = jnp.concatenate([held, lax.ppermute(held, ("ta", "tp"), route)])
+    first, middle, last = tp_bits[:1], tp_bits[1:-1], tp_bits[-1:]
+    ta_bit = [tp_count]
+    return [
+        (first + middle + last + ta_bit, first + middle + ta_bit + last),
+        (first + middle + ta_bit + last, first + middle + last + ta_bit),
+    ]
+
+
+def gathered(pieces, orders, count):
+    held = [piece[None] for piece in pieces]
+    for step in range(len(orders[0][0])):
+        for index, (even, odd) in enumerate(orders):
+            masks = (even[step], odd[step])
+            route = [(i, i ^ masks[i % 2]) for i in range(count)]
+            arriving = lax.ppermute(held[index], ("ta", "tp"), route)
+            held[index] = jnp.concatenate([held[index], arriving])
     return held
 
 
@@ -153,7 +159,7 @@
 
 def make_iterations(orders, ta_count, tp_count, stripe, block_rows, factor):
     order_size = ta_count * block_rows
-    offsets = [offsets_of(order) for order in orders]
+    offsets = [[offsets_of(order) for order in pair] for pair in orders]
     half = jnp.bfloat16
 
     def square_of(values):
@@ -189,25 +195,36 @@
             bf16_dot(high, high_table) + bf16_dot(low, high_table) + bf16_dot(high, low_table)
         )
 
-    def kernel(place, near, far, weights_ref, high_ref, low_ref, out, values, lows, nexts, low_next):
-        ta_place = place[0]
-        tp_place = place[1]
+    def repeated(tile):
+        return jnp.concatenate([tile] * (block_rows // NO), axis=1)
+
+    def kernel(*refs):
+        sources = refs[: 2 * ta_count]
+        hamiltonian, interaction, out, values, lows, nexts, low_next = refs[2 * ta_count :]
+        ta_place = lax.axis_index("ta")
+        tp_place = lax.axis_index("tp")
         me = ta_place * tp_count + tp_place
         odd = me % 2
-        for source, flip in ((near, 0), (far, 1)):
-            for index in range(len(offsets[0])):
-                mask = jnp.where(odd == flip, offsets[0][index], offsets[1][index])
-                device = (me ^ flip) ^ mask
-                row = pl.multiple_of((device % tp_count) * stripe, stripe)
-                block = device // tp_count
-                for part in range(2):
-                    for group in range(ta_count):
-                        values[part, block, group, pl.ds(row, stripe), :] = source[
-                            index, part, group
-                        ]
-        weights = weights_ref[...]
-        high_table = high_ref[...]
-        low_table = low_ref[...]
+        for group in range(ta_count):
+            for flip in range(2):
+                source = sources[2 * group + flip]
+                pair = offsets[group]
+                for index in range(len(pair[0])):
+                    mask = jnp.where(odd == flip, pair[0][index], pair[1][index])
+                    device = (me ^ flip) ^ mask
+                    row = pl.multiple_of((device % tp_count) * stripe, stripe)
+                    block = device // tp_count
+                    for part in range(2):
+                        values[part, block, group, pl.ds(row, stripe), :] = source[index, part]
+        weights = repeated(jnp.transpose(interaction[...] * interaction[...]))
+        table = jnp.concatenate([repeated(jnp.transpose(hamiltonian[...]))] * (block_rows // NO))
+        same_time = (
+            lax.broadcasted_iota(jnp.int32, table.shape, 0) // NO
+            == lax.broadcasted_iota(jnp.int32, table.shape, 1) // NO
+        )
+        table = jnp.where(same_time, table, 0.0)
+        high_table = table.astype(half)
+        low_table = (table - high_table.astype(jnp.float32)).astype(half)
         for block in range(ta_count):
             for part in range(2):
                 for group in range(ta_count):
@@ -256,8 +273,7 @@
     return pl.pallas_call(
         kernel,
         out_shape=jax.ShapeDtypeStruct((2, ta_count, stripe, block_rows), jnp.float32),
-        in_specs=[pl.BlockSpec(memory_space=pltpu.SMEM)]
-        + [pl.BlockSpec(memory_space=pltpu.VMEM)] * 5,
+        in_specs=[pl.BlockSpec(memory_space=pltpu.VMEM)] * (2 * ta_count + 2),
         out_specs=pl.BlockSpec(memory_space=pltpu.VMEM),
         scratch_shapes=[
             pltpu.VMEM(big, jnp.float32),
@@ -265,6 +281,7 @@
             pltpu.VMEM(big, jnp.float32),
             pltpu.VMEM(flat, half),
         ],
+        compiler_params=pltpu.CompilerParams(vmem_limit_bytes=24 << 20),
         name="iterations",
     )
 
@@ -277,15 +294,13 @@
     factor = 1.0 / math.sqrt(2 * block_rows)
     orders = exchange_orders(ta_count, tp_count)
     count = ta_count * tp_count
-    near = gathered(green[:, :, 0], orders, count)
-    far = lax.ppermute(near, ("ta", "tp"), [(i, i ^ 1) for i in range(count)])
-    place = jnp.stack([lax.axis_index("ta"), lax.axis_index("tp")]).astype(jnp.int32)
-    weights = jnp.tile((interaction * interaction).T, (1, block_rows // NO))
-    table = jnp.kron(jnp.eye(block_rows // NO, dtype=jnp.float32), hamiltonian.T)
-    high_table = table.astype(jnp.bfloat16)
-    low_table = (table - high_table.astype(jnp.float32)).astype(jnp.bfloat16)
+    held = gathered([green[:, group, 0] for group in range(ta_count)], orders, count)
+    swap = [(i, i ^ 1) for i in range(count)]
+    sources = []
+    for near in held:
+        sources += [near, lax.ppermute(near, ("ta", "tp"), swap)]
     step = make_iterations(orders, ta_count, tp_count, stripe, block_rows, factor)
-    result = step(place, near, far, weights, high_table, low_table)
+    result = step(*sources, hamiltonian, interaction)
     return result[:, :, None]
 
 

time: 41 us -> 33.6 us (0.82)
  waiting for transfers between devices: 20.5 us -> 13.2 us
  starting transfers between devices: 8.26 us -> 14.6 us
  local copies, waits for them, and re-layouts: 3.51 us -> 0.94 us
  other arithmetic: 2.37 us -> 0.07 us
  Pallas kernels: 5.94 us -> 4.57 us
    ppermute x5 -> x10, waiting for transfers between devices: 20.5 us -> 13.2 us  [the longest x8 11.3 us: gathered(): arriving = lax.ppermute(held[index], ('ta', 'tp'), route)]
    ppermute x5 -> x10, starting transfers between devices: 8.26 us -> 14.6 us  [the longest x8 14.4 us: gathered(): arriving = lax.ppermute(held[index], ('ta', 'tp'), route)]
    unnamed x14 -> x13, local copies, waits for them, and re-layouts: 2.3 us -> 0.06 us
    pallas_call x1, Pallas kernels: 5.94 us -> 4.57 us  [replicated(): result = step(*sources, hamiltonian, interaction)]
    concatenate x3 -> x6, other arithmetic: 0.91 us -> 0.07 us  [gathered(): held[index] = jnp.concatenate([held[index], arriving])]
    convert_element_type x2 -> x0, other arithmetic: 0.73 us -> none  [the longest x1 0.72 us: replicated(): low_table = (table - high_table.astype(jnp.float32)).astype(jnp.bfloat16)]
    another operation x1 -> x0, other arithmetic: 0.6 us -> none  [replicated(): jnp.stack([lax.axis_index('ta'), lax.axis_index('tp')]).astype(jnp.int32)]
    another operation x2 -> x1, local copies, waits for them, and re-layouts: 0.72 us -> 0.84 us  [gathered(): held = [piece[None] for piece in pieces]]
  transfers between devices with their start and end apart: 5 -> 10, of which waited for: 4 -> 9; matrix products, arithmetic and copies ran while one was open for 7% -> 0% of each run, Pallas kernels for 0% -> 0%
where the time goes in v2:
time: 33.6 us; the launch traced here: 33.4 us
  starting transfers between devices  14.6 us (43%)
  waiting for transfers between devices  13.2 us (39%)
  Pallas kernels  4.57 us (14%)
  local copies, waits for them, and re-layouts  0.94 us (3%)
    ppermute x8, starting transfers between devices, gathered(): arriving = lax.ppermute(held[index], ('ta', 'tp'), route)  14.4 us
    ppermute x8, waiting for transfers between devices, gathered(): arriving = lax.ppermute(held[index], ('ta', 'tp'), route)  11.3 us
    pallas_call x1, Pallas kernels, replicated(): result = step(*sources, hamiltonian, interaction)  4.57 us
    ppermute x2, waiting for transfers between devices, replicated(): sources += [near, lax.ppermute(near, ('ta', 'tp'), swap)]  1.9 us
    another operation x1, local copies, waits for them, and re-layouts, gathered(): held = [piece[None] for piece in pieces]  0.84 us
  transfers between devices with their start and end apart: 10, of which 9 were waited for; matrix products, arithmetic and copies ran while one was open for 0% of the time, Pallas kernels for 0%

profile of v2, /device:TPU:0, one launch (start us, length us, event | category | flops | bytes accessed | tf_op | source)
XLA Modules:
  0.0 33.4 jit_solution(4348759785095194319)
XLA Ops:
  0.0 0.0 copy-start.2
  0.0 0.8 %slice_bitcast_fusion = (f32[1,2,16,256]{3,2,1,0:T(8,128)S(1)}, f32[1,2,16,256]{3,2,1,0:T(8,128)S(1)}) fusion(f32[2,2,1,16,256]{4,3,2,1,0:T(8,128)} %param.3), kind=kLoop, calls=%fused_computation.6 | loop fusion | bytes 131072 | tf_op jit(solution)/shard_map/broadcast_in_dim;squeeze | solution.py:137
  0.8 4.1 %collective-permute-start.5 = (f32[1,2,16,256]{3,2,1,0:T(8,128)S(1)}, f32[1,2,16,256]{3,2,1,0:T(8,128)S(1)}, u32[]{:S(2)}, u32[]{:S(2)}) collective-permute-start(f32[1,2,16,256]{3,2,1,0:T(8,128)S(1)} %get-tuple-element.5), channel_id=1, source_target_pairs={{0,8},{1,9},{2,10},{3,11},{4,12},{5,13},{6,14},{7,15},{8,0},{9,1},... | collective-permute-start | bytes 98312 | tf_op jit(solution)/shard_map/ppermute | solution.py:142
  4.9 0.1 collective-permute-start
  5.0 0.0 copy-done.2
  5.0 2.2 %collective-permute-done.5 = f32[1,2,16,256]{3,2,1,0:T(8,128)S(1)} collective-permute-done((f32[1,2,16,256]{3,2,1,0:T(8,128)S(1)}, f32[1,2,16,256]{3,2,1,0:T(8,128)S(1)}, u32[]{:S(2)}, u32[]{:S(2)}) %collective-permute-start.5) | collective-permute-done | bytes 32800 | tf_op jit(solution)/shard_map/ppermute | solution.py:142
  7.2 1.6 %collective-permute-start.6 = (f32[2,2,16,256]{3,2,1,0:T(8,128)S(1)}, f32[2,2,16,256]{3,2,1,0:T(8,128)S(1)}, u32[]{:S(2)}, u32[]{:S(2)}) collective-permute-start(f32[2,2,16,256]{3,2,1,0:T(8,128)S(1)} %pad_maximum_fusion.5), channel_id=1, source_target_pairs={{0,4},{1,5},{2,6},{3,7},{4,0},{5,1},{6,2},{7,3},{8,12},{9,13},{10,... | collective-permute-start | bytes 196616 | tf_op jit(solution)/shard_map/ppermute | solution.py:142
  8.8 0.9 %collective-permute-done = f32[1,2,16,256]{3,2,1,0:T(8,128)S(1)} collective-permute-done((f32[1,2,16,256]{3,2,1,0:T(8,128)S(1)}, f32[1,2,16,256]{3,2,1,0:T(8,128)S(1)}, u32[]{:S(2)}, u32[]{:S(2)}) %collective-permute-start) | collective-permute-done | bytes 32800 | tf_op jit(solution)/shard_map/ppermute | solution.py:142
  9.7 1.6 %collective-permute-start.1 = (f32[2,2,16,256]{3,2,1,0:T(8,128)S(1)}, f32[2,2,16,256]{3,2,1,0:T(8,128)S(1)}, u32[]{:S(2)}, u32[]{:S(2)}) collective-permute-start(f32[2,2,16,256]{3,2,1,0:T(8,128)S(1)} %pad_maximum_fusion.4), channel_id=1, source_target_pairs={{0,4},{1,5},{2,6},{3,7},{4,0},{5,1},{6,2},{7,3},{8,12},{9,13},{10,... | collective-permute-start | bytes 196616 | tf_op jit(solution)/shard_map/ppermute | solution.py:142
  11.3 0.6 %collective-permute-done.6 = f32[2,2,16,256]{3,2,1,0:T(8,128)S(1)} collective-permute-done((f32[2,2,16,256]{3,2,1,0:T(8,128)S(1)}, f32[2,2,16,256]{3,2,1,0:T(8,128)S(1)}, u32[]{:S(2)}, u32[]{:S(2)}) %collective-permute-start.6) | collective-permute-done | bytes 65568 | tf_op jit(solution)/shard_map/ppermute | solution.py:142
  11.9 2.0 %collective-permute-start.7 = (f32[4,2,16,256]{3,2,1,0:T(8,128)S(1)}, f32[4,2,16,256]{3,2,1,0:T(8,128)S(1)}, u32[]{:S(2)}, u32[]{:S(2)}) collective-permute-start(f32[4,2,16,256]{3,2,1,0:T(8,128)S(1)} %pad_maximum_fusion.3), channel_id=1, source_target_pairs={{0,16},{1,3},{2,18},{3,1},{4,20},{5,7},{6,22},{7,5},{8,24},{9,11},... | collective-permute-start | bytes 393224 | tf_op jit(solution)/shard_map/ppermute | solution.py:142
  13.9 0.1 collective-permute-done.1
  14.0 1.6 %collective-permute-start.2 = (f32[4,2,16,256]{3,2,1,0:T(8,128)S(1)}, f32[4,2,16,256]{3,2,1,0:T(8,128)S(1)}, u32[]{:S(2)}, u32[]{:S(2)}) collective-permute-start(f32[4,2,16,256]{3,2,1,0:T(8,128)S(1)} %pad_maximum_fusion.2), channel_id=1, source_target_pairs={{0,2},{1,17},{2,0},{3,19},{4,6},{5,21},{6,4},{7,23},{8,10},{9,25},... | collective-permute-start | bytes 393224 | tf_op jit(solution)/shard_map/ppermute | solution.py:142
  15.6 2.8 %collective-permute-done.7 = f32[4,2,16,256]{3,2,1,0:T(8,128)S(1)} collective-permute-done((f32[4,2,16,256]{3,2,1,0:T(8,128)S(1)}, f32[4,2,16,256]{3,2,1,0:T(8,128)S(1)}, u32[]{:S(2)}, u32[]{:S(2)}) %collective-permute-start.7) | collective-permute-done | bytes 131104 | tf_op jit(solution)/shard_map/ppermute | solution.py:142
  18.4 2.0 %collective-permute-start.8 = (f32[8,2,16,256]{3,2,1,0:T(8,128)S(1)}, f32[8,2,16,256]{3,2,1,0:T(8,128)S(1)}, u32[]{:S(2)}, u32[]{:S(2)}) collective-permute-start(f32[8,2,16,256]{3,2,1,0:T(8,128)S(1)} %pad_maximum_fusion.1), channel_id=1, source_target_pairs={{0,2},{1,17},{2,0},{3,19},{4,6},{5,21},{6,4},{7,23},{8,10},{9,25},... | collective-permute-start | bytes 786440 | tf_op jit(solution)/shard_map/ppermute | solution.py:142
  20.4 0.0 collective-permute-done.2
  20.4 1.6 %collective-permute-start.3 = (f32[8,2,16,256]{3,2,1,0:T(8,128)S(1)}, f32[8,2,16,256]{3,2,1,0:T(8,128)S(1)}, u32[]{:S(2)}, u32[]{:S(2)}) collective-permute-start(f32[8,2,16,256]{3,2,1,0:T(8,128)S(1)} %pad_maximum_fusion), channel_id=1, source_target_pairs={{0,16},{1,3},{2,18},{3,1},{4,20},{5,7},{6,22},{7,5},{8,24},{9,11},... | collective-permute-start | bytes 786440 | tf_op jit(solution)/shard_map/ppermute | solution.py:142
  22.0 3.4 %collective-permute-done.8 = f32[8,2,16,256]{3,2,1,0:T(8,128)S(1)} collective-permute-done((f32[8,2,16,256]{3,2,1,0:T(8,128)S(1)}, f32[8,2,16,256]{3,2,1,0:T(8,128)S(1)}, u32[]{:S(2)}, u32[]{:S(2)}) %collective-permute-start.8) | collective-permute-done | bytes 262176 | tf_op jit(solution)/shard_map/ppermute | solution.py:142
  25.4 0.0 copy-start
  25.4 0.0 copy-start.1
  25.4 0.1 collective-permute-start.9
  25.5 1.3 %collective-permute-done.3 = f32[8,2,16,256]{3,2,1,0:T(8,128)S(1)} collective-permute-done((f32[8,2,16,256]{3,2,1,0:T(8,128)S(1)}, f32[8,2,16,256]{3,2,1,0:T(8,128)S(1)}, u32[]{:S(2)}, u32[]{:S(2)}) %collective-permute-start.3) | collective-permute-done | bytes 262176 | tf_op jit(solution)/shard_map/ppermute | solution.py:142
  26.9 0.1 collective-permute-start.4
  26.9 0.4 %collective-permute-done.9.refs_3_ = f32[16,2,16,256]{3,2,1,0:T(8,128)S(1)} collective-permute-done((f32[16,2,16,256]{3,2,1,0:T(8,128)S(1)}, f32[16,2,16,256]{3,2,1,0:T(8,128)S(1)}, u32[]{:S(2)}, u32[]{:S(2)}) %collective-permute-start.9) | collective-permute-done | bytes 524320 | tf_op jit(solution)/shard_map/ppermute | solution.py:301
  27.4 1.4 %collective-permute-done.4.refs_1_ = f32[16,2,16,256]{3,2,1,0:T(8,128)S(1)} collective-permute-done((f32[16,2,16,256]{3,2,1,0:T(8,128)S(1)}, f32[16,2,16,256]{3,2,1,0:T(8,128)S(1)}, u32[]{:S(2)}, u32[]{:S(2)}) %collective-permute-start.4) | collective-permute-done | bytes 524320 | tf_op jit(solution)/shard_map/ppermute | solution.py:301
  28.8 0.0 copy-done
  28.8 0.0 copy-done.1
  28.8 4.6 %iterations.1 = f32[2,2,16,256]{3,2,1,0:T(8,128)} custom-call(f32[16,2,16,256]{3,2,1,0:T(8,128)S(1)} %constant_dynamic-update-slice_fusion.refs_0_, f32[16,2,16,256]{3,2,1,0:T(8,128)S(1)} %collective-permute-done.4.refs_1_, f32[16,2,16,256]{3,2,1,0:T(8,128)S(1)} %constant_dynamic-update-slice_fusion.5.refs_2_, ...), custom_call_target="tpu_custom_call" | custom-call | tf_op jit(solution)/shard_map/iterations/pallas_call | solution.py:303
  (15 shorter events, 0.1 us)
Async XLA Ops:
  0.0 5.0 %copy-start.2 = (f32[2,2,1,16,256]{4,3,2,1,0:T(8,128)S(1)}, f32[2,2,1,16,256]{4,3,2,1,0:T(8,128)}, u32[]{:S(2)}) copy-start(f32[2,2,1,16,256]{4,3,2,1,0:T(8,128)} %param.3) | copy-start | bytes 196612
  0.8 6.3 %collective-permute-start.5 = (f32[1,2,16,256]{3,2,1,0:T(8,128)S(1)}, f32[1,2,16,256]{3,2,1,0:T(8,128)S(1)}, u32[]{:S(2)}, u32[]{:S(2)}) collective-permute-start(f32[1,2,16,256]{3,2,1,0:T(8,128)S(1)} %get-tuple-element.5), channel_id=1, source_target_pairs={{0,8},{1,9},{2,10},{3,11},{4,12},{5,13},{6,14},{7,15},{8,0},{9,1},... | collective-permute-start | bytes 98312 | tf_op jit(solution)/shard_map/ppermute | solution.py:142
  4.9 4.8 %collective-permute-start = (f32[1,2,16,256]{3,2,1,0:T(8,128)S(1)}, f32[1,2,16,256]{3,2,1,0:T(8,128)S(1)}, u32[]{:S(2)}, u32[]{:S(2)}) collective-permute-start(f32[1,2,16,256]{3,2,1,0:T(8,128)S(1)} %get-tuple-element.6), channel_id=1, source_target_pairs={{0,8},{1,9},{2,10},{3,11},{4,12},{5,13},{6,14},{7,15},{8,0},{9,1},... | collective-permute-start | bytes 98312 | tf_op jit(solution)/shard_map/ppermute | solution.py:142
  7.2 4.8 %collective-permute-start.6 = (f32[2,2,16,256]{3,2,1,0:T(8,128)S(1)}, f32[2,2,16,256]{3,2,1,0:T(8,128)S(1)}, u32[]{:S(2)}, u32[]{:S(2)}) collective-permute-start(f32[2,2,16,256]{3,2,1,0:T(8,128)S(1)} %pad_maximum_fusion.5), channel_id=1, source_target_pairs={{0,4},{1,5},{2,6},{3,7},{4,0},{5,1},{6,2},{7,3},{8,12},{9,13},{10,... | collective-permute-start | bytes 196616 | tf_op jit(solution)/shard_map/ppermute | solution.py:142
  9.7 4.3 %collective-permute-start.1 = (f32[2,2,16,256]{3,2,1,0:T(8,128)S(1)}, f32[2,2,16,256]{3,2,1,0:T(8,128)S(1)}, u32[]{:S(2)}, u32[]{:S(2)}) collective-permute-start(f32[2,2,16,256]{3,2,1,0:T(8,128)S(1)} %pad_maximum_fusion.4), channel_id=1, source_target_pairs={{0,4},{1,5},{2,6},{3,7},{4,0},{5,1},{6,2},{7,3},{8,12},{9,13},{10,... | collective-permute-start | bytes 196616 | tf_op jit(solution)/shard_map/ppermute | solution.py:142
  11.9 6.4 %collective-permute-start.7 = (f32[4,2,16,256]{3,2,1,0:T(8,128)S(1)}, f32[4,2,16,256]{3,2,1,0:T(8,128)S(1)}, u32[]{:S(2)}, u32[]{:S(2)}) collective-permute-start(f32[4,2,16,256]{3,2,1,0:T(8,128)S(1)} %pad_maximum_fusion.3), channel_id=1, source_target_pairs={{0,16},{1,3},{2,18},{3,1},{4,20},{5,7},{6,22},{7,5},{8,24},{9,11},... | collective-permute-start | bytes 393224 | tf_op jit(solution)/shard_map/ppermute | solution.py:142
  14.0 6.4 %collective-permute-start.2 = (f32[4,2,16,256]{3,2,1,0:T(8,128)S(1)}, f32[4,2,16,256]{3,2,1,0:T(8,128)S(1)}, u32[]{:S(2)}, u32[]{:S(2)}) collective-permute-start(f32[4,2,16,256]{3,2,1,0:T(8,128)S(1)} %pad_maximum_fusion.2), channel_id=1, source_target_pairs={{0,2},{1,17},{2,0},{3,19},{4,6},{5,21},{6,4},{7,23},{8,10},{9,25},... | collective-permute-start | bytes 393224 | tf_op jit(solution)/shard_map/ppermute | solution.py:142
  18.4 7.0 %collective-permute-start.8 = (f32[8,2,16,256]{3,2,1,0:T(8,128)S(1)}, f32[8,2,16,256]{3,2,1,0:T(8,128)S(1)}, u32[]{:S(2)}, u32[]{:S(2)}) collective-permute-start(f32[8,2,16,256]{3,2,1,0:T(8,128)S(1)} %pad_maximum_fusion.1), channel_id=1, source_target_pairs={{0,2},{1,17},{2,0},{3,19},{4,6},{5,21},{6,4},{7,23},{8,10},{9,25},... | collective-permute-start | bytes 786440 | tf_op jit(solution)/shard_map/ppermute | solution.py:142
  20.4 6.4 %collective-permute-start.3 = (f32[8,2,16,256]{3,2,1,0:T(8,128)S(1)}, f32[8,2,16,256]{3,2,1,0:T(8,128)S(1)}, u32[]{:S(2)}, u32[]{:S(2)}) collective-permute-start(f32[8,2,16,256]{3,2,1,0:T(8,128)S(1)} %pad_maximum_fusion), channel_id=1, source_target_pairs={{0,16},{1,3},{2,18},{3,1},{4,20},{5,7},{6,22},{7,5},{8,24},{9,11},... | collective-permute-start | bytes 786440 | tf_op jit(solution)/shard_map/ppermute | solution.py:142
  25.4 3.5 %copy-start = (f32[32,32]{1,0:T(8,128)S(1)}, f32[32,32]{1,0:T(8,128)}, u32[]{:S(2)}) copy-start(f32[32,32]{1,0:T(8,128)} %refs_4_.1) | copy-start | bytes 12292
  25.4 3.4 %copy-start.1 = (f32[32,32]{1,0:T(8,128)S(1)}, f32[32,32]{1,0:T(8,128)}, u32[]{:S(2)}) copy-start(f32[32,32]{1,0:T(8,128)} %refs_5_.1) | copy-start | bytes 12292
  25.4 2.0 %collective-permute-start.9 = (f32[16,2,16,256]{3,2,1,0:T(8,128)S(1)}, f32[16,2,16,256]{3,2,1,0:T(8,128)S(1)}, u32[]{:S(2)}, u32[]{:S(2)}) collective-permute-start(f32[16,2,16,256]{3,2,1,0:T(8,128)S(1)} %constant_dynamic-update-slice_fusion.5.refs_2_), channel_id=1, source_target_pairs={{0,1},{1,0},{2,3},{3,2},{4,5},{5,4},{6,7},{7,6},{8,9},{9,8},{10,11... | collective-permute-start | bytes 1572872 | tf_op jit(solution)/shard_map/ppermute | solution.py:301
  26.9 2.0 %collective-permute-start.4 = (f32[16,2,16,256]{3,2,1,0:T(8,128)S(1)}, f32[16,2,16,256]{3,2,1,0:T(8,128)S(1)}, u32[]{:S(2)}, u32[]{:S(2)}) collective-permute-start(f32[16,2,16,256]{3,2,1,0:T(8,128)S(1)} %constant_dynamic-update-slice_fusion.refs_0_), channel_id=1, source_target_pairs={{0,1},{1,0},{2,3},{3,2},{4,5},{5,4},{6,7},{7,6},{8,9},{9,8},{10,11... | collective-permute-start | bytes 1572872 | tf_op jit(solution)/shard_map/ppermute | solution.py:301

commit v3 on v2

--- a/solution.py
+++ b/solution.py
@@ -125,23 +125,31 @@
 
 def exchange_orders(ta_count, tp_count):
     tp_bits = [1 << bit for bit in reversed(range(1, tp_count.bit_length() - 1))]
-    first, middle, last = tp_bits[:1], tp_bits[1:-1], tp_bits[-1:]
-    ta_bit = [tp_count]
+    high, low, ta_bit = tp_bits[:-1], tp_bits[-1:], [tp_count]
+    turned = high[::-1]
     return [
-        (first + middle + last + ta_bit, first + middle + ta_bit + last),
-        (first + middle + ta_bit + last, first + middle + last + ta_bit),
+        (high + low + ta_bit, turned + low + ta_bit),
+        (low + ta_bit + high, low + ta_bit + turned),
     ]
 
 
 def gathered(pieces, orders, count):
+    swap = [(i, i ^ 1) for i in range(count)]
     held = [piece[None] for piece in pieces]
-    for step in range(len(orders[0][0])):
+    near = [[] for _ in pieces]
+    far = [[] for _ in pieces]
+    steps = len(orders[0][0])
+    for step in range(steps):
         for index, (even, odd) in enumerate(orders):
             masks = (even[step], odd[step])
             route = [(i, i ^ masks[i % 2]) for i in range(count)]
             arriving = lax.ppermute(held[index], ("ta", "tp"), route)
-            held[index] = jnp.concatenate([held[index], arriving])
-    return held
+            if step == steps - 1:
+                near[index] = [held[index], arriving]
+                far[index] = [lax.ppermute(part, ("ta", "tp"), swap) for part in near[index]]
+            else:
+                held[index] = jnp.concatenate([held[index], arriving])
+    return [near[index] + far[index] for index in range(len(pieces))]
 
 
 def offsets_of(order):
@@ -199,23 +207,25 @@
         return jnp.concatenate([tile] * (block_rows // NO), axis=1)
 
     def kernel(*refs):
-        sources = refs[: 2 * ta_count]
-        hamiltonian, interaction, out, values, lows, nexts, low_next = refs[2 * ta_count :]
+        sources = refs[: 4 * ta_count]
+        hamiltonian, interaction, out, values, lows, nexts, low_next = refs[4 * ta_count :]
         ta_place = lax.axis_index("ta")
         tp_place = lax.axis_index("tp")
         me = ta_place * tp_count + tp_place
         odd = me % 2
         for group in range(ta_count):
             for flip in range(2):
-                source = sources[2 * group + flip]
                 pair = offsets[group]
-                for index in range(len(pair[0])):
+                steps = len(pair[0])
+                for index in range(steps):
+                    late, slot = divmod(index, steps // 2)
+                    source = sources[4 * group + 2 * flip + late]
                     mask = jnp.where(odd == flip, pair[0][index], pair[1][index])
                     device = (me ^ flip) ^ mask
                     row = pl.multiple_of((device % tp_count) * stripe, stripe)
                     block = device // tp_count
                     for part in range(2):
-                        values[part, block, group, pl.ds(row, stripe), :] = source[index, part]
+                        values[part, block, group, pl.ds(row, stripe), :] = source[slot, part]
         weights = repeated(jnp.transpose(interaction[...] * interaction[...]))
         table = jnp.concatenate([repeated(jnp.transpose(hamiltonian[...]))] * (block_rows // NO))
         same_time = (
@@ -273,7 +283,7 @@
     return pl.pallas_call(
         kernel,
         out_shape=jax.ShapeDtypeStruct((2, ta_count, stripe, block_rows), jnp.float32),
-        in_specs=[pl.BlockSpec(memory_space=pltpu.VMEM)] * (2 * ta_count + 2),
+        in_specs=[pl.BlockSpec(memory_space=pltpu.VMEM)] * (4 * ta_count + 2),
         out_specs=pl.BlockSpec(memory_space=pltpu.VMEM),
         scratch_shapes=[
             pltpu.VMEM(big, jnp.float32),
@@ -294,11 +304,8 @@
     factor = 1.0 / math.sqrt(2 * block_rows)
     orders = exchange_orders(ta_count, tp_count)
     count = ta_count * tp_count
-    held = gathered([green[:, group, 0] for group in range(ta_count)], orders, count)
-    swap = [(i, i ^ 1) for i in range(count)]
-    sources = []
-    for near in held:
-        sources += [near, lax.ppermute(near, ("ta", "tp"), swap)]
+    pieces = [green[:, group, 0] for group in range(ta_count)]
+    sources = sum(gathered(pieces, orders, count), [])
     step = make_iterations(orders, ta_count, tp_count, stripe, block_rows, factor)
     result = step(*sources, hamiltonian, interaction)
     return result[:, :, None]

time: 33.6 us -> 36.5 us (1.086)
  starting transfers between devices: 14.6 us -> 17.9 us
    ppermute x8, starting transfers between devices: 14.4 us -> 17.4 us  [gathered(): arriving = lax.ppermute(held[index], ('ta', 'tp'), route)]
    ppermute x2 -> x4, waiting for transfers between devices: 1.9 us -> 1.52 us  [gathered(): lax.ppermute(part, ('ta', 'tp'), swap)]
    ppermute x2 -> x4, starting transfers between devices: 0.14 us -> 0.52 us  [gathered(): lax.ppermute(part, ('ta', 'tp'), swap)]
  transfers between devices with their start and end apart: 10 -> 12, of which waited for: 9 -> 8; matrix products, arithmetic and copies ran while one was open for 0% -> 0% of each run, Pallas kernels for 0% -> 0%
where the time goes in v3:
time: 36.5 us; the launch traced here: 36.3 us
  starting transfers between devices  17.9 us (49%)
  waiting for transfers between devices  12.9 us (35%)
  Pallas kernels  4.56 us (12%)
  local copies, waits for them, and re-layouts  0.79 us (2%)
    ppermute x8, starting transfers between devices, gathered(): arriving = lax.ppermute(held[index], ('ta', 'tp'), route)  17.4 us
    ppermute x8, waiting for transfers between devices, gathered(): arriving = lax.ppermute(held[index], ('ta', 'tp'), route)  11.4 us
    pallas_call x1, Pallas kernels, replicated(): result = step(*sources, hamiltonian, interaction)  4.56 us
    ppermute x4, waiting for transfers between devices, gathered(): lax.ppermute(part, ('ta', 'tp'), swap)  1.52 us
    another operation x1, local copies, waits for them, and re-layouts, gathered(): held = [piece[None] for piece in pieces]  0.78 us
  transfers between devices with their start and end apart: 12, of which 8 were waited for; matrix products, arithmetic and copies ran while one was open for 0% of the time, Pallas kernels for 0%

profile of v3, /device:TPU:0, one launch (start us, length us, event | category | flops | bytes accessed | tf_op | source)
XLA Modules:
  0.0 36.3 jit_solution(8721244905641460570)
XLA Ops:
  0.0 0.8 %slice_bitcast_fusion = (f32[1,2,16,256]{3,2,1,0:T(8,128)S(1)}, f32[1,2,16,256]{3,2,1,0:T(8,128)S(1)}) fusion(f32[2,2,1,16,256]{4,3,2,1,0:T(8,128)} %param.3), kind=kLoop, calls=%fused_computation.6 | loop fusion | bytes 131072 | tf_op jit(solution)/shard_map/broadcast_in_dim;squeeze | solution.py:138
  0.8 4.1 %collective-permute-start = (f32[1,2,16,256]{3,2,1,0:T(8,128)S(1)}, f32[1,2,16,256]{3,2,1,0:T(8,128)S(1)}, u32[]{:S(2)}, u32[]{:S(2)}) collective-permute-start(f32[1,2,16,256]{3,2,1,0:T(8,128)S(1)} %get-tuple-element.6), channel_id=1, source_target_pairs={{0,8},{1,5},{2,10},{3,7},{4,12},{5,1},{6,14},{7,3},{8,0},{9,13},{1... | collective-permute-start | bytes 98312 | tf_op jit(solution)/shard_map/ppermute | solution.py:146
  4.8 1.5 %collective-permute-start.6 = (f32[1,2,16,256]{3,2,1,0:T(8,128)S(1)}, f32[1,2,16,256]{3,2,1,0:T(8,128)S(1)}, u32[]{:S(2)}, u32[]{:S(2)}) collective-permute-start(f32[1,2,16,256]{3,2,1,0:T(8,128)S(1)} %get-tuple-element.5), channel_id=1, source_target_pairs={{0,2},{1,3},{2,0},{3,1},{4,6},{5,7},{6,4},{7,5},{8,10},{9,11},{10,... | collective-permute-start | bytes 98312 | tf_op jit(solution)/shard_map/ppermute | solution.py:146
  6.4 0.4 %collective-permute-done = f32[1,2,16,256]{3,2,1,0:T(8,128)S(1)} collective-permute-done((f32[1,2,16,256]{3,2,1,0:T(8,128)S(1)}, f32[1,2,16,256]{3,2,1,0:T(8,128)S(1)}, u32[]{:S(2)}, u32[]{:S(2)}) %collective-permute-start) | collective-permute-done | bytes 32800 | tf_op jit(solution)/shard_map/ppermute | solution.py:146
  6.7 1.9 %collective-permute-start.1 = (f32[2,2,16,256]{3,2,1,0:T(8,128)S(1)}, f32[2,2,16,256]{3,2,1,0:T(8,128)S(1)}, u32[]{:S(2)}, u32[]{:S(2)}) collective-permute-start(f32[2,2,16,256]{3,2,1,0:T(8,128)S(1)} %pad_maximum_fusion.4), channel_id=1, source_target_pairs={{0,4},{1,9},{2,6},{3,11},{4,0},{5,13},{6,2},{7,15},{8,12},{9,1},{1... | collective-permute-start | bytes 196616 | tf_op jit(solution)/shard_map/ppermute | solution.py:146
  8.7 0.1 collective-permute-done.6
  8.8 1.5 %collective-permute-start.7 = (f32[2,2,16,256]{3,2,1,0:T(8,128)S(1)}, f32[2,2,16,256]{3,2,1,0:T(8,128)S(1)}, u32[]{:S(2)}, u32[]{:S(2)}) collective-permute-start(f32[2,2,16,256]{3,2,1,0:T(8,128)S(1)} %pad_maximum_fusion.5), channel_id=1, source_target_pairs={{0,16},{1,17},{2,18},{3,19},{4,20},{5,21},{6,22},{7,23},{8,24},{9,... | collective-permute-start | bytes 196616 | tf_op jit(solution)/shard_map/ppermute | solution.py:146
  10.3 0.8 %collective-permute-done.1 = f32[2,2,16,256]{3,2,1,0:T(8,128)S(1)} collective-permute-done((f32[2,2,16,256]{3,2,1,0:T(8,128)S(1)}, f32[2,2,16,256]{3,2,1,0:T(8,128)S(1)}, u32[]{:S(2)}, u32[]{:S(2)}) %collective-permute-start.1) | collective-permute-done | bytes 65568 | tf_op jit(solution)/shard_map/ppermute | solution.py:146
  11.0 1.9 %collective-permute-start.2 = (f32[4,2,16,256]{3,2,1,0:T(8,128)S(1)}, f32[4,2,16,256]{3,2,1,0:T(8,128)S(1)}, u32[]{:S(2)}, u32[]{:S(2)}) collective-permute-start(f32[4,2,16,256]{3,2,1,0:T(8,128)S(1)} %pad_maximum_fusion.2), channel_id=1, source_target_pairs={{0,2},{1,3},{2,0},{3,1},{4,6},{5,7},{6,4},{7,5},{8,10},{9,11},{10,... | collective-permute-start | bytes 393224 | tf_op jit(solution)/shard_map/ppermute | solution.py:146
  12.9 0.1 collective-permute-done.7
  13.0 2.9 %collective-permute-start.8 = (f32[4,2,16,256]{3,2,1,0:T(8,128)S(1)}, f32[4,2,16,256]{3,2,1,0:T(8,128)S(1)}, u32[]{:S(2)}, u32[]{:S(2)}) collective-permute-start(f32[4,2,16,256]{3,2,1,0:T(8,128)S(1)} %pad_maximum_fusion.3), channel_id=1, source_target_pairs={{0,8},{1,5},{2,10},{3,7},{4,12},{5,1},{6,14},{7,3},{8,0},{9,13},{1... | collective-permute-start | bytes 393224 | tf_op jit(solution)/shard_map/ppermute | solution.py:146
  15.9 0.2 collective-permute-done.2
  16.1 0.0 copy-start
  16.1 0.0 copy-start.1
  16.1 1.9 %collective-permute-start.3 = (f32[8,2,16,256]{3,2,1,0:T(8,128)S(1)}, f32[8,2,16,256]{3,2,1,0:T(8,128)S(1)}, u32[]{:S(2)}, u32[]{:S(2)}) collective-permute-start(f32[8,2,16,256]{3,2,1,0:T(8,128)S(1)} %pad_maximum_fusion.refs_0_), channel_id=1, source_target_pairs={{0,16},{1,17},{2,18},{3,19},{4,20},{5,21},{6,22},{7,23},{8,24},{9,... | collective-permute-start | bytes 786440 | tf_op jit(solution)/shard_map/ppermute | solution.py:146
  18.0 5.7 %collective-permute-done.8 = f32[4,2,16,256]{3,2,1,0:T(8,128)S(1)} collective-permute-done((f32[4,2,16,256]{3,2,1,0:T(8,128)S(1)}, f32[4,2,16,256]{3,2,1,0:T(8,128)S(1)}, u32[]{:S(2)}, u32[]{:S(2)}) %collective-permute-start.8) | collective-permute-done | bytes 131104 | tf_op jit(solution)/shard_map/ppermute | solution.py:146
  23.8 1.7 %collective-permute-start.9 = (f32[8,2,16,256]{3,2,1,0:T(8,128)S(1)}, f32[8,2,16,256]{3,2,1,0:T(8,128)S(1)}, u32[]{:S(2)}, u32[]{:S(2)}) collective-permute-start(f32[8,2,16,256]{3,2,1,0:T(8,128)S(1)} %pad_maximum_fusion.1.refs_4_), channel_id=1, source_target_pairs={{0,4},{1,9},{2,6},{3,11},{4,0},{5,13},{6,2},{7,15},{8,12},{9,1},{1... | collective-permute-start | bytes 786440 | tf_op jit(solution)/shard_map/ppermute | solution.py:146
  25.5 0.0 collective-permute-start.4
  25.5 0.5 %collective-permute-start.10 = (f32[8,2,16,256]{3,2,1,0:T(8,128)S(1)}, f32[8,2,16,256]{3,2,1,0:T(8,128)S(1)}, u32[]{:S(2)}, u32[]{:S(2)}) collective-permute-start(f32[8,2,16,256]{3,2,1,0:T(8,128)S(1)} %pad_maximum_fusion.1.refs_4_), channel_id=1, source_target_pairs={{0,1},{1,0},{2,3},{3,2},{4,5},{5,4},{6,7},{7,6},{8,9},{9,8},{10,11... | collective-permute-start | bytes 786440 | tf_op jit(solution)/shard_map/ppermute | solution.py:149
  26.0 0.0 collective-permute-done.3.refs_1_
  26.0 0.0 collective-permute-start.5
  26.0 4.2 %collective-permute-done.9.refs_5_ = f32[8,2,16,256]{3,2,1,0:T(8,128)S(1)} collective-permute-done((f32[8,2,16,256]{3,2,1,0:T(8,128)S(1)}, f32[8,2,16,256]{3,2,1,0:T(8,128)S(1)}, u32[]{:S(2)}, u32[]{:S(2)}) %collective-permute-start.9) | collective-permute-done | bytes 262176 | tf_op jit(solution)/shard_map/ppermute | solution.py:146
  30.2 0.0 collective-permute-start.11
  30.2 0.0 collective-permute-done.4.refs_2_
  30.2 0.0 collective-permute-done.10.refs_6_
  30.2 0.0 collective-permute-done.5.refs_3_
  30.2 1.5 %collective-permute-done.11.refs_7_ = f32[8,2,16,256]{3,2,1,0:T(8,128)S(1)} collective-permute-done((f32[8,2,16,256]{3,2,1,0:T(8,128)S(1)}, f32[8,2,16,256]{3,2,1,0:T(8,128)S(1)}, u32[]{:S(2)}, u32[]{:S(2)}) %collective-permute-start.11) | collective-permute-done | bytes 262176 | tf_op jit(solution)/shard_map/ppermute | solution.py:149
  31.7 0.0 copy-done
  31.7 0.0 copy-done.1
  31.7 4.6 %iterations.1 = f32[2,2,16,256]{3,2,1,0:T(8,128)} custom-call(f32[8,2,16,256]{3,2,1,0:T(8,128)S(1)} %pad_maximum_fusion.refs_0_, f32[8,2,16,256]{3,2,1,0:T(8,128)S(1)} %collective-permute-done.3.refs_1_, f32[8,2,16,256]{3,2,1,0:T(8,128)S(1)} %collective-permute-done.4.refs_2_, f32[8,2,16,256]{3,2,1,0:T(8,128)S(1)} %collective-permute-done.5.refs_3_, ...), custom_call_target="tpu_custom_call" | custom-call | tf_op jit(solution)/shard_map/iterations/pallas_call | solution.py:310
  (6 shorter events, 0.1 us)
Async XLA Ops:
  0.8 6.0 %collective-permute-start = (f32[1,2,16,256]{3,2,1,0:T(8,128)S(1)}, f32[1,2,16,256]{3,2,1,0:T(8,128)S(1)}, u32[]{:S(2)}, u32[]{:S(2)}) collective-permute-start(f32[1,2,16,256]{3,2,1,0:T(8,128)S(1)} %get-tuple-element.6), channel_id=1, source_target_pairs={{0,8},{1,5},{2,10},{3,7},{4,12},{5,1},{6,14},{7,3},{8,0},{9,13},{1... | collective-permute-start | bytes 98312 | tf_op jit(solution)/shard_map/ppermute | solution.py:146
  4.8 3.9 %collective-permute-start.6 = (f32[1,2,16,256]{3,2,1,0:T(8,128)S(1)}, f32[1,2,16,256]{3,2,1,0:T(8,128)S(1)}, u32[]{:S(2)}, u32[]{:S(2)}) collective-permute-start(f32[1,2,16,256]{3,2,1,0:T(8,128)S(1)} %get-tuple-element.5), channel_id=1, source_target_pairs={{0,2},{1,3},{2,0},{3,1},{4,6},{5,7},{6,4},{7,5},{8,10},{9,11},{10,... | collective-permute-start | bytes 98312 | tf_op jit(solution)/shard_map/ppermute | solution.py:146
  6.7 4.3 %collective-permute-start.1 = (f32[2,2,16,256]{3,2,1,0:T(8,128)S(1)}, f32[2,2,16,256]{3,2,1,0:T(8,128)S(1)}, u32[]{:S(2)}, u32[]{:S(2)}) collective-permute-start(f32[2,2,16,256]{3,2,1,0:T(8,128)S(1)} %pad_maximum_fusion.4), channel_id=1, source_target_pairs={{0,4},{1,9},{2,6},{3,11},{4,0},{5,13},{6,2},{7,15},{8,12},{9,1},{1... | collective-permute-start | bytes 196616 | tf_op jit(solution)/shard_map/ppermute | solution.py:146
  8.8 4.3 %collective-permute-start.7 = (f32[2,2,16,256]{3,2,1,0:T(8,128)S(1)}, f32[2,2,16,256]{3,2,1,0:T(8,128)S(1)}, u32[]{:S(2)}, u32[]{:S(2)}) collective-permute-start(f32[2,2,16,256]{3,2,1,0:T(8,128)S(1)} %pad_maximum_fusion.5), channel_id=1, source_target_pairs={{0,16},{1,17},{2,18},{3,19},{4,20},{5,21},{6,22},{7,23},{8,24},{9,... | collective-permute-start | bytes 196616 | tf_op jit(solution)/shard_map/ppermute | solution.py:146
  11.0 5.0 %collective-permute-start.2 = (f32[4,2,16,256]{3,2,1,0:T(8,128)S(1)}, f32[4,2,16,256]{3,2,1,0:T(8,128)S(1)}, u32[]{:S(2)}, u32[]{:S(2)}) collective-permute-start(f32[4,2,16,256]{3,2,1,0:T(8,128)S(1)} %pad_maximum_fusion.2), channel_id=1, source_target_pairs={{0,2},{1,3},{2,0},{3,1},{4,6},{5,7},{6,4},{7,5},{8,10},{9,11},{10,... | collective-permute-start | bytes 393224 | tf_op jit(solution)/shard_map/ppermute | solution.py:146
  13.0 10.7 %collective-permute-start.8 = (f32[4,2,16,256]{3,2,1,0:T(8,128)S(1)}, f32[4,2,16,256]{3,2,1,0:T(8,128)S(1)}, u32[]{:S(2)}, u32[]{:S(2)}) collective-permute-start(f32[4,2,16,256]{3,2,1,0:T(8,128)S(1)} %pad_maximum_fusion.3), channel_id=1, source_target_pairs={{0,8},{1,5},{2,10},{3,7},{4,12},{5,1},{6,14},{7,3},{8,0},{9,13},{1... | collective-permute-start | bytes 393224 | tf_op jit(solution)/shard_map/ppermute | solution.py:146
  16.1 15.7 %copy-start = (f32[32,32]{1,0:T(8,128)S(1)}, f32[32,32]{1,0:T(8,128)}, u32[]{:S(2)}) copy-start(f32[32,32]{1,0:T(8,128)} %refs_8_.1) | copy-start | bytes 12292
  16.1 15.6 %copy-start.1 = (f32[32,32]{1,0:T(8,128)S(1)}, f32[32,32]{1,0:T(8,128)}, u32[]{:S(2)}) copy-start(f32[32,32]{1,0:T(8,128)} %refs_9_.1) | copy-start | bytes 12292
  16.1 9.9 %collective-permute-start.3 = (f32[8,2,16,256]{3,2,1,0:T(8,128)S(1)}, f32[8,2,16,256]{3,2,1,0:T(8,128)S(1)}, u32[]{:S(2)}, u32[]{:S(2)}) collective-permute-start(f32[8,2,16,256]{3,2,1,0:T(8,128)S(1)} %pad_maximum_fusion.refs_0_), channel_id=1, source_target_pairs={{0,16},{1,17},{2,18},{3,19},{4,20},{5,21},{6,22},{7,23},{8,24},{9,... | collective-permute-start | bytes 786440 | tf_op jit(solution)/shard_map/ppermute | solution.py:146
  23.8 6.4 %collective-permute-start.9 = (f32[8,2,16,256]{3,2,1,0:T(8,128)S(1)}, f32[8,2,16,256]{3,2,1,0:T(8,128)S(1)}, u32[]{:S(2)}, u32[]{:S(2)}) collective-permute-start(f32[8,2,16,256]{3,2,1,0:T(8,128)S(1)} %pad_maximum_fusion.1.refs_4_), channel_id=1, source_target_pairs={{0,4},{1,9},{2,6},{3,11},{4,0},{5,13},{6,2},{7,15},{8,12},{9,1},{1... | collective-permute-start | bytes 786440 | tf_op jit(solution)/shard_map/ppermute | solution.py:146
  25.5 4.7 %collective-permute-start.4 = (f32[8,2,16,256]{3,2,1,0:T(8,128)S(1)}, f32[8,2,16,256]{3,2,1,0:T(8,128)S(1)}, u32[]{:S(2)}, u32[]{:S(2)}) collective-permute-start(f32[8,2,16,256]{3,2,1,0:T(8,128)S(1)} %pad_maximum_fusion.refs_0_), channel_id=1, source_target_pairs={{0,1},{1,0},{2,3},{3,2},{4,5},{5,4},{6,7},{7,6},{8,9},{9,8},{10,11... | collective-permute-start | bytes 786440 | tf_op jit(solution)/shard_map/ppermute | solution.py:149
  25.5 4.7 %collective-permute-start.10 = (f32[8,2,16,256]{3,2,1,0:T(8,128)S(1)}, f32[8,2,16,256]{3,2,1,0:T(8,128)S(1)}, u32[]{:S(2)}, u32[]{:S(2)}) collective-permute-start(f32[8,2,16,256]{3,2,1,0:T(8,128)S(1)} %pad_maximum_fusion.1.refs_4_), channel_id=1, source_target_pairs={{0,1},{1,0},{2,3},{3,2},{4,5},{5,4},{6,7},{7,6},{8,9},{9,8},{10,11... | collective-permute-start | bytes 786440 | tf_op jit(solution)/shard_map/ppermute | solution.py:149
  26.0 4.2 %collective-permute-start.5 = (f32[8,2,16,256]{3,2,1,0:T(8,128)S(1)}, f32[8,2,16,256]{3,2,1,0:T(8,128)S(1)}, u32[]{:S(2)}, u32[]{:S(2)}) collective-permute-start(f32[8,2,16,256]{3,2,1,0:T(8,128)S(1)} %collective-permute-done.3.refs_1_), channel_id=1, source_target_pairs={{0,1},{1,0},{2,3},{3,2},{4,5},{5,4},{6,7},{7,6},{8,9},{9,8},{10,11... | collective-permute-start | bytes 786440 | tf_op jit(solution)/shard_map/ppermute | solution.py:149
  30.2 1.5 %collective-permute-start.11 = (f32[8,2,16,256]{3,2,1,0:T(8,128)S(1)}, f32[8,2,16,256]{3,2,1,0:T(8,128)S(1)}, u32[]{:S(2)}, u32[]{:S(2)}) collective-permute-start(f32[8,2,16,256]{3,2,1,0:T(8,128)S(1)} %collective-permute-done.9.refs_5_), channel_id=1, source_target_pairs={{0,1},{1,0},{2,3},{3,2},{4,5},{5,4},{6,7},{7,6},{8,9},{9,8},{10,11... | collective-permute-start | bytes 786440 | tf_op jit(solution)/shard_map/ppermute | solution.py:149

commit v4 on v3

--- a/solution.py
+++ b/solution.py
@@ -125,11 +125,10 @@
 
 def exchange_orders(ta_count, tp_count):
     tp_bits = [1 << bit for bit in reversed(range(1, tp_count.bit_length() - 1))]
-    high, low, ta_bit = tp_bits[:-1], tp_bits[-1:], [tp_count]
-    turned = high[::-1]
+    first, middle, last, ta_bit = tp_bits[:1], tp_bits[1:-1], tp_bits[-1:], [tp_count]
     return [
-        (high + low + ta_bit, turned + low + ta_bit),
-        (low + ta_bit + high, low + ta_bit + turned),
+        (first + last + ta_bit + middle,) * 2,
+        (ta_bit + first + middle + last,) * 2,
     ]
 
 
@@ -244,11 +243,18 @@
         rounded = [lows[part].reshape(order_size, order_size) for part in range(2)]
         for block in range(ta_count):
             current = [values[part, block].reshape(order_size, block_rows) for part in range(2)]
+            width = (block + 1) * block_rows
             mirror = [
-                jnp.transpose(lows[part, block].astype(jnp.float32)) for part in range(2)
+                jnp.transpose(lows[part, block, :, :width].astype(jnp.float32))
+                for part in range(2)
             ]
-            window = window_of(current, mirror, weights, block * (block_rows // NO))
-            memory = products(rounded, window)
+            window = window_of(
+                [current[part][:width] for part in range(2)],
+                mirror,
+                weights,
+                block * (block_rows // NO),
+            )
+            memory = products([rounded[part][:, :width] for part in range(2)], window)
             hamilton = [rotated(current[part], high_table, low_table) for part in range(2)]
             shape = (ta_count, block_rows, block_rows)
             next_real = current[0] + 0.5 * (hamilton[1] + factor * memory[1])
@@ -319,7 +325,7 @@
 
     def shards(green, hamiltonian, interaction):
         whole_bytes = green.size * green.dtype.itemsize * ta_count * tp_count
-        covered = ta_count == 2 and green.shape[1] == 2 and tp_count >= 4
+        covered = ta_count == 2 and green.shape[1] == 2 and tp_count >= 8
         if covered and tp_count & (tp_count - 1) == 0 and whole_bytes <= 1 << 22:
             return replicated(green, hamiltonian, interaction)
         return windowed(green, hamiltonian, interaction)

time: 36.5 us -> 32.9 us (0.901)
  starting transfers between devices: 17.9 us -> 16.1 us
  waiting for transfers between devices: 12.9 us -> 11.5 us
    ppermute x8, starting transfers between devices: 17.4 us -> 15.6 us  [gathered(): arriving = lax.ppermute(held[index], ('ta', 'tp'), route)]
    ppermute x8, waiting for transfers between devices: 11.4 us -> 10 us  [gathered(): arriving = lax.ppermute(held[index], ('ta', 'tp'), route)]
where the time goes in v4:
time: 32.9 us; the launch traced here: 32.8 us
  starting transfers between devices  16.1 us (49%)
  waiting for transfers between devices  11.5 us (35%)
  Pallas kernels  4.23 us (13%)
  local copies, waits for them, and re-layouts  0.79 us (2%)
    ppermute x8, starting transfers between devices, gathered(): arriving = lax.ppermute(held[index], ('ta', 'tp'), route)  15.6 us
    ppermute x8, waiting for transfers between devices, gathered(): arriving = lax.ppermute(held[index], ('ta', 'tp'), route)  10 us
    pallas_call x1, Pallas kernels, replicated(): result = step(*sources, hamiltonian, interaction)  4.23 us
    ppermute x4, waiting for transfers between devices, gathered(): lax.ppermute(part, ('ta', 'tp'), swap)  1.52 us
    another operation x1, local copies, waits for them, and re-layouts, gathered(): held = [piece[None] for piece in pieces]  0.78 us
  transfers between devices with their start and end apart: 12, of which 8 were waited for; matrix products, arithmetic and copies ran while one was open for 0% of the time, Pallas kernels for 0%

profile of v4, /device:TPU:0, one launch (start us, length us, event | category | flops | bytes accessed | tf_op | source)
XLA Modules:
  0.0 32.8 jit_solution(2296833700603090318)
XLA Ops:
  0.0 0.8 %slice_bitcast_fusion = (f32[1,2,16,256]{3,2,1,0:T(8,128)S(1)}, f32[1,2,16,256]{3,2,1,0:T(8,128)S(1)}) fusion(f32[2,2,1,16,256]{4,3,2,1,0:T(8,128)} %param.3), kind=kLoop, calls=%fused_computation.6 | loop fusion | bytes 131072 | tf_op jit(solution)/shard_map/broadcast_in_dim;squeeze | solution.py:137
  0.8 4.1 %collective-permute-start = (f32[1,2,16,256]{3,2,1,0:T(8,128)S(1)}, f32[1,2,16,256]{3,2,1,0:T(8,128)S(1)}, u32[]{:S(2)}, u32[]{:S(2)}) collective-permute-start(f32[1,2,16,256]{3,2,1,0:T(8,128)S(1)} %get-tuple-element.6), channel_id=1, source_target_pairs={{0,8},{1,9},{2,10},{3,11},{4,12},{5,13},{6,14},{7,15},{8,0},{9,1},... | collective-permute-start | bytes 98312 | tf_op jit(solution)/shard_map/ppermute | solution.py:145
  4.8 1.5 %collective-permute-start.6 = (f32[1,2,16,256]{3,2,1,0:T(8,128)S(1)}, f32[1,2,16,256]{3,2,1,0:T(8,128)S(1)}, u32[]{:S(2)}, u32[]{:S(2)}) collective-permute-start(f32[1,2,16,256]{3,2,1,0:T(8,128)S(1)} %get-tuple-element.5), channel_id=1, source_target_pairs={{0,16},{1,17},{2,18},{3,19},{4,20},{5,21},{6,22},{7,23},{8,24},{9,... | collective-permute-start | bytes 98312 | tf_op jit(solution)/shard_map/ppermute | solution.py:145
  6.3 0.8 %collective-permute-done = f32[1,2,16,256]{3,2,1,0:T(8,128)S(1)} collective-permute-done((f32[1,2,16,256]{3,2,1,0:T(8,128)S(1)}, f32[1,2,16,256]{3,2,1,0:T(8,128)S(1)}, u32[]{:S(2)}, u32[]{:S(2)}) %collective-permute-start) | collective-permute-done | bytes 32800 | tf_op jit(solution)/shard_map/ppermute | solution.py:145
  7.1 1.7 %collective-permute-start.1 = (f32[2,2,16,256]{3,2,1,0:T(8,128)S(1)}, f32[2,2,16,256]{3,2,1,0:T(8,128)S(1)}, u32[]{:S(2)}, u32[]{:S(2)}) collective-permute-start(f32[2,2,16,256]{3,2,1,0:T(8,128)S(1)} %pad_maximum_fusion.4), channel_id=1, source_target_pairs={{0,2},{1,3},{2,0},{3,1},{4,6},{5,7},{6,4},{7,5},{8,10},{9,11},{10,... | collective-permute-start | bytes 196616 | tf_op jit(solution)/shard_map/ppermute | solution.py:145
  8.8 0.0 collective-permute-done.6
  8.8 2.4 %collective-permute-start.7 = (f32[2,2,16,256]{3,2,1,0:T(8,128)S(1)}, f32[2,2,16,256]{3,2,1,0:T(8,128)S(1)}, u32[]{:S(2)}, u32[]{:S(2)}) collective-permute-start(f32[2,2,16,256]{3,2,1,0:T(8,128)S(1)} %pad_maximum_fusion.5), channel_id=1, source_target_pairs={{0,8},{1,9},{2,10},{3,11},{4,12},{5,13},{6,14},{7,15},{8,0},{9,1},... | collective-permute-start | bytes 196616 | tf_op jit(solution)/shard_map/ppermute | solution.py:145
  11.3 0.1 collective-permute-done.1
  11.4 1.8 %collective-permute-start.2 = (f32[4,2,16,256]{3,2,1,0:T(8,128)S(1)}, f32[4,2,16,256]{3,2,1,0:T(8,128)S(1)}, u32[]{:S(2)}, u32[]{:S(2)}) collective-permute-start(f32[4,2,16,256]{3,2,1,0:T(8,128)S(1)} %pad_maximum_fusion.2), channel_id=1, source_target_pairs={{0,16},{1,17},{2,18},{3,19},{4,20},{5,21},{6,22},{7,23},{8,24},{9,... | collective-permute-start | bytes 393224 | tf_op jit(solution)/shard_map/ppermute | solution.py:145
  13.1 0.9 %collective-permute-done.7 = f32[2,2,16,256]{3,2,1,0:T(8,128)S(1)} collective-permute-done((f32[2,2,16,256]{3,2,1,0:T(8,128)S(1)}, f32[2,2,16,256]{3,2,1,0:T(8,128)S(1)}, u32[]{:S(2)}, u32[]{:S(2)}) %collective-permute-start.7) | collective-permute-done | bytes 65568 | tf_op jit(solution)/shard_map/ppermute | solution.py:145
  14.1 1.5 %collective-permute-start.8 = (f32[4,2,16,256]{3,2,1,0:T(8,128)S(1)}, f32[4,2,16,256]{3,2,1,0:T(8,128)S(1)}, u32[]{:S(2)}, u32[]{:S(2)}) collective-permute-start(f32[4,2,16,256]{3,2,1,0:T(8,128)S(1)} %pad_maximum_fusion.3), channel_id=1, source_target_pairs={{0,4},{1,5},{2,6},{3,7},{4,0},{5,1},{6,2},{7,3},{8,12},{9,13},{10,... | collective-permute-start | bytes 393224 | tf_op jit(solution)/shard_map/ppermute | solution.py:145
  15.6 0.8 %collective-permute-done.2 = f32[4,2,16,256]{3,2,1,0:T(8,128)S(1)} collective-permute-done((f32[4,2,16,256]{3,2,1,0:T(8,128)S(1)}, f32[4,2,16,256]{3,2,1,0:T(8,128)S(1)}, u32[]{:S(2)}, u32[]{:S(2)}) %collective-permute-start.2) | collective-permute-done | bytes 131104 | tf_op jit(solution)/shard_map/ppermute | solution.py:145
  16.4 0.0 copy-start
  16.4 0.0 copy-start.1
  16.5 1.8 %collective-permute-start.3 = (f32[8,2,16,256]{3,2,1,0:T(8,128)S(1)}, f32[8,2,16,256]{3,2,1,0:T(8,128)S(1)}, u32[]{:S(2)}, u32[]{:S(2)}) collective-permute-start(f32[8,2,16,256]{3,2,1,0:T(8,128)S(1)} %pad_maximum_fusion.refs_0_), channel_id=1, source_target_pairs={{0,4},{1,5},{2,6},{3,7},{4,0},{5,1},{6,2},{7,3},{8,12},{9,13},{10,... | collective-permute-start | bytes 786440 | tf_op jit(solution)/shard_map/ppermute | solution.py:145
  18.2 2.3 %collective-permute-done.8 = f32[4,2,16,256]{3,2,1,0:T(8,128)S(1)} collective-permute-done((f32[4,2,16,256]{3,2,1,0:T(8,128)S(1)}, f32[4,2,16,256]{3,2,1,0:T(8,128)S(1)}, u32[]{:S(2)}, u32[]{:S(2)}) %collective-permute-start.8) | collective-permute-done | bytes 131104 | tf_op jit(solution)/shard_map/ppermute | solution.py:145
  20.6 0.8 %collective-permute-start.9 = (f32[8,2,16,256]{3,2,1,0:T(8,128)S(1)}, f32[8,2,16,256]{3,2,1,0:T(8,128)S(1)}, u32[]{:S(2)}, u32[]{:S(2)}) collective-permute-start(f32[8,2,16,256]{3,2,1,0:T(8,128)S(1)} %pad_maximum_fusion.1.refs_4_), channel_id=1, source_target_pairs={{0,2},{1,3},{2,0},{3,1},{4,6},{5,7},{6,4},{7,5},{8,10},{9,11},{10,... | collective-permute-start | bytes 786440 | tf_op jit(solution)/shard_map/ppermute | solution.py:145
  21.3 0.0 collective-permute-start.4
  21.3 0.5 %collective-permute-start.10 = (f32[8,2,16,256]{3,2,1,0:T(8,128)S(1)}, f32[8,2,16,256]{3,2,1,0:T(8,128)S(1)}, u32[]{:S(2)}, u32[]{:S(2)}) collective-permute-start(f32[8,2,16,256]{3,2,1,0:T(8,128)S(1)} %pad_maximum_fusion.1.refs_4_), channel_id=1, source_target_pairs={{0,1},{1,0},{2,3},{3,2},{4,5},{5,4},{6,7},{7,6},{8,9},{9,8},{10,11... | collective-permute-start | bytes 786440 | tf_op jit(solution)/shard_map/ppermute | solution.py:148
  21.8 1.5 %collective-permute-done.3.refs_1_ = f32[8,2,16,256]{3,2,1,0:T(8,128)S(1)} collective-permute-done((f32[8,2,16,256]{3,2,1,0:T(8,128)S(1)}, f32[8,2,16,256]{3,2,1,0:T(8,128)S(1)}, u32[]{:S(2)}, u32[]{:S(2)}) %collective-permute-start.3) | collective-permute-done | bytes 262176 | tf_op jit(solution)/shard_map/ppermute | solution.py:145
  23.4 0.0 collective-permute-start.5
  23.4 3.6 %collective-permute-done.9.refs_5_ = f32[8,2,16,256]{3,2,1,0:T(8,128)S(1)} collective-permute-done((f32[8,2,16,256]{3,2,1,0:T(8,128)S(1)}, f32[8,2,16,256]{3,2,1,0:T(8,128)S(1)}, u32[]{:S(2)}, u32[]{:S(2)}) %collective-permute-start.9) | collective-permute-done | bytes 262176 | tf_op jit(solution)/shard_map/ppermute | solution.py:145
  27.0 0.0 collective-permute-start.11
  27.0 0.0 collective-permute-done.4.refs_2_
  27.0 0.0 collective-permute-done.10.refs_6_
  27.0 0.0 collective-permute-done.5.refs_3_
  27.0 1.5 %collective-permute-done.11.refs_7_ = f32[8,2,16,256]{3,2,1,0:T(8,128)S(1)} collective-permute-done((f32[8,2,16,256]{3,2,1,0:T(8,128)S(1)}, f32[8,2,16,256]{3,2,1,0:T(8,128)S(1)}, u32[]{:S(2)}, u32[]{:S(2)}) %collective-permute-start.11) | collective-permute-done | bytes 262176 | tf_op jit(solution)/shard_map/ppermute | solution.py:148
  28.5 0.0 copy-done
  28.5 0.0 copy-done.1
  28.5 4.2 %iterations.1 = f32[2,2,16,256]{3,2,1,0:T(8,128)} custom-call(f32[8,2,16,256]{3,2,1,0:T(8,128)S(1)} %pad_maximum_fusion.refs_0_, f32[8,2,16,256]{3,2,1,0:T(8,128)S(1)} %collective-permute-done.3.refs_1_, f32[8,2,16,256]{3,2,1,0:T(8,128)S(1)} %collective-permute-done.4.refs_2_, f32[8,2,16,256]{3,2,1,0:T(8,128)S(1)} %collective-permute-done.5.refs_3_, ...), custom_call_target="tpu_custom_call" | custom-call | tf_op jit(solution)/shard_map/iterations/pallas_call | solution.py:316
  (6 shorter events, 0.1 us)
Async XLA Ops:
  0.8 6.3 %collective-permute-start = (f32[1,2,16,256]{3,2,1,0:T(8,128)S(1)}, f32[1,2,16,256]{3,2,1,0:T(8,128)S(1)}, u32[]{:S(2)}, u32[]{:S(2)}) collective-permute-start(f32[1,2,16,256]{3,2,1,0:T(8,128)S(1)} %get-tuple-element.6), channel_id=1, source_target_pairs={{0,8},{1,9},{2,10},{3,11},{4,12},{5,13},{6,14},{7,15},{8,0},{9,1},... | collective-permute-start | bytes 98312 | tf_op jit(solution)/shard_map/ppermute | solution.py:145
  4.8 4.0 %collective-permute-start.6 = (f32[1,2,16,256]{3,2,1,0:T(8,128)S(1)}, f32[1,2,16,256]{3,2,1,0:T(8,128)S(1)}, u32[]{:S(2)}, u32[]{:S(2)}) collective-permute-start(f32[1,2,16,256]{3,2,1,0:T(8,128)S(1)} %get-tuple-element.5), channel_id=1, source_target_pairs={{0,16},{1,17},{2,18},{3,19},{4,20},{5,21},{6,22},{7,23},{8,24},{9,... | collective-permute-start | bytes 98312 | tf_op jit(solution)/shard_map/ppermute | solution.py:145
  7.1 4.3 %collective-permute-start.1 = (f32[2,2,16,256]{3,2,1,0:T(8,128)S(1)}, f32[2,2,16,256]{3,2,1,0:T(8,128)S(1)}, u32[]{:S(2)}, u32[]{:S(2)}) collective-permute-start(f32[2,2,16,256]{3,2,1,0:T(8,128)S(1)} %pad_maximum_fusion.4), channel_id=1, source_target_pairs={{0,2},{1,3},{2,0},{3,1},{4,6},{5,7},{6,4},{7,5},{8,10},{9,11},{10,... | collective-permute-start | bytes 196616 | tf_op jit(solution)/shard_map/ppermute | solution.py:145
  8.8 5.2 %collective-permute-start.7 = (f32[2,2,16,256]{3,2,1,0:T(8,128)S(1)}, f32[2,2,16,256]{3,2,1,0:T(8,128)S(1)}, u32[]{:S(2)}, u32[]{:S(2)}) collective-permute-start(f32[2,2,16,256]{3,2,1,0:T(8,128)S(1)} %pad_maximum_fusion.5), channel_id=1, source_target_pairs={{0,8},{1,9},{2,10},{3,11},{4,12},{5,13},{6,14},{7,15},{8,0},{9,1},... | collective-permute-start | bytes 196616 | tf_op jit(solution)/shard_map/ppermute | solution.py:145
  11.4 5.0 %collective-permute-start.2 = (f32[4,2,16,256]{3,2,1,0:T(8,128)S(1)}, f32[4,2,16,256]{3,2,1,0:T(8,128)S(1)}, u32[]{:S(2)}, u32[]{:S(2)}) collective-permute-start(f32[4,2,16,256]{3,2,1,0:T(8,128)S(1)} %pad_maximum_fusion.2), channel_id=1, source_target_pairs={{0,16},{1,17},{2,18},{3,19},{4,20},{5,21},{6,22},{7,23},{8,24},{9,... | collective-permute-start | bytes 393224 | tf_op jit(solution)/shard_map/ppermute | solution.py:145
  14.1 6.4 %collective-permute-start.8 = (f32[4,2,16,256]{3,2,1,0:T(8,128)S(1)}, f32[4,2,16,256]{3,2,1,0:T(8,128)S(1)}, u32[]{:S(2)}, u32[]{:S(2)}) collective-permute-start(f32[4,2,16,256]{3,2,1,0:T(8,128)S(1)} %pad_maximum_fusion.3), channel_id=1, source_target_pairs={{0,4},{1,5},{2,6},{3,7},{4,0},{5,1},{6,2},{7,3},{8,12},{9,13},{10,... | collective-permute-start | bytes 393224 | tf_op jit(solution)/shard_map/ppermute | solution.py:145
  16.4 12.1 %copy-start = (f32[32,32]{1,0:T(8,128)S(1)}, f32[32,32]{1,0:T(8,128)}, u32[]{:S(2)}) copy-start(f32[32,32]{1,0:T(8,128)} %refs_8_.1) | copy-start | bytes 12292
  16.4 12.1 %copy-start.1 = (f32[32,32]{1,0:T(8,128)S(1)}, f32[32,32]{1,0:T(8,128)}, u32[]{:S(2)}) copy-start(f32[32,32]{1,0:T(8,128)} %refs_9_.1) | copy-start | bytes 12292
  16.5 6.9 %collective-permute-start.3 = (f32[8,2,16,256]{3,2,1,0:T(8,128)S(1)}, f32[8,2,16,256]{3,2,1,0:T(8,128)S(1)}, u32[]{:S(2)}, u32[]{:S(2)}) collective-permute-start(f32[8,2,16,256]{3,2,1,0:T(8,128)S(1)} %pad_maximum_fusion.refs_0_), channel_id=1, source_target_pairs={{0,4},{1,5},{2,6},{3,7},{4,0},{5,1},{6,2},{7,3},{8,12},{9,13},{10,... | collective-permute-start | bytes 786440 | tf_op jit(solution)/shard_map/ppermute | solution.py:145
  20.6 6.4 %collective-permute-start.9 = (f32[8,2,16,256]{3,2,1,0:T(8,128)S(1)}, f32[8,2,16,256]{3,2,1,0:T(8,128)S(1)}, u32[]{:S(2)}, u32[]{:S(2)}) collective-permute-start(f32[8,2,16,256]{3,2,1,0:T(8,128)S(1)} %pad_maximum_fusion.1.refs_4_), channel_id=1, source_target_pairs={{0,2},{1,3},{2,0},{3,1},{4,6},{5,7},{6,4},{7,5},{8,10},{9,11},{10,... | collective-permute-start | bytes 786440 | tf_op jit(solution)/shard_map/ppermute | solution.py:145
  21.3 5.7 %collective-permute-start.4 = (f32[8,2,16,256]{3,2,1,0:T(8,128)S(1)}, f32[8,2,16,256]{3,2,1,0:T(8,128)S(1)}, u32[]{:S(2)}, u32[]{:S(2)}) collective-permute-start(f32[8,2,16,256]{3,2,1,0:T(8,128)S(1)} %pad_maximum_fusion.refs_0_), channel_id=1, source_target_pairs={{0,1},{1,0},{2,3},{3,2},{4,5},{5,4},{6,7},{7,6},{8,9},{9,8},{10,11... | collective-permute-start | bytes 786440 | tf_op jit(solution)/shard_map/ppermute | solution.py:148
  21.3 5.7 %collective-permute-start.10 = (f32[8,2,16,256]{3,2,1,0:T(8,128)S(1)}, f32[8,2,16,256]{3,2,1,0:T(8,128)S(1)}, u32[]{:S(2)}, u32[]{:S(2)}) collective-permute-start(f32[8,2,16,256]{3,2,1,0:T(8,128)S(1)} %pad_maximum_fusion.1.refs_4_), channel_id=1, source_target_pairs={{0,1},{1,0},{2,3},{3,2},{4,5},{5,4},{6,7},{7,6},{8,9},{9,8},{10,11... | collective-permute-start | bytes 786440 | tf_op jit(solution)/shard_map/ppermute | solution.py:148
  23.4 3.6 %collective-permute-start.5 = (f32[8,2,16,256]{3,2,1,0:T(8,128)S(1)}, f32[8,2,16,256]{3,2,1,0:T(8,128)S(1)}, u32[]{:S(2)}, u32[]{:S(2)}) collective-permute-start(f32[8,2,16,256]{3,2,1,0:T(8,128)S(1)} %collective-permute-done.3.refs_1_), channel_id=1, source_target_pairs={{0,1},{1,0},{2,3},{3,2},{4,5},{5,4},{6,7},{7,6},{8,9},{9,8},{10,11... | collective-permute-start | bytes 786440 | tf_op jit(solution)/shard_map/ppermute | solution.py:148
  27.0 1.5 %collective-permute-start.11 = (f32[8,2,16,256]{3,2,1,0:T(8,128)S(1)}, f32[8,2,16,256]{3,2,1,0:T(8,128)S(1)}, u32[]{:S(2)}, u32[]{:S(2)}) collective-permute-start(f32[8,2,16,256]{3,2,1,0:T(8,128)S(1)} %collective-permute-done.9.refs_5_), channel_id=1, source_target_pairs={{0,1},{1,0},{2,3},{3,2},{4,5},{5,4},{6,7},{7,6},{8,9},{9,8},{10,11... | collective-permute-start | bytes 786440 | tf_op jit(solution)/shard_map/ppermute | solution.py:148

commit v5 on v0

--- a/solution.py
+++ b/solution.py
@@ -3,6 +3,8 @@
 import jax
 import jax.numpy as jnp
 from jax import lax
+from jax.experimental import pallas as pl
+from jax.experimental.pallas import tpu as pltpu
 from jax.sharding import PartitionSpec as P
 
 NO = 32
@@ -36,7 +38,7 @@
     return jnp.stack([sigma_real, sigma_imag])
 
 
-def shards(green, hamiltonian, interaction):
+def windowed(green, hamiltonian, interaction):
     tp_count = lax.axis_size("tp")
     ta_place = lax.axis_index("ta")
     tp_place = lax.axis_index("tp")
@@ -121,7 +123,279 @@
     return current.reshape(2, groups, 1, stripe, block_rows)
 
 
+def exchange_masks(ta_count, tp_count):
+    bits = [1 << bit for bit in reversed(range(1, tp_count.bit_length() - 1))]
+    first, middle, last = bits[:1], bits[1:-1], bits[-1:]
+    return first + last + [ta_count * tp_count // 2] + middle, first + middle + last
+
+
+def offsets_of(masks):
+    offsets = [0]
+    for mask in masks:
+        offsets = offsets + [known ^ mask for known in offsets]
+    return offsets
+
+
+def bf16_dot(left_side, right_side):
+    return lax.dot_general(
+        left_side, right_side, (((1,), (0,)), ((), ())), preferred_element_type=jnp.float32
+    )
+
+
+def halves(values):
+    high = values.astype(jnp.bfloat16)
+    return high, (values - high.astype(jnp.float32)).astype(jnp.bfloat16)
+
+
+def window_of(values, mirror, weights, first_time):
+    rows, width = values[0].shape
+    real_square = values[0] * values[0] - values[1] * values[1]
+    imag_square = 2.0 * values[0] * values[1]
+    real = real_square * mirror[0] - imag_square * mirror[1]
+    imag = real_square * mirror[1] + imag_square * mirror[0]
+    source_time = lax.broadcasted_iota(jnp.int32, (rows, width), 0) // NO
+    target_time = lax.broadcasted_iota(jnp.int32, (rows, width), 1) // NO + first_time
+    inside = source_time <= target_time
+
+    def weighted(part):
+        part = (part.reshape(rows // NO, NO, width) * weights[None]).reshape(rows, width)
+        return jnp.where(inside, part, 0.0).astype(jnp.bfloat16)
+
+    return weighted(real), weighted(imag)
+
+
+def mirrored(rounded):
+    return [jnp.transpose(part.astype(jnp.float32)) for part in rounded]
+
+
+def products(left_side, right_side):
+    real = bf16_dot(left_side[0], right_side[0]) - bf16_dot(left_side[1], right_side[1])
+    imag = bf16_dot(left_side[0], right_side[1]) + bf16_dot(left_side[1], right_side[0])
+    return real, imag
+
+
+def tables_of(hamiltonian, interaction, block_rows):
+    def repeated(tile):
+        return jnp.concatenate([tile] * (block_rows // NO), axis=1)
+
+    weights = repeated(jnp.transpose(interaction[...] * interaction[...]))
+    table = jnp.concatenate([repeated(jnp.transpose(hamiltonian[...]))] * (block_rows // NO))
+    same_time = (
+        lax.broadcasted_iota(jnp.int32, table.shape, 0) // NO
+        == lax.broadcasted_iota(jnp.int32, table.shape, 1) // NO
+    )
+    return weights, halves(jnp.where(same_time, table, 0.0))
+
+
+def one_body(values, high, low, table):
+    turned = [
+        bf16_dot(high[part], table[0])
+        + bf16_dot(low[part], table[0])
+        + bf16_dot(high[part], table[1])
+        for part in range(2)
+    ]
+    return values[0] + 0.5 * turned[1], values[1] - 0.5 * turned[0]
+
+
+def placed(tp_count, stripe, flip, mask):
+    me = lax.axis_index("ta") * tp_count + lax.axis_index("tp")
+    device = me ^ (flip ^ mask)
+    return device // tp_count, pl.multiple_of((device % tp_count) * stripe, stripe)
+
+
+def first_stage(masks, tp_count, stripe, block_rows, factor):
+    offsets = offsets_of(masks)
+    half_count = len(offsets) // 2
+
+    def kernel(*refs):
+        sources = refs[:4]
+        hamiltonian, interaction, values, lows, bases, window = refs[4:]
+        for flip in range(2):
+            for index, mask in enumerate(offsets):
+                late, slot = divmod(index, half_count)
+                block, row = placed(tp_count, stripe, flip, mask)
+                for part in range(2):
+                    values[part, block, pl.ds(row, stripe), :] = sources[2 * flip + late][
+                        slot, part
+                    ]
+        weights, table = tables_of(hamiltonian, interaction, block_rows)
+        for block in range(2):
+            current = [values[part, block] for part in range(2)]
+            split = [halves(part) for part in current]
+            high = [part[0] for part in split]
+            base = one_body(current, high, [part[1] for part in split], table)
+            for part in range(2):
+                lows[part, :, block * block_rows : (block + 1) * block_rows] = high[part]
+            if block == 0:
+                made = window_of(current, mirrored(high), weights, 0)
+                memory = products(high, made)
+                scale = 0.5 * factor
+                base = (base[0] + scale * memory[1], base[1] - scale * memory[0])
+                window[0] = made[0]
+                window[1] = made[1]
+            bases[0, block] = base[0]
+            bases[1, block] = base[1]
+
+    block = jax.ShapeDtypeStruct((2, 2, block_rows, block_rows), jnp.float32)
+    return pl.pallas_call(
+        kernel,
+        out_shape=[
+            block,
+            jax.ShapeDtypeStruct((2, block_rows, 2 * block_rows), jnp.bfloat16),
+            block,
+            jax.ShapeDtypeStruct((2, block_rows, block_rows), jnp.bfloat16),
+        ],
+        in_specs=[pl.BlockSpec(memory_space=pltpu.VMEM)] * 6,
+        out_specs=[pl.BlockSpec(memory_space=pltpu.VMEM)] * 4,
+        compiler_params=pltpu.CompilerParams(vmem_limit_bytes=16 << 20),
+        name="first_stage",
+    )
+
+
+def second_stage(masks, tp_count, stripe, block_rows, factor):
+    offsets = offsets_of(masks)
+    half_count = len(offsets) // 2
+    order_size = 2 * block_rows
+    scale = 0.5 * factor
+
+    def kernel(*refs):
+        sources = refs[:4]
+        hamiltonian, interaction, values, lows, bases, window = refs[4:10]
+        out, highs, rests, nexts, low_next = refs[10:]
+        ta_place = lax.axis_index("ta")
+        tp_place = lax.axis_index("tp")
+        for flip in range(2):
+            for index, mask in enumerate(offsets):
+                late, slot = divmod(index, half_count)
+                block, row = placed(tp_count, stripe, flip, mask)
+                source = sources[2 * flip + late]
+                for part in range(2):
+                    highs[part, block, pl.ds(row, stripe), :] = source[slot, 0, part]
+                    highs[part, 1 - block, pl.ds(row, stripe), :] = source[slot, 1, part]
+                    rests[part, block, pl.ds(row, stripe), :] = source[slot, 2, part]
+                    rests[part, 1 - block, pl.ds(row, stripe), :] = jnp.zeros(
+                        (stripe, block_rows), jnp.bfloat16
+                    )
+        weights, table = tables_of(hamiltonian, interaction, block_rows)
+        high = [[highs[part, block] for part in range(2)] for block in range(2)]
+        rest = [[rests[part, block] for part in range(2)] for block in range(2)]
+        full = [
+            [
+                high[block][part].astype(jnp.float32) + rest[block][part].astype(jnp.float32)
+                for part in range(2)
+            ]
+            for block in range(2)
+        ]
+        base = [one_body(full[block], high[block], rest[block], table) for block in range(2)]
+
+        def stored(block, group, real, imag):
+            for part, result in ((0, real), (1, imag)):
+                nexts[part, block, group] = result
+                low_next[part, group, :, block * block_rows : (block + 1) * block_rows] = (
+                    result.astype(jnp.bfloat16)
+                )
+
+        stored(0, 0, bases[0, 0], bases[1, 0])
+        memory = products(high[0], (window[0], window[1]))
+        stored(0, 1, base[0][0] + scale * memory[1], base[0][1] - scale * memory[0])
+        later = [
+            window_of(
+                [values[part, 1] for part in range(2)], mirrored(high[0]), weights, block_rows // NO
+            ),
+            window_of(full[1], mirrored(high[1]), weights, 0),
+        ]
+        rows = [[lows[part, :, :block_rows] for part in range(2)]]
+        rows.append([lows[part, :, block_rows:] for part in range(2)])
+        early_memory = [products(rows[0], later[0]), products(high[0], later[0])]
+        late_memory = [products(rows[1], later[1]), products(high[1], later[1])]
+        for group in range(2):
+            start = (bases[0, 1], bases[1, 1]) if group == 0 else base[1]
+            real = early_memory[group][0] + late_memory[group][0]
+            imag = early_memory[group][1] + late_memory[group][1]
+            stored(1, group, start[0] + scale * imag, start[1] - scale * real)
+
+        current = [nexts[part, ta_place].reshape(order_size, block_rows) for part in range(2)]
+        mirror = mirrored([low_next[part, ta_place] for part in range(2)])
+        last = window_of(current, mirror, weights, ta_place * (block_rows // NO))
+        row = pl.multiple_of(tp_place * stripe, stripe)
+        own = [
+            nexts[part, ta_place, :, pl.ds(row, stripe), :].reshape(2 * stripe, block_rows)
+            for part in range(2)
+        ]
+        own_rounded = [
+            low_next[part, :, pl.ds(row, stripe), :].reshape(2 * stripe, order_size)
+            for part in range(2)
+        ]
+        memory = products(own_rounded, last)
+        split = [halves(part) for part in own]
+        real, imag = one_body(own, [part[0] for part in split], [part[1] for part in split], table)
+        shape = (2, stripe, block_rows)
+        out[0] = (real + scale * memory[1]).reshape(shape)
+        out[1] = (imag - scale * memory[0]).reshape(shape)
+
+    square = (2, 2, block_rows, block_rows)
+    return pl.pallas_call(
+        kernel,
+        out_shape=jax.ShapeDtypeStruct((2, 2, stripe, block_rows), jnp.float32),
+        in_specs=[pl.BlockSpec(memory_space=pltpu.VMEM)] * 10,
+        out_specs=pl.BlockSpec(memory_space=pltpu.VMEM),
+        scratch_shapes=[
+            pltpu.VMEM(square, jnp.bfloat16),
+            pltpu.VMEM(square, jnp.bfloat16),
+            pltpu.VMEM((2,) + square, jnp.float32),
+            pltpu.VMEM((2, 2, block_rows, order_size), jnp.bfloat16),
+        ],
+        compiler_params=pltpu.CompilerParams(vmem_limit_bytes=24 << 20),
+        name="second_stage",
+    )
+
+
+def replicated(green, hamiltonian, interaction):
+    tp_count = lax.axis_size("tp")
+    count = 2 * tp_count
+    stripe = green.shape[3]
+    block_rows = green.shape[4]
+    factor = 1.0 / math.sqrt(2 * block_rows)
+    first_masks, second_masks = exchange_masks(2, tp_count)
+
+    def exchanged(block, mask):
+        return lax.ppermute(block, ("ta", "tp"), [(i, i ^ mask) for i in range(count)])
+
+    first = green[:, 0, 0]
+    second = green[:, 1, 0]
+    high = lax.reduce_precision(second, 8, 7)
+    low = (second - high).astype(jnp.bfloat16)
+    high = high.astype(jnp.bfloat16)
+    arriving = exchanged(first, first_masks[0])
+    other_high = exchanged(high, tp_count)
+    first = jnp.stack([first, arriving])
+    second = jnp.stack([high, other_high, low])[None]
+    for first_mask, second_mask in zip(first_masks[1:-1], second_masks[:-1]):
+        arriving = exchanged(first, first_mask)
+        second_arriving = exchanged(second, second_mask)
+        first = jnp.concatenate([first, arriving])
+        second = jnp.concatenate([second, second_arriving])
+    first_parts = [first, exchanged(first, first_masks[-1])]
+    second_parts = [second, exchanged(second, second_masks[-1])]
+    first_parts += [exchanged(part, 1) for part in first_parts]
+    second_parts += [exchanged(part, 1) for part in second_parts]
+    early = first_stage(first_masks, tp_count, stripe, block_rows, factor)
+    late = second_stage(second_masks, tp_count, stripe, block_rows, factor)
+    known = early(*first_parts, hamiltonian, interaction)
+    return late(*second_parts, hamiltonian, interaction, *known)[:, :, None]
+
+
 def solution(mesh):
     in_specs = (P(None, None, "tp", None, "ta"), P(), P())
     out_specs = P(None, None, "tp", None, "ta")
+    ta_count = mesh.shape["ta"]
+    tp_count = mesh.shape["tp"]
+
+    def shards(green, hamiltonian, interaction):
+        whole_bytes = green.size * green.dtype.itemsize * ta_count * tp_count
+        covered = ta_count == 2 and green.shape[1] == 2 and tp_count >= 8
+        if covered and tp_count & (tp_count - 1) == 0 and whole_bytes <= 1 << 22:
+            return replicated(green, hamiltonian, interaction)
+        return windowed(green, hamiltonian, interaction)
+
     return jax.shard_map(shards, mesh=mesh, in_specs=in_specs, out_specs=out_specs, check_vma=False)

time: 90.9 us -> 30.4 us (0.33)
  blocking collectives: 38.9 us -> 0 us
  waiting for transfers between devices: 16.3 us -> 8.24 us
  starting transfers between devices: 24 us -> 16.5 us
  local copies, waits for them, and re-layouts: 5.72 us -> 0.85 us
  Pallas kernels: 0 us -> 4.5 us
  other arithmetic: 2.58 us -> 0.08 us
  matrix products: 2.07 us -> 0 us
    all_gather x2 -> x0, blocking collectives: 38.9 us -> none  [shards(): portion = lax.all_gather(sending, 'tp', axis=2, tiled=True)]
    all_to_all x2 -> x0, waiting for transfers between devices: 11.7 us -> none  [shards(): lax.all_to_all(nearby, 'tp', split_axis=3, concat_axis=3, tiled=True)]
    all_to_all x2 -> x0, starting transfers between devices: 9.57 us -> none  [shards(): lax.all_to_all(nearby, 'tp', split_axis=3, concat_axis=3, tiled=True)]
    pallas_call x0 -> x2, Pallas kernels: none -> 4.5 us  [the longest x1 3.34 us: replicated(): return late(*second_parts, hamiltonian, interaction, *known)[:, :, None]]
    ppermute x8 -> x12, waiting for transfers between devices: 4.51 us -> 8.24 us  [exchanged(): lax.ppermute(block, ('ta', 'tp'), [(i, i ^ mask) for i in range(count)])]
    unnamed x11 -> x6, local copies, waits for them, and re-layouts: 2.65 us -> 0.02 us
    dot_general x11 -> x0, matrix products: 2.07 us -> none  [the longest x8 1.48 us: half_dot(): return jnp.dot(left_side, right_side, preferred_element_type=jnp.float32)]
    ppermute x8 -> x12, starting transfers between devices: 14.5 us -> 16.5 us  [exchanged(): lax.ppermute(block, ('ta', 'tp'), [(i, i ^ mask) for i in range(count)])]
  transfers between devices with their start and end apart: 10 -> 12, of which waited for: 4 -> 8; matrix products, arithmetic and copies ran while one was open for 6% -> 0% of each run, Pallas kernels for 0% -> 4%
where the time goes in v5:
time: 30.4 us; the launch traced here: 30.3 us
  starting transfers between devices  16.5 us (54%)
  waiting for transfers between devices  8.24 us (27%)
  Pallas kernels  4.5 us (15%)
  local copies, waits for them, and re-layouts  0.85 us (3%)
    ppermute x12, starting transfers between devices, exchanged(): lax.ppermute(block, ('ta', 'tp'), [(i, i ^ mask) for i in range(count)])  16.5 us
    ppermute x12, waiting for transfers between devices, exchanged(): lax.ppermute(block, ('ta', 'tp'), [(i, i ^ mask) for i in range(count)])  8.24 us
    pallas_call x1, Pallas kernels, replicated(): return late(*second_parts, hamiltonian, interaction, *known)[:, :, None]  3.34 us
    pallas_call x1, Pallas kernels, replicated(): known = early(*first_parts, hamiltonian, interaction)  1.16 us
    another operation x1, local copies, waits for them, and re-layouts, replicated(): first = jnp.stack([first, arriving])  0.83 us
  transfers between devices with their start and end apart: 12, of which 8 were waited for; matrix products, arithmetic and copies ran while one was open for 0% of the time, Pallas kernels for 4%

profile of v5, /device:TPU:0, one launch (start us, length us, event | category | flops | bytes accessed | tf_op | source)
XLA Modules:
  0.0 30.3 jit_solution(9060685365834285821)
XLA Ops:
  0.0 0.0 copy-start.2
  0.0 0.8 %slice_bitcast_fusion = (f32[1,2,16,256]{3,2,1,0:T(8,128)S(1)}, f32[2,16,256]{2,1,0:T(8,128)S(1)}) fusion(f32[2,2,1,16,256]{4,3,2,1,0:T(8,128)} %param.3), kind=kLoop, calls=%fused_computation.11 | loop fusion | bytes 98304 | tf_op jit(solution)/shard_map/stack;squeeze | solution.py:371
  0.8 4.1 %collective-permute-start.6 = (f32[2,16,256]{2,1,0:T(8,128)S(1)}, f32[2,16,256]{2,1,0:T(8,128)S(1)}, u32[]{:S(2)}, u32[]{:S(2)}) collective-permute-start(f32[2,16,256]{2,1,0:T(8,128)S(1)} %get-tuple-element.14), channel_id=1, source_target_pairs={{0,8},{1,9},{2,10},{3,11},{4,12},{5,13},{6,14},{7,15},{8,0},{9,1},... | collective-permute-start | bytes 98312 | tf_op jit(solution)/shard_map/ppermute | solution.py:362
  4.9 0.0 copy-done.2
  4.9 1.5 %collective-permute-start = (bf16[2,16,256]{2,1,0:T(8,128)(2,1)S(1)}, bf16[2,16,256]{2,1,0:T(8,128)(2,1)S(1)}, u32[]{:S(2)}, u32[]{:S(2)}) collective-permute-start(bf16[2,16,256]{2,1,0:T(8,128)(2,1)S(1)} %fusion.2), channel_id=1, source_target_pairs={{0,16},{1,17},{2,18},{3,19},{4,20},{5,21},{6,22},{7,23},{8,24},{9,... | collective-permute-start | bytes 49160 | tf_op jit(solution)/shard_map/ppermute | solution.py:362
  6.4 0.7 %collective-permute-done.6 = f32[2,16,256]{2,1,0:T(8,128)S(1)} collective-permute-done((f32[2,16,256]{2,1,0:T(8,128)S(1)}, f32[2,16,256]{2,1,0:T(8,128)S(1)}, u32[]{:S(2)}, u32[]{:S(2)}) %collective-permute-start.6) | collective-permute-done | bytes 32800 | tf_op jit(solution)/shard_map/ppermute | solution.py:362
  7.2 1.7 %collective-permute-start.7 = (f32[2,2,16,256]{3,2,1,0:T(8,128)S(1)}, f32[2,2,16,256]{3,2,1,0:T(8,128)S(1)}, u32[]{:S(2)}, u32[]{:S(2)}) collective-permute-start(f32[2,2,16,256]{3,2,1,0:T(8,128)S(1)} %pad_maximum_fusion.4), channel_id=1, source_target_pairs={{0,2},{1,3},{2,0},{3,1},{4,6},{5,7},{6,4},{7,5},{8,10},{9,11},{10,... | collective-permute-start | bytes 196616 | tf_op jit(solution)/shard_map/ppermute | solution.py:362
  8.9 0.0 collective-permute-done
  8.9 2.4 %collective-permute-start.1 = (bf16[1,3,2,16,256]{4,3,2,1,0:T(8,128)(2,1)S(1)}, bf16[1,3,2,16,256]{4,3,2,1,0:T(8,128)(2,1)S(1)}, u32[]{:S(2)}, u32[]{:S(2)}) collective-permute-start(bf16[1,3,2,16,256]{4,3,2,1,0:T(8,128)(2,1)S(1)} %maximum_bitcast_fusion), channel_id=1, source_target_pairs={{0,8},{1,9},{2,10},{3,11},{4,12},{5,13},{6,14},{7,15},{8,0},{9,1},... | collective-permute-start | bytes 147464 | tf_op jit(solution)/shard_map/ppermute | solution.py:362
  11.3 0.1 collective-permute-done.7
  11.4 1.8 %collective-permute-start.8 = (f32[4,2,16,256]{3,2,1,0:T(8,128)S(1)}, f32[4,2,16,256]{3,2,1,0:T(8,128)S(1)}, u32[]{:S(2)}, u32[]{:S(2)}) collective-permute-start(f32[4,2,16,256]{3,2,1,0:T(8,128)S(1)} %pad_maximum_fusion.2), channel_id=1, source_target_pairs={{0,16},{1,17},{2,18},{3,19},{4,20},{5,21},{6,22},{7,23},{8,24},{9,... | collective-permute-start | bytes 393224 | tf_op jit(solution)/shard_map/ppermute | solution.py:362
  13.2 0.8 %collective-permute-done.1 = bf16[1,3,2,16,256]{4,3,2,1,0:T(8,128)(2,1)S(1)} collective-permute-done((bf16[1,3,2,16,256]{4,3,2,1,0:T(8,128)(2,1)S(1)}, bf16[1,3,2,16,256]{4,3,2,1,0:T(8,128)(2,1)S(1)}, u32[]{:S(2)}, u32[]{:S(2)}) %collective-permute-start.1) | collective-permute-done | bytes 49184 | tf_op jit(solution)/shard_map/ppermute | solution.py:362
  14.0 1.4 %collective-permute-start.2 = (bf16[2,3,2,16,256]{4,3,2,1,0:T(8,128)(2,1)S(1)}, bf16[2,3,2,16,256]{4,3,2,1,0:T(8,128)(2,1)S(1)}, u32[]{:S(2)}, u32[]{:S(2)}) collective-permute-start(bf16[2,3,2,16,256]{4,3,2,1,0:T(8,128)(2,1)S(1)} %pad_maximum_fusion.3), channel_id=1, source_target_pairs={{0,4},{1,5},{2,6},{3,7},{4,0},{5,1},{6,2},{7,3},{8,12},{9,13},{10,... | collective-permute-start | bytes 294920 | tf_op jit(solution)/shard_map/ppermute | solution.py:362
  15.4 1.1 %collective-permute-done.8 = f32[4,2,16,256]{3,2,1,0:T(8,128)S(1)} collective-permute-done((f32[4,2,16,256]{3,2,1,0:T(8,128)S(1)}, f32[4,2,16,256]{3,2,1,0:T(8,128)S(1)}, u32[]{:S(2)}, u32[]{:S(2)}) %collective-permute-start.8) | collective-permute-done | bytes 131104 | tf_op jit(solution)/shard_map/ppermute | solution.py:362
  16.5 0.0 copy-start
  16.5 0.0 copy-start.1
  16.5 1.8 %collective-permute-start.9 = (f32[8,2,16,256]{3,2,1,0:T(8,128)S(1)}, f32[8,2,16,256]{3,2,1,0:T(8,128)S(1)}, u32[]{:S(2)}, u32[]{:S(2)}) collective-permute-start(f32[8,2,16,256]{3,2,1,0:T(8,128)S(1)} %pad_maximum_fusion.refs_0_), channel_id=1, source_target_pairs={{0,4},{1,5},{2,6},{3,7},{4,0},{5,1},{6,2},{7,3},{8,12},{9,13},{10,... | collective-permute-start | bytes 786440 | tf_op jit(solution)/shard_map/ppermute | solution.py:362
  18.3 1.4 %collective-permute-done.2 = bf16[2,3,2,16,256]{4,3,2,1,0:T(8,128)(2,1)S(1)} collective-permute-done((bf16[2,3,2,16,256]{4,3,2,1,0:T(8,128)(2,1)S(1)}, bf16[2,3,2,16,256]{4,3,2,1,0:T(8,128)(2,1)S(1)}, u32[]{:S(2)}, u32[]{:S(2)}) %collective-permute-start.2) | collective-permute-done | bytes 98336 | tf_op jit(solution)/shard_map/ppermute | solution.py:362
  19.7 1.3 %collective-permute-start.3 = (bf16[4,3,2,16,256]{4,3,2,1,0:T(8,128)(2,1)S(1)}, bf16[4,3,2,16,256]{4,3,2,1,0:T(8,128)(2,1)S(1)}, u32[]{:S(2)}, u32[]{:S(2)}) collective-permute-start(bf16[4,3,2,16,256]{4,3,2,1,0:T(8,128)(2,1)S(1)} %pad_maximum_fusion.1.refs_0_), channel_id=1, source_target_pairs={{0,2},{1,3},{2,0},{3,1},{4,6},{5,7},{6,4},{7,5},{8,10},{9,11},{10,... | collective-permute-start | bytes 589832 | tf_op jit(solution)/shard_map/ppermute | solution.py:362
  21.0 0.0 collective-permute-start.10
  21.0 2.0 %collective-permute-done.9.refs_1_ = f32[8,2,16,256]{3,2,1,0:T(8,128)S(1)} collective-permute-done((f32[8,2,16,256]{3,2,1,0:T(8,128)S(1)}, f32[8,2,16,256]{3,2,1,0:T(8,128)S(1)}, u32[]{:S(2)}, u32[]{:S(2)}) %collective-permute-start.9) | collective-permute-done | bytes 262176 | tf_op jit(solution)/shard_map/ppermute | solution.py:362
  23.1 0.0 collective-permute-start.11
  23.1 0.5 %collective-permute-start.4 = (bf16[4,3,2,16,256]{4,3,2,1,0:T(8,128)(2,1)S(1)}, bf16[4,3,2,16,256]{4,3,2,1,0:T(8,128)(2,1)S(1)}, u32[]{:S(2)}, u32[]{:S(2)}) collective-permute-start(bf16[4,3,2,16,256]{4,3,2,1,0:T(8,128)(2,1)S(1)} %pad_maximum_fusion.1.refs_0_), channel_id=1, source_target_pairs={{0,1},{1,0},{2,3},{3,2},{4,5},{5,4},{6,7},{7,6},{8,9},{9,8},{10,11... | collective-permute-start | bytes 589832 | tf_op jit(solution)/shard_map/ppermute | solution.py:362
  23.6 1.9 %collective-permute-done.3.refs_1_ = bf16[4,3,2,16,256]{4,3,2,1,0:T(8,128)(2,1)S(1)} collective-permute-done((bf16[4,3,2,16,256]{4,3,2,1,0:T(8,128)(2,1)S(1)}, bf16[4,3,2,16,256]{4,3,2,1,0:T(8,128)(2,1)S(1)}, u32[]{:S(2)}, u32[]{:S(2)}) %collective-permute-start.3) | collective-permute-done | bytes 196640 | tf_op jit(solution)/shard_map/ppermute | solution.py:362
  25.5 0.0 collective-permute-start.5
  25.5 0.0 collective-permute-done.10.refs_2_
  25.5 0.0 collective-permute-done.11.refs_3_
  25.5 0.0 copy-done
  25.5 0.0 copy-done.1
  25.5 1.2 %first_stage.1 = (f32[2,2,256,256]{3,2,1,0:T(8,128)S(1)}, bf16[2,256,512]{2,1,0:T(8,128)(2,1)S(1)}, f32[2,2,256,256]{3,2,1,0:T(8,128)S(1)}, bf16[2,256,256]{2,1,0:T(8,128)(2,1)S(1)}) custom-call(f32[8,2,16,256]{3,2,1,0:T(8,128)S(1)} %pad_maximum_fusion.refs_0_, f32[8,2,16,256]{3,2,1,0:T(8,128)S(1)} %collective-permute-done.9.refs_1_, ...), custom_call_target="tpu_custom_call" | custom-call | tf_op jit(solution)/shard_map/first_stage/pallas_call | solution.py:384
  26.7 0.0 collective-permute-done.4.refs_2_
  26.7 0.2 collective-permute-done.5.refs_3_
  26.9 3.3 %second_stage.1 = f32[2,2,16,256]{3,2,1,0:T(8,128)} custom-call(bf16[4,3,2,16,256]{4,3,2,1,0:T(8,128)(2,1)S(1)} %pad_maximum_fusion.1.refs_0_, bf16[4,3,2,16,256]{4,3,2,1,0:T(8,128)(2,1)S(1)} %collective-permute-done.3.refs_1_, bf16[4,3,2,16,256]{4,3,2,1,0:T(8,128)(2,1)S(1)} %collective-permute-done.4.refs_2_, ...), custom_call_target="tpu_custom_call" | custom-call | tf_op jit(solution)/shard_map/second_stage/pallas_call | solution.py:385
  (8 shorter events, 0.1 us)
Async XLA Ops:
  0.0 4.9 %copy-start.2 = (f32[2,2,1,16,256]{4,3,2,1,0:T(8,128)S(1)}, f32[2,2,1,16,256]{4,3,2,1,0:T(8,128)}, u32[]{:S(2)}) copy-start(f32[2,2,1,16,256]{4,3,2,1,0:T(8,128)} %param.3) | copy-start | bytes 196612
  0.8 6.3 %collective-permute-start.6 = (f32[2,16,256]{2,1,0:T(8,128)S(1)}, f32[2,16,256]{2,1,0:T(8,128)S(1)}, u32[]{:S(2)}, u32[]{:S(2)}) collective-permute-start(f32[2,16,256]{2,1,0:T(8,128)S(1)} %get-tuple-element.14), channel_id=1, source_target_pairs={{0,8},{1,9},{2,10},{3,11},{4,12},{5,13},{6,14},{7,15},{8,0},{9,1},... | collective-permute-start | bytes 98312 | tf_op jit(solution)/shard_map/ppermute | solution.py:362
  4.9 4.0 %collective-permute-start = (bf16[2,16,256]{2,1,0:T(8,128)(2,1)S(1)}, bf16[2,16,256]{2,1,0:T(8,128)(2,1)S(1)}, u32[]{:S(2)}, u32[]{:S(2)}) collective-permute-start(bf16[2,16,256]{2,1,0:T(8,128)(2,1)S(1)} %fusion.2), channel_id=1, source_target_pairs={{0,16},{1,17},{2,18},{3,19},{4,20},{5,21},{6,22},{7,23},{8,24},{9,... | collective-permute-start | bytes 49160 | tf_op jit(solution)/shard_map/ppermute | solution.py:362
  7.2 4.3 %collective-permute-start.7 = (f32[2,2,16,256]{3,2,1,0:T(8,128)S(1)}, f32[2,2,16,256]{3,2,1,0:T(8,128)S(1)}, u32[]{:S(2)}, u32[]{:S(2)}) collective-permute-start(f32[2,2,16,256]{3,2,1,0:T(8,128)S(1)} %pad_maximum_fusion.4), channel_id=1, source_target_pairs={{0,2},{1,3},{2,0},{3,1},{4,6},{5,7},{6,4},{7,5},{8,10},{9,11},{10,... | collective-permute-start | bytes 196616 | tf_op jit(solution)/shard_map/ppermute | solution.py:362
  8.9 5.1 %collective-permute-start.1 = (bf16[1,3,2,16,256]{4,3,2,1,0:T(8,128)(2,1)S(1)}, bf16[1,3,2,16,256]{4,3,2,1,0:T(8,128)(2,1)S(1)}, u32[]{:S(2)}, u32[]{:S(2)}) collective-permute-start(bf16[1,3,2,16,256]{4,3,2,1,0:T(8,128)(2,1)S(1)} %maximum_bitcast_fusion), channel_id=1, source_target_pairs={{0,8},{1,9},{2,10},{3,11},{4,12},{5,13},{6,14},{7,15},{8,0},{9,1},... | collective-permute-start | bytes 147464 | tf_op jit(solution)/shard_map/ppermute | solution.py:362
  11.4 5.0 %collective-permute-start.8 = (f32[4,2,16,256]{3,2,1,0:T(8,128)S(1)}, f32[4,2,16,256]{3,2,1,0:T(8,128)S(1)}, u32[]{:S(2)}, u32[]{:S(2)}) collective-permute-start(f32[4,2,16,256]{3,2,1,0:T(8,128)S(1)} %pad_maximum_fusion.2), channel_id=1, source_target_pairs={{0,16},{1,17},{2,18},{3,19},{4,20},{5,21},{6,22},{7,23},{8,24},{9,... | collective-permute-start | bytes 393224 | tf_op jit(solution)/shard_map/ppermute | solution.py:362
  14.0 5.7 %collective-permute-start.2 = (bf16[2,3,2,16,256]{4,3,2,1,0:T(8,128)(2,1)S(1)}, bf16[2,3,2,16,256]{4,3,2,1,0:T(8,128)(2,1)S(1)}, u32[]{:S(2)}, u32[]{:S(2)}) collective-permute-start(bf16[2,3,2,16,256]{4,3,2,1,0:T(8,128)(2,1)S(1)} %pad_maximum_fusion.3), channel_id=1, source_target_pairs={{0,4},{1,5},{2,6},{3,7},{4,0},{5,1},{6,2},{7,3},{8,12},{9,13},{10,... | collective-permute-start | bytes 294920 | tf_op jit(solution)/shard_map/ppermute | solution.py:362
  16.5 9.0 %copy-start = (f32[32,32]{1,0:T(8,128)S(1)}, f32[32,32]{1,0:T(8,128)}, u32[]{:S(2)}) copy-start(f32[32,32]{1,0:T(8,128)} %refs_4_.3) | copy-start | bytes 12292
  16.5 9.0 %copy-start.1 = (f32[32,32]{1,0:T(8,128)S(1)}, f32[32,32]{1,0:T(8,128)}, u32[]{:S(2)}) copy-start(f32[32,32]{1,0:T(8,128)} %refs_5_.3) | copy-start | bytes 12292
  16.5 6.5 %collective-permute-start.9 = (f32[8,2,16,256]{3,2,1,0:T(8,128)S(1)}, f32[8,2,16,256]{3,2,1,0:T(8,128)S(1)}, u32[]{:S(2)}, u32[]{:S(2)}) collective-permute-start(f32[8,2,16,256]{3,2,1,0:T(8,128)S(1)} %pad_maximum_fusion.refs_0_), channel_id=1, source_target_pairs={{0,4},{1,5},{2,6},{3,7},{4,0},{5,1},{6,2},{7,3},{8,12},{9,13},{10,... | collective-permute-start | bytes 786440 | tf_op jit(solution)/shard_map/ppermute | solution.py:362
  19.7 5.7 %collective-permute-start.3 = (bf16[4,3,2,16,256]{4,3,2,1,0:T(8,128)(2,1)S(1)}, bf16[4,3,2,16,256]{4,3,2,1,0:T(8,128)(2,1)S(1)}, u32[]{:S(2)}, u32[]{:S(2)}) collective-permute-start(bf16[4,3,2,16,256]{4,3,2,1,0:T(8,128)(2,1)S(1)} %pad_maximum_fusion.1.refs_0_), channel_id=1, source_target_pairs={{0,2},{1,3},{2,0},{3,1},{4,6},{5,7},{6,4},{7,5},{8,10},{9,11},{10,... | collective-permute-start | bytes 589832 | tf_op jit(solution)/shard_map/ppermute | solution.py:362
  21.0 4.5 %collective-permute-start.10 = (f32[8,2,16,256]{3,2,1,0:T(8,128)S(1)}, f32[8,2,16,256]{3,2,1,0:T(8,128)S(1)}, u32[]{:S(2)}, u32[]{:S(2)}) collective-permute-start(f32[8,2,16,256]{3,2,1,0:T(8,128)S(1)} %pad_maximum_fusion.refs_0_), channel_id=1, source_target_pairs={{0,1},{1,0},{2,3},{3,2},{4,5},{5,4},{6,7},{7,6},{8,9},{9,8},{10,11... | collective-permute-start | bytes 786440 | tf_op jit(solution)/shard_map/ppermute | solution.py:362
  23.1 2.4 %collective-permute-start.11 = (f32[8,2,16,256]{3,2,1,0:T(8,128)S(1)}, f32[8,2,16,256]{3,2,1,0:T(8,128)S(1)}, u32[]{:S(2)}, u32[]{:S(2)}) collective-permute-start(f32[8,2,16,256]{3,2,1,0:T(8,128)S(1)} %collective-permute-done.9.refs_1_), channel_id=1, source_target_pairs={{0,1},{1,0},{2,3},{3,2},{4,5},{5,4},{6,7},{7,6},{8,9},{9,8},{10,11... | collective-permute-start | bytes 786440 | tf_op jit(solution)/shard_map/ppermute | solution.py:362
  23.1 3.6 %collective-permute-start.4 = (bf16[4,3,2,16,256]{4,3,2,1,0:T(8,128)(2,1)S(1)}, bf16[4,3,2,16,256]{4,3,2,1,0:T(8,128)(2,1)S(1)}, u32[]{:S(2)}, u32[]{:S(2)}) collective-permute-start(bf16[4,3,2,16,256]{4,3,2,1,0:T(8,128)(2,1)S(1)} %pad_maximum_fusion.1.refs_0_), channel_id=1, source_target_pairs={{0,1},{1,0},{2,3},{3,2},{4,5},{5,4},{6,7},{7,6},{8,9},{9,8},{10,11... | collective-permute-start | bytes 589832 | tf_op jit(solution)/shard_map/ppermute | solution.py:362
  25.5 1.4 %collective-permute-start.5 = (bf16[4,3,2,16,256]{4,3,2,1,0:T(8,128)(2,1)S(1)}, bf16[4,3,2,16,256]{4,3,2,1,0:T(8,128)(2,1)S(1)}, u32[]{:S(2)}, u32[]{:S(2)}) collective-permute-start(bf16[4,3,2,16,256]{4,3,2,1,0:T(8,128)(2,1)S(1)} %collective-permute-done.3.refs_1_), channel_id=1, source_target_pairs={{0,1},{1,0},{2,3},{3,2},{4,5},{5,4},{6,7},{7,6},{8,9},{9,8},{10,11... | collective-permute-start | bytes 589832 | tf_op jit(solution)/shard_map/ppermute | solution.py:362

commit v6 on v5

--- a/solution.py
+++ b/solution.py
@@ -125,8 +125,9 @@
 
 def exchange_masks(ta_count, tp_count):
     bits = [1 << bit for bit in reversed(range(1, tp_count.bit_length() - 1))]
-    first, middle, last = bits[:1], bits[1:-1], bits[-1:]
-    return first + last + [ta_count * tp_count // 2] + middle, first + middle + last
+    first, middle, last = bits[0], bits[1:-1], bits[-1:]
+    ta_bit = [ta_count * tp_count // 2]
+    return first, middle + last + ta_bit, last + ta_bit + middle
 
 
 def offsets_of(masks):
@@ -197,12 +198,6 @@
     return values[0] + 0.5 * turned[1], values[1] - 0.5 * turned[0]
 
 
-def placed(tp_count, stripe, flip, mask):
-    me = lax.axis_index("ta") * tp_count + lax.axis_index("tp")
-    device = me ^ (flip ^ mask)
-    return device // tp_count, pl.multiple_of((device % tp_count) * stripe, stripe)
-
-
 def first_stage(masks, tp_count, stripe, block_rows, factor):
     offsets = offsets_of(masks)
     half_count = len(offsets) // 2
@@ -210,17 +205,21 @@
     def kernel(*refs):
         sources = refs[:4]
         hamiltonian, interaction, values, lows, bases, window = refs[4:]
+        me = lax.axis_index("ta") * tp_count + lax.axis_index("tp")
         for flip in range(2):
             for index, mask in enumerate(offsets):
                 late, slot = divmod(index, half_count)
-                block, row = placed(tp_count, stripe, flip, mask)
+                device = me ^ (flip ^ mask)
                 for part in range(2):
-                    values[part, block, pl.ds(row, stripe), :] = sources[2 * flip + late][
-                        slot, part
-                    ]
+                    values[part, device] = sources[2 * flip + late][slot, part]
         weights, table = tables_of(hamiltonian, interaction, block_rows)
         for block in range(2):
-            current = [values[part, block] for part in range(2)]
+            current = [
+                values[part, block * tp_count : (block + 1) * tp_count].reshape(
+                    block_rows, block_rows
+                )
+                for part in range(2)
+            ]
             split = [halves(part) for part in current]
             high = [part[0] for part in split]
             base = one_body(current, high, [part[1] for part in split], table)
@@ -240,7 +239,7 @@
     return pl.pallas_call(
         kernel,
         out_shape=[
-            block,
+            jax.ShapeDtypeStruct((2, 2 * tp_count, stripe, block_rows), jnp.float32),
             jax.ShapeDtypeStruct((2, block_rows, 2 * block_rows), jnp.bfloat16),
             block,
             jax.ShapeDtypeStruct((2, block_rows, block_rows), jnp.bfloat16),
@@ -264,21 +263,31 @@
         out, highs, rests, nexts, low_next = refs[10:]
         ta_place = lax.axis_index("ta")
         tp_place = lax.axis_index("tp")
+        me = ta_place * tp_count + tp_place
+        blank = jnp.zeros((stripe, block_rows), jnp.bfloat16)
         for flip in range(2):
             for index, mask in enumerate(offsets):
                 late, slot = divmod(index, half_count)
-                block, row = placed(tp_count, stripe, flip, mask)
+                device = me ^ (flip ^ mask)
+                other = device ^ tp_count
                 source = sources[2 * flip + late]
                 for part in range(2):
-                    highs[part, block, pl.ds(row, stripe), :] = source[slot, 0, part]
-                    highs[part, 1 - block, pl.ds(row, stripe), :] = source[slot, 1, part]
-                    rests[part, block, pl.ds(row, stripe), :] = source[slot, 2, part]
-                    rests[part, 1 - block, pl.ds(row, stripe), :] = jnp.zeros(
-                        (stripe, block_rows), jnp.bfloat16
-                    )
+                    highs[part, device] = source[slot, 0, part]
+                    highs[part, other] = source[slot, 1, part]
+                    rests[part, device] = source[slot, 2, part]
+                    rests[part, other] = blank
         weights, table = tables_of(hamiltonian, interaction, block_rows)
-        high = [[highs[part, block] for part in range(2)] for block in range(2)]
-        rest = [[rests[part, block] for part in range(2)] for block in range(2)]
+
+        def whole(source, block):
+            return [
+                source[part, block * tp_count : (block + 1) * tp_count].reshape(
+                    block_rows, block_rows
+                )
+                for part in range(2)
+            ]
+
+        high = [whole(highs, block) for block in range(2)]
+        rest = [whole(rests, block) for block in range(2)]
         full = [
             [
                 high[block][part].astype(jnp.float32) + rest[block][part].astype(jnp.float32)
@@ -299,9 +308,7 @@
         memory = products(high[0], (window[0], window[1]))
         stored(0, 1, base[0][0] + scale * memory[1], base[0][1] - scale * memory[0])
         later = [
-            window_of(
-                [values[part, 1] for part in range(2)], mirrored(high[0]), weights, block_rows // NO
-            ),
+            window_of(whole(values, 1), mirrored(high[0]), weights, block_rows // NO),
             window_of(full[1], mirrored(high[1]), weights, 0),
         ]
         rows = [[lows[part, :, :block_rows] for part in range(2)]]
@@ -340,8 +347,8 @@
         in_specs=[pl.BlockSpec(memory_space=pltpu.VMEM)] * 10,
         out_specs=pl.BlockSpec(memory_space=pltpu.VMEM),
         scratch_shapes=[
-            pltpu.VMEM(square, jnp.bfloat16),
-            pltpu.VMEM(square, jnp.bfloat16),
+            pltpu.VMEM((2, 2 * tp_count, stripe, block_rows), jnp.bfloat16),
+            pltpu.VMEM((2, 2 * tp_count, stripe, block_rows), jnp.bfloat16),
             pltpu.VMEM((2,) + square, jnp.float32),
             pltpu.VMEM((2, 2, block_rows, order_size), jnp.bfloat16),
         ],
@@ -356,29 +363,30 @@
     stripe = green.shape[3]
     block_rows = green.shape[4]
     factor = 1.0 / math.sqrt(2 * block_rows)
-    first_masks, second_masks = exchange_masks(2, tp_count)
+    mask, first_masks, second_masks = exchange_masks(2, tp_count)
 
     def exchanged(block, mask):
         return lax.ppermute(block, ("ta", "tp"), [(i, i ^ mask) for i in range(count)])
 
-    first = green[:, 0, 0]
-    second = green[:, 1, 0]
+    arriving = exchanged(green.reshape(-1, block_rows), mask).reshape(green.shape)
+    first = jnp.stack([green[:, 0, 0], arriving[:, 0, 0]])
+    second = jnp.stack([green[:, 1, 0], arriving[:, 1, 0]])
     high = lax.reduce_precision(second, 8, 7)
-    low = (second - high).astype(jnp.bfloat16)
-    high = high.astype(jnp.bfloat16)
-    arriving = exchanged(first, first_masks[0])
-    other_high = exchanged(high, tp_count)
-    first = jnp.stack([first, arriving])
-    second = jnp.stack([high, other_high, low])[None]
-    for first_mask, second_mask in zip(first_masks[1:-1], second_masks[:-1]):
-        arriving = exchanged(first, first_mask)
-        second_arriving = exchanged(second, second_mask)
-        first = jnp.concatenate([first, arriving])
-        second = jnp.concatenate([second, second_arriving])
-    first_parts = [first, exchanged(first, first_masks[-1])]
-    second_parts = [second, exchanged(second, second_masks[-1])]
+    second = jnp.stack([high, second - high], 1).astype(jnp.bfloat16)
+    first_parts = second_parts = ()
+    for first_mask, second_mask in zip(first_masks, second_masks):
+        first_parts = [first, exchanged(first, first_mask)]
+        first = jnp.concatenate(first_parts)
+        if second_mask == tp_count:
+            other_high = exchanged(second[:, 0], second_mask)[:, None]
+            second = jnp.concatenate([second[:, :1], other_high, second[:, 1:]], 1)
+        else:
+            second_parts = [second, exchanged(second, second_mask)]
+            second = jnp.concatenate(second_parts)
     first_parts += [exchanged(part, 1) for part in first_parts]
     second_parts += [exchanged(part, 1) for part in second_parts]
+    first_masks = [mask] + first_masks
+    second_masks = [mask] + [later for later in second_masks if later != tp_count]
     early = first_stage(first_masks, tp_count, stripe, block_rows, factor)
     late = second_stage(second_masks, tp_count, stripe, block_rows, factor)
     known = early(*first_parts, hamiltonian, interaction)
@@ -393,7 +401,7 @@
 
     def shards(green, hamiltonian, interaction):
         whole_bytes = green.size * green.dtype.itemsize * ta_count * tp_count
-        covered = ta_count == 2 and green.shape[1] == 2 and tp_count >= 8
+        covered = ta_count == 2 and green.shape[1] == 2 and tp_count >= 16
         if covered and tp_count & (tp_count - 1) == 0 and whole_bytes <= 1 << 22:
             return replicated(green, hamiltonian, interaction)
         return windowed(green, hamiltonian, interaction)

time: 30.4 us -> 29.9 us (0.984)
  starting transfers between devices: 16.5 us -> 12.8 us
  waiting for transfers between devices: 8.24 us -> 11.6 us
    ppermute x12 -> x11, starting transfers between devices: 16.5 us -> 12.8 us  [exchanged(): lax.ppermute(block, ('ta', 'tp'), [(i, i ^ mask) for i in range(count)])]
    ppermute x12 -> x11, waiting for transfers between devices: 8.24 us -> 11.6 us  [exchanged(): lax.ppermute(block, ('ta', 'tp'), [(i, i ^ mask) for i in range(count)])]
    another operation x1 -> x2, local copies, waits for them, and re-layouts: 0.83 us -> 0.8 us  [replicated(): first = jnp.stack([green[:, 0, 0], arriving[:, 0, 0]])]
  transfers between devices with their start and end apart: 12 -> 11, of which waited for: 8 -> 6; matrix products, arithmetic and copies ran while one was open for 0% -> 3% of each run, Pallas kernels for 4% -> 3%
where the time goes in v6:
time: 29.9 us; the launch traced here: 29.7 us
  starting transfers between devices  12.8 us (43%)
  waiting for transfers between devices  11.6 us (39%)
  Pallas kernels  4.33 us (14%)
  local copies, waits for them, and re-layouts  0.83 us (3%)
    ppermute x11, starting transfers between devices, exchanged(): lax.ppermute(block, ('ta', 'tp'), [(i, i ^ mask) for i in range(count)])  12.8 us
    ppermute x11, waiting for transfers between devices, exchanged(): lax.ppermute(block, ('ta', 'tp'), [(i, i ^ mask) for i in range(count)])  11.6 us
    pallas_call x1, Pallas kernels, replicated(): return late(*second_parts, hamiltonian, interaction, *known)[:, :, None]  3.31 us
    pallas_call x1, Pallas kernels, replicated(): known = early(*first_parts, hamiltonian, interaction)  1.03 us
    another operation x2, local copies, waits for them, and re-layouts, replicated(): first = jnp.stack([green[:, 0, 0], arriving[:, 0, 0]])  0.8 us
  transfers between devices with their start and end apart: 11, of which 6 were waited for; matrix products, arithmetic and copies ran while one was open for 3% of the time, Pallas kernels for 3%

profile of v6, /device:TPU:0, one launch (start us, length us, event | category | flops | bytes accessed | tf_op | source)
XLA Modules:
  0.0 29.7 jit_solution(7314141011109162979)
XLA Ops:
  0.0 4.1 %collective-permute-start = (f32[64,256]{1,0:T(8,128)}, f32[64,256]{1,0:T(8,128)S(1)}, u32[]{:S(2)}, u32[]{:S(2)}) collective-permute-start(f32[64,256]{1,0:T(8,128)} %bitcast.26), channel_id=1, source_target_pairs={{0,8},{1,9},{2,10},{3,11},{4,12},{5,13},{6,14},{7,15},{8,0},{9,1},... | collective-permute-start | bytes 196616 | tf_op jit(solution)/shard_map/ppermute | solution.py:369
  4.1 0.8 %slice_bitcast_fusion.2 = (f32[1,2,16,256]{3,2,1,0:T(8,128)S(1)}, f32[1,1,2,16,256]{4,3,2,1,0:T(8,128)S(1)}) fusion(f32[2,2,1,16,256]{4,3,2,1,0:T(8,128)} %param.3), kind=kLoop, calls=%fused_computation.12 | loop fusion | bytes 131072 | tf_op jit(solution)/shard_map/stack;squeeze | solution.py:372
  4.9 3.1 %collective-permute-done = f32[64,256]{1,0:T(8,128)S(1)} collective-permute-done((f32[64,256]{1,0:T(8,128)}, f32[64,256]{1,0:T(8,128)S(1)}, u32[]{:S(2)}, u32[]{:S(2)}) %collective-permute-start) | collective-permute-done | bytes 65568 | tf_op jit(solution)/shard_map/ppermute | solution.py:369
  7.9 0.7 %collective-permute-start.6 = (f32[2,2,16,256]{3,2,1,0:T(8,128)S(1)}, f32[2,2,16,256]{3,2,1,0:T(8,128)S(1)}, u32[]{:S(2)}, u32[]{:S(2)}) collective-permute-start(f32[2,2,16,256]{3,2,1,0:T(8,128)S(1)} %pad_maximum_fusion.6), channel_id=1, source_target_pairs={{0,4},{1,5},{2,6},{3,7},{4,0},{5,1},{6,2},{7,3},{8,12},{9,13},{10,... | collective-permute-start | bytes 196616 | tf_op jit(solution)/shard_map/ppermute | solution.py:369
  8.7 1.6 %collective-permute-start.1 = (bf16[2,2,2,16,256]{4,3,2,1,0:T(8,128)(2,1)S(1)}, bf16[2,2,2,16,256]{4,3,2,1,0:T(8,128)(2,1)S(1)}, u32[]{:S(2)}, u32[]{:S(2)}) collective-permute-start(bf16[2,2,2,16,256]{4,3,2,1,0:T(8,128)(2,1)S(1)} %pad_maximum_fusion.5), channel_id=1, source_target_pairs={{0,2},{1,3},{2,0},{3,1},{4,6},{5,7},{6,4},{7,5},{8,10},{9,11},{10,... | collective-permute-start | bytes 196616 | tf_op jit(solution)/shard_map/ppermute | solution.py:369
  10.3 2.0 %collective-permute-done.6 = f32[2,2,16,256]{3,2,1,0:T(8,128)S(1)} collective-permute-done((f32[2,2,16,256]{3,2,1,0:T(8,128)S(1)}, f32[2,2,16,256]{3,2,1,0:T(8,128)S(1)}, u32[]{:S(2)}, u32[]{:S(2)}) %collective-permute-start.6) | collective-permute-done | bytes 65568 | tf_op jit(solution)/shard_map/ppermute | solution.py:369
  12.3 1.8 %collective-permute-start.7 = (f32[4,2,16,256]{3,2,1,0:T(8,128)S(1)}, f32[4,2,16,256]{3,2,1,0:T(8,128)S(1)}, u32[]{:S(2)}, u32[]{:S(2)}) collective-permute-start(f32[4,2,16,256]{3,2,1,0:T(8,128)S(1)} %pad_maximum_fusion.3), channel_id=1, source_target_pairs={{0,2},{1,3},{2,0},{3,1},{4,6},{5,7},{6,4},{7,5},{8,10},{9,11},{10,... | collective-permute-start | bytes 393224 | tf_op jit(solution)/shard_map/ppermute | solution.py:369
  14.1 0.0 collective-permute-done.1
  14.1 1.6 %collective-permute-start.2 = (bf16[4,2,16,256]{3,2,1,0:T(8,128)(2,1)S(1)}, bf16[4,2,16,256]{3,2,1,0:T(8,128)(2,1)S(1)}, u32[]{:S(2)}, u32[]{:S(2)}) collective-permute-start(bf16[4,2,16,256]{3,2,1,0:T(8,128)(2,1)S(1)} %get-tuple-element.14), channel_id=1, source_target_pairs={{0,16},{1,17},{2,18},{3,19},{4,20},{5,21},{6,22},{7,23},{8,24},{9,... | collective-permute-start | bytes 196616 | tf_op jit(solution)/shard_map/ppermute | solution.py:369
  15.7 1.6 %collective-permute-done.7 = f32[4,2,16,256]{3,2,1,0:T(8,128)S(1)} collective-permute-done((f32[4,2,16,256]{3,2,1,0:T(8,128)S(1)}, f32[4,2,16,256]{3,2,1,0:T(8,128)S(1)}, u32[]{:S(2)}, u32[]{:S(2)}) %collective-permute-start.7) | collective-permute-done | bytes 131104 | tf_op jit(solution)/shard_map/ppermute | solution.py:369
  17.3 1.8 %collective-permute-start.8 = (f32[8,2,16,256]{3,2,1,0:T(8,128)S(1)}, f32[8,2,16,256]{3,2,1,0:T(8,128)S(1)}, u32[]{:S(2)}, u32[]{:S(2)}) collective-permute-start(f32[8,2,16,256]{3,2,1,0:T(8,128)S(1)} %pad_maximum_fusion.refs_0_), channel_id=1, source_target_pairs={{0,16},{1,17},{2,18},{3,19},{4,20},{5,21},{6,22},{7,23},{8,24},{9,... | collective-permute-start | bytes 786440 | tf_op jit(solution)/shard_map/ppermute | solution.py:369
  19.1 0.0 collective-permute-done.2
  19.2 0.0 copy-start
  19.2 0.0 copy-start.1
  19.2 0.8 %collective-permute-start.3 = (bf16[4,3,2,16,256]{4,3,2,1,0:T(8,128)(2,1)S(1)}, bf16[4,3,2,16,256]{4,3,2,1,0:T(8,128)(2,1)S(1)}, u32[]{:S(2)}, u32[]{:S(2)}) collective-permute-start(bf16[4,3,2,16,256]{4,3,2,1,0:T(8,128)(2,1)S(1)} %pad_maximum_fusion.1.refs_0_), channel_id=1, source_target_pairs={{0,4},{1,5},{2,6},{3,7},{4,0},{5,1},{6,2},{7,3},{8,12},{9,13},{10,... | collective-permute-start | bytes 589832 | tf_op jit(solution)/shard_map/ppermute | solution.py:369
  19.9 0.0 collective-permute-start.9
  19.9 3.8 %collective-permute-done.8.refs_1_ = f32[8,2,16,256]{3,2,1,0:T(8,128)S(1)} collective-permute-done((f32[8,2,16,256]{3,2,1,0:T(8,128)S(1)}, f32[8,2,16,256]{3,2,1,0:T(8,128)S(1)}, u32[]{:S(2)}, u32[]{:S(2)}) %collective-permute-start.8) | collective-permute-done | bytes 262176 | tf_op jit(solution)/shard_map/ppermute | solution.py:369
  23.8 0.0 collective-permute-start.10
  23.8 0.5 %collective-permute-start.4 = (bf16[4,3,2,16,256]{4,3,2,1,0:T(8,128)(2,1)S(1)}, bf16[4,3,2,16,256]{4,3,2,1,0:T(8,128)(2,1)S(1)}, u32[]{:S(2)}, u32[]{:S(2)}) collective-permute-start(bf16[4,3,2,16,256]{4,3,2,1,0:T(8,128)(2,1)S(1)} %pad_maximum_fusion.1.refs_0_), channel_id=1, source_target_pairs={{0,1},{1,0},{2,3},{3,2},{4,5},{5,4},{6,7},{7,6},{8,9},{9,8},{10,11... | collective-permute-start | bytes 589832 | tf_op jit(solution)/shard_map/ppermute | solution.py:369
  24.3 0.6 %collective-permute-done.3.refs_1_ = bf16[4,3,2,16,256]{4,3,2,1,0:T(8,128)(2,1)S(1)} collective-permute-done((bf16[4,3,2,16,256]{4,3,2,1,0:T(8,128)(2,1)S(1)}, bf16[4,3,2,16,256]{4,3,2,1,0:T(8,128)(2,1)S(1)}, u32[]{:S(2)}, u32[]{:S(2)}) %collective-permute-start.3) | collective-permute-done | bytes 196640 | tf_op jit(solution)/shard_map/ppermute | solution.py:369
  24.9 0.0 collective-permute-start.5
  24.9 0.0 collective-permute-done.9.refs_2_
  24.9 0.4 %collective-permute-done.10.refs_3_ = f32[8,2,16,256]{3,2,1,0:T(8,128)S(1)} collective-permute-done((f32[8,2,16,256]{3,2,1,0:T(8,128)S(1)}, f32[8,2,16,256]{3,2,1,0:T(8,128)S(1)}, u32[]{:S(2)}, u32[]{:S(2)}) %collective-permute-start.10) | collective-permute-done | bytes 262176 | tf_op jit(solution)/shard_map/ppermute | solution.py:369
  25.3 0.0 copy-done
  25.3 0.0 copy-done.1
  25.3 1.0 %first_stage.1 = (f32[2,32,16,256]{3,2,1,0:T(8,128)S(1)}, bf16[2,256,512]{2,1,0:T(8,128)(2,1)S(1)}, f32[2,2,256,256]{3,2,1,0:T(8,128)S(1)}, bf16[2,256,256]{2,1,0:T(8,128)(2,1)S(1)}) custom-call(f32[8,2,16,256]{3,2,1,0:T(8,128)S(1)} %pad_maximum_fusion.refs_0_, f32[8,2,16,256]{3,2,1,0:T(8,128)S(1)} %collective-permute-done.8.refs_1_, ...), custom_call_target="tpu_custom_call" | custom-call | tf_op jit(solution)/shard_map/first_stage/pallas_call | solution.py:392
  26.4 0.0 collective-permute-done.4.refs_2_
  26.4 0.0 collective-permute-done.5.refs_3_
  26.4 3.3 %second_stage.1 = f32[2,2,16,256]{3,2,1,0:T(8,128)} custom-call(bf16[4,3,2,16,256]{4,3,2,1,0:T(8,128)(2,1)S(1)} %pad_maximum_fusion.1.refs_0_, bf16[4,3,2,16,256]{4,3,2,1,0:T(8,128)(2,1)S(1)} %collective-permute-done.3.refs_1_, bf16[4,3,2,16,256]{4,3,2,1,0:T(8,128)(2,1)S(1)} %collective-permute-done.4.refs_2_, ...), custom_call_target="tpu_custom_call" | custom-call | tf_op jit(solution)/shard_map/second_stage/pallas_call | solution.py:393
  (9 shorter events, 0.1 us)
Async XLA Ops:
  0.0 7.9 %collective-permute-start = (f32[64,256]{1,0:T(8,128)}, f32[64,256]{1,0:T(8,128)S(1)}, u32[]{:S(2)}, u32[]{:S(2)}) collective-permute-start(f32[64,256]{1,0:T(8,128)} %bitcast.26), channel_id=1, source_target_pairs={{0,8},{1,9},{2,10},{3,11},{4,12},{5,13},{6,14},{7,15},{8,0},{9,1},... | collective-permute-start | bytes 196616 | tf_op jit(solution)/shard_map/ppermute | solution.py:369
  7.9 4.3 %collective-permute-start.6 = (f32[2,2,16,256]{3,2,1,0:T(8,128)S(1)}, f32[2,2,16,256]{3,2,1,0:T(8,128)S(1)}, u32[]{:S(2)}, u32[]{:S(2)}) collective-permute-start(f32[2,2,16,256]{3,2,1,0:T(8,128)S(1)} %pad_maximum_fusion.6), channel_id=1, source_target_pairs={{0,4},{1,5},{2,6},{3,7},{4,0},{5,1},{6,2},{7,3},{8,12},{9,13},{10,... | collective-permute-start | bytes 196616 | tf_op jit(solution)/shard_map/ppermute | solution.py:369
  8.7 5.4 %collective-permute-start.1 = (bf16[2,2,2,16,256]{4,3,2,1,0:T(8,128)(2,1)S(1)}, bf16[2,2,2,16,256]{4,3,2,1,0:T(8,128)(2,1)S(1)}, u32[]{:S(2)}, u32[]{:S(2)}) collective-permute-start(bf16[2,2,2,16,256]{4,3,2,1,0:T(8,128)(2,1)S(1)} %pad_maximum_fusion.5), channel_id=1, source_target_pairs={{0,2},{1,3},{2,0},{3,1},{4,6},{5,7},{6,4},{7,5},{8,10},{9,11},{10,... | collective-permute-start | bytes 196616 | tf_op jit(solution)/shard_map/ppermute | solution.py:369
  12.3 5.0 %collective-permute-start.7 = (f32[4,2,16,256]{3,2,1,0:T(8,128)S(1)}, f32[4,2,16,256]{3,2,1,0:T(8,128)S(1)}, u32[]{:S(2)}, u32[]{:S(2)}) collective-permute-start(f32[4,2,16,256]{3,2,1,0:T(8,128)S(1)} %pad_maximum_fusion.3), channel_id=1, source_target_pairs={{0,2},{1,3},{2,0},{3,1},{4,6},{5,7},{6,4},{7,5},{8,10},{9,11},{10,... | collective-permute-start | bytes 393224 | tf_op jit(solution)/shard_map/ppermute | solution.py:369
  14.1 5.0 %collective-permute-start.2 = (bf16[4,2,16,256]{3,2,1,0:T(8,128)(2,1)S(1)}, bf16[4,2,16,256]{3,2,1,0:T(8,128)(2,1)S(1)}, u32[]{:S(2)}, u32[]{:S(2)}) collective-permute-start(bf16[4,2,16,256]{3,2,1,0:T(8,128)(2,1)S(1)} %get-tuple-element.14), channel_id=1, source_target_pairs={{0,16},{1,17},{2,18},{3,19},{4,20},{5,21},{6,22},{7,23},{8,24},{9,... | collective-permute-start | bytes 196616 | tf_op jit(solution)/shard_map/ppermute | solution.py:369
  17.3 6.4 %collective-permute-start.8 = (f32[8,2,16,256]{3,2,1,0:T(8,128)S(1)}, f32[8,2,16,256]{3,2,1,0:T(8,128)S(1)}, u32[]{:S(2)}, u32[]{:S(2)}) collective-permute-start(f32[8,2,16,256]{3,2,1,0:T(8,128)S(1)} %pad_maximum_fusion.refs_0_), channel_id=1, source_target_pairs={{0,16},{1,17},{2,18},{3,19},{4,20},{5,21},{6,22},{7,23},{8,24},{9,... | collective-permute-start | bytes 786440 | tf_op jit(solution)/shard_map/ppermute | solution.py:369
  19.2 6.2 %copy-start = (f32[32,32]{1,0:T(8,128)S(1)}, f32[32,32]{1,0:T(8,128)}, u32[]{:S(2)}) copy-start(f32[32,32]{1,0:T(8,128)} %refs_4_.3) | copy-start | bytes 12292
  19.2 6.2 %copy-start.1 = (f32[32,32]{1,0:T(8,128)S(1)}, f32[32,32]{1,0:T(8,128)}, u32[]{:S(2)}) copy-start(f32[32,32]{1,0:T(8,128)} %refs_5_.3) | copy-start | bytes 12292
  19.2 5.7 %collective-permute-start.3 = (bf16[4,3,2,16,256]{4,3,2,1,0:T(8,128)(2,1)S(1)}, bf16[4,3,2,16,256]{4,3,2,1,0:T(8,128)(2,1)S(1)}, u32[]{:S(2)}, u32[]{:S(2)}) collective-permute-start(bf16[4,3,2,16,256]{4,3,2,1,0:T(8,128)(2,1)S(1)} %pad_maximum_fusion.1.refs_0_), channel_id=1, source_target_pairs={{0,4},{1,5},{2,6},{3,7},{4,0},{5,1},{6,2},{7,3},{8,12},{9,13},{10,... | collective-permute-start | bytes 589832 | tf_op jit(solution)/shard_map/ppermute | solution.py:369
  19.9 5.0 %collective-permute-start.9 = (f32[8,2,16,256]{3,2,1,0:T(8,128)S(1)}, f32[8,2,16,256]{3,2,1,0:T(8,128)S(1)}, u32[]{:S(2)}, u32[]{:S(2)}) collective-permute-start(f32[8,2,16,256]{3,2,1,0:T(8,128)S(1)} %pad_maximum_fusion.refs_0_), channel_id=1, source_target_pairs={{0,1},{1,0},{2,3},{3,2},{4,5},{5,4},{6,7},{7,6},{8,9},{9,8},{10,11... | collective-permute-start | bytes 786440 | tf_op jit(solution)/shard_map/ppermute | solution.py:369
  23.8 1.5 %collective-permute-start.10 = (f32[8,2,16,256]{3,2,1,0:T(8,128)S(1)}, f32[8,2,16,256]{3,2,1,0:T(8,128)S(1)}, u32[]{:S(2)}, u32[]{:S(2)}) collective-permute-start(f32[8,2,16,256]{3,2,1,0:T(8,128)S(1)} %collective-permute-done.8.refs_1_), channel_id=1, source_target_pairs={{0,1},{1,0},{2,3},{3,2},{4,5},{5,4},{6,7},{7,6},{8,9},{9,8},{10,11... | collective-permute-start | bytes 786440 | tf_op jit(solution)/shard_map/ppermute | solution.py:369
  23.8 2.6 %collective-permute-start.4 = (bf16[4,3,2,16,256]{4,3,2,1,0:T(8,128)(2,1)S(1)}, bf16[4,3,2,16,256]{4,3,2,1,0:T(8,128)(2,1)S(1)}, u32[]{:S(2)}, u32[]{:S(2)}) collective-permute-start(bf16[4,3,2,16,256]{4,3,2,1,0:T(8,128)(2,1)S(1)} %pad_maximum_fusion.1.refs_0_), channel_id=1, source_target_pairs={{0,1},{1,0},{2,3},{3,2},{4,5},{5,4},{6,7},{7,6},{8,9},{9,8},{10,11... | collective-permute-start | bytes 589832 | tf_op jit(solution)/shard_map/ppermute | solution.py:369
  24.9 1.4 %collective-permute-start.5 = (bf16[4,3,2,16,256]{4,3,2,1,0:T(8,128)(2,1)S(1)}, bf16[4,3,2,16,256]{4,3,2,1,0:T(8,128)(2,1)S(1)}, u32[]{:S(2)}, u32[]{:S(2)}) collective-permute-start(bf16[4,3,2,16,256]{4,3,2,1,0:T(8,128)(2,1)S(1)} %collective-permute-done.3.refs_1_), channel_id=1, source_target_pairs={{0,1},{1,0},{2,3},{3,2},{4,5},{5,4},{6,7},{7,6},{8,9},{9,8},{10,11... | collective-permute-start | bytes 589832 | tf_op jit(solution)/shard_map/ppermute | solution.py:369

commit v7 on v5

--- a/solution.py
+++ b/solution.py
@@ -123,10 +123,10 @@
     return current.reshape(2, groups, 1, stripe, block_rows)
 
 
-def exchange_masks(ta_count, tp_count):
+def exchange_masks(tp_count):
     bits = [1 << bit for bit in reversed(range(1, tp_count.bit_length() - 1))]
-    first, middle, last = bits[:1], bits[1:-1], bits[-1:]
-    return first + last + [ta_count * tp_count // 2] + middle, first + middle + last
+    top, middle = bits[:1], bits[1:-1]
+    return bits[-1], top + [tp_count] + middle, middle + top + [tp_count]
 
 
 def offsets_of(masks):
@@ -197,96 +197,88 @@
     return values[0] + 0.5 * turned[1], values[1] - 0.5 * turned[0]
 
 
-def placed(tp_count, stripe, flip, mask):
-    me = lax.axis_index("ta") * tp_count + lax.axis_index("tp")
-    device = me ^ (flip ^ mask)
-    return device // tp_count, pl.multiple_of((device % tp_count) * stripe, stripe)
-
-
-def first_stage(masks, tp_count, stripe, block_rows, factor):
+def whole(source, block, tp_count, block_rows):
+    return [
+        source[part, block * tp_count : (block + 1) * tp_count].reshape(block_rows, block_rows)
+        for part in range(2)
+    ]
+
+
+def second_group(masks, tp_count, stripe, block_rows, factor):
     offsets = offsets_of(masks)
-    half_count = len(offsets) // 2
+    scale = 0.5 * factor
 
     def kernel(*refs):
-        sources = refs[:4]
-        hamiltonian, interaction, values, lows, bases, window = refs[4:]
+        sources, hamiltonian, interaction = refs[:4], refs[4], refs[5]
+        highs, bases, window, mirror, rests = refs[6:]
+        me = lax.axis_index("ta") * tp_count + lax.axis_index("tp")
+        blank = jnp.zeros((stripe, block_rows), jnp.bfloat16)
         for flip in range(2):
+            both, opposite = sources[2 * flip], sources[2 * flip + 1]
             for index, mask in enumerate(offsets):
-                late, slot = divmod(index, half_count)
-                block, row = placed(tp_count, stripe, flip, mask)
+                device = me ^ (flip ^ mask)
+                other = device ^ tp_count
                 for part in range(2):
-                    values[part, block, pl.ds(row, stripe), :] = sources[2 * flip + late][
-                        slot, part
-                    ]
+                    highs[part, device] = both[0, index, part]
+                    rests[part, device] = both[1, index, part]
+                    highs[part, other] = opposite[index, part]
+                    rests[part, other] = blank
         weights, table = tables_of(hamiltonian, interaction, block_rows)
         for block in range(2):
-            current = [values[part, block] for part in range(2)]
-            split = [halves(part) for part in current]
-            high = [part[0] for part in split]
-            base = one_body(current, high, [part[1] for part in split], table)
-            for part in range(2):
-                lows[part, :, block * block_rows : (block + 1) * block_rows] = high[part]
+            high = whole(highs, block, tp_count, block_rows)
+            rest = whole(rests, block, tp_count, block_rows)
+            full = [high[k].astype(jnp.float32) + rest[k].astype(jnp.float32) for k in range(2)]
+            base = one_body(full, high, rest, table)
+            turned = mirrored(high)
             if block == 0:
-                made = window_of(current, mirrored(high), weights, 0)
+                mirror[0] = turned[0]
+                mirror[1] = turned[1]
+            else:
+                made = window_of(full, turned, weights, 0)
                 memory = products(high, made)
-                scale = 0.5 * factor
                 base = (base[0] + scale * memory[1], base[1] - scale * memory[0])
                 window[0] = made[0]
                 window[1] = made[1]
             bases[0, block] = base[0]
             bases[1, block] = base[1]
 
-    block = jax.ShapeDtypeStruct((2, 2, block_rows, block_rows), jnp.float32)
+    square = (2, block_rows, block_rows)
+    pieces = (2, 2 * tp_count, stripe, block_rows)
     return pl.pallas_call(
         kernel,
         out_shape=[
-            block,
-            jax.ShapeDtypeStruct((2, block_rows, 2 * block_rows), jnp.bfloat16),
-            block,
-            jax.ShapeDtypeStruct((2, block_rows, block_rows), jnp.bfloat16),
+            jax.ShapeDtypeStruct(pieces, jnp.bfloat16),
+            jax.ShapeDtypeStruct((2,) + square, jnp.float32),
+            jax.ShapeDtypeStruct(square, jnp.bfloat16),
+            jax.ShapeDtypeStruct(square, jnp.float32),
         ],
         in_specs=[pl.BlockSpec(memory_space=pltpu.VMEM)] * 6,
         out_specs=[pl.BlockSpec(memory_space=pltpu.VMEM)] * 4,
+        scratch_shapes=[pltpu.VMEM(pieces, jnp.bfloat16)],
         compiler_params=pltpu.CompilerParams(vmem_limit_bytes=16 << 20),
-        name="first_stage",
-    )
-
-
-def second_stage(masks, tp_count, stripe, block_rows, factor):
+        name="second_group",
+    )
+
+
+def both_groups(masks, tp_count, stripe, block_rows, factor):
     offsets = offsets_of(masks)
     half_count = len(offsets) // 2
     order_size = 2 * block_rows
     scale = 0.5 * factor
 
     def kernel(*refs):
-        sources = refs[:4]
-        hamiltonian, interaction, values, lows, bases, window = refs[4:10]
-        out, highs, rests, nexts, low_next = refs[10:]
+        sources, hamiltonian, interaction = refs[:4], refs[4], refs[5]
+        highs, bases, window, mirror, out, values, nexts, low_next = refs[6:]
         ta_place = lax.axis_index("ta")
         tp_place = lax.axis_index("tp")
+        me = ta_place * tp_count + tp_place
         for flip in range(2):
             for index, mask in enumerate(offsets):
                 late, slot = divmod(index, half_count)
-                block, row = placed(tp_count, stripe, flip, mask)
-                source = sources[2 * flip + late]
+                device = me ^ (flip ^ mask)
                 for part in range(2):
-                    highs[part, block, pl.ds(row, stripe), :] = source[slot, 0, part]
-                    highs[part, 1 - block, pl.ds(row, stripe), :] = source[slot, 1, part]
-                    rests[part, block, pl.ds(row, stripe), :] = source[slot, 2, part]
-                    rests[part, 1 - block, pl.ds(row, stripe), :] = jnp.zeros(
-                        (stripe, block_rows), jnp.bfloat16
-                    )
+                    values[part, device] = sources[2 * flip + late][slot, part]
         weights, table = tables_of(hamiltonian, interaction, block_rows)
-        high = [[highs[part, block] for part in range(2)] for block in range(2)]
-        rest = [[rests[part, block] for part in range(2)] for block in range(2)]
-        full = [
-            [
-                high[block][part].astype(jnp.float32) + rest[block][part].astype(jnp.float32)
-                for part in range(2)
-            ]
-            for block in range(2)
-        ]
-        base = [one_body(full[block], high[block], rest[block], table) for block in range(2)]
 
         def stored(block, group, real, imag):
             for part, result in ((0, real), (1, imag)):
@@ -295,28 +287,33 @@
                     result.astype(jnp.bfloat16)
                 )
 
-        stored(0, 0, bases[0, 0], bases[1, 0])
-        memory = products(high[0], (window[0], window[1]))
-        stored(0, 1, base[0][0] + scale * memory[1], base[0][1] - scale * memory[0])
-        later = [
-            window_of(
-                [values[part, 1] for part in range(2)], mirrored(high[0]), weights, block_rows // NO
-            ),
-            window_of(full[1], mirrored(high[1]), weights, 0),
+        second_high = whole(highs, 0, tp_count, block_rows)
+        current = [whole(values, block, tp_count, block_rows) for block in range(2)]
+        split = [[halves(part) for part in current[block]] for block in range(2)]
+        high = [[part[0] for part in split[block]] for block in range(2)]
+        base = [
+            one_body(current[block], high[block], [part[1] for part in split[block]], table)
+            for block in range(2)
         ]
-        rows = [[lows[part, :, :block_rows] for part in range(2)]]
-        rows.append([lows[part, :, block_rows:] for part in range(2)])
-        early_memory = [products(rows[0], later[0]), products(high[0], later[0])]
-        late_memory = [products(rows[1], later[1]), products(high[1], later[1])]
-        for group in range(2):
-            start = (bases[0, 1], bases[1, 1]) if group == 0 else base[1]
-            real = early_memory[group][0] + late_memory[group][0]
-            imag = early_memory[group][1] + late_memory[group][1]
-            stored(1, group, start[0] + scale * imag, start[1] - scale * real)
-
-        current = [nexts[part, ta_place].reshape(order_size, block_rows) for part in range(2)]
-        mirror = mirrored([low_next[part, ta_place] for part in range(2)])
-        last = window_of(current, mirror, weights, ta_place * (block_rows // NO))
+        early = window_of(current[0], mirrored(high[0]), weights, 0)
+        for group, rows in ((0, high[0]), (1, second_high)):
+            start = base[0] if group == 0 else (bases[0, 0], bases[1, 0])
+            memory = products(rows, early)
+            stored(0, group, start[0] + scale * memory[1], start[1] - scale * memory[0])
+        cross = window_of(
+            current[1], [mirror[0], mirror[1]], weights, block_rows // NO
+        )
+        memory = products(second_high, cross)
+        stored(1, 1, bases[0, 1] + scale * memory[1], bases[1, 1] - scale * memory[0])
+        memory = products(high[0], cross)
+        late = products(high[1], [window[0], window[1]])
+        real = memory[0] + late[0]
+        imag = memory[1] + late[1]
+        stored(1, 0, base[1][0] + scale * imag, base[1][1] - scale * real)
+
+        present = [nexts[part, ta_place].reshape(order_size, block_rows) for part in range(2)]
+        turned = mirrored([low_next[part, ta_place] for part in range(2)])
+        last = window_of(present, turned, weights, ta_place * (block_rows // NO))
         row = pl.multiple_of(tp_place * stripe, stripe)
         own = [
             nexts[part, ta_place, :, pl.ds(row, stripe), :].reshape(2 * stripe, block_rows)
@@ -340,13 +337,12 @@
         in_specs=[pl.BlockSpec(memory_space=pltpu.VMEM)] * 10,
         out_specs=pl.BlockSpec(memory_space=pltpu.VMEM),
         scratch_shapes=[
-            pltpu.VMEM(square, jnp.bfloat16),
-            pltpu.VMEM(square, jnp.bfloat16),
+            pltpu.VMEM((2, 2 * tp_count, stripe, block_rows), jnp.float32),
             pltpu.VMEM((2,) + square, jnp.float32),
             pltpu.VMEM((2, 2, block_rows, order_size), jnp.bfloat16),
         ],
         compiler_params=pltpu.CompilerParams(vmem_limit_bytes=24 << 20),
-        name="second_stage",
+        name="both_groups",
     )
 
 
@@ -356,33 +352,34 @@
     stripe = green.shape[3]
     block_rows = green.shape[4]
     factor = 1.0 / math.sqrt(2 * block_rows)
-    first_masks, second_masks = exchange_masks(2, tp_count)
+    mask, first_masks, second_masks = exchange_masks(tp_count)
 
     def exchanged(block, mask):
         return lax.ppermute(block, ("ta", "tp"), [(i, i ^ mask) for i in range(count)])
 
-    first = green[:, 0, 0]
-    second = green[:, 1, 0]
+    arriving = exchanged(green.reshape(-1, block_rows), mask).reshape(green.shape)
+    first = jnp.stack([green[:, 0, 0], arriving[:, 0, 0]])
+    second = jnp.stack([green[:, 1, 0], arriving[:, 1, 0]])
     high = lax.reduce_precision(second, 8, 7)
-    low = (second - high).astype(jnp.bfloat16)
-    high = high.astype(jnp.bfloat16)
-    arriving = exchanged(first, first_masks[0])
-    other_high = exchanged(high, tp_count)
-    first = jnp.stack([first, arriving])
-    second = jnp.stack([high, other_high, low])[None]
-    for first_mask, second_mask in zip(first_masks[1:-1], second_masks[:-1]):
-        arriving = exchanged(first, first_mask)
-        second_arriving = exchanged(second, second_mask)
-        first = jnp.concatenate([first, arriving])
-        second = jnp.concatenate([second, second_arriving])
-    first_parts = [first, exchanged(first, first_masks[-1])]
-    second_parts = [second, exchanged(second, second_masks[-1])]
+    second = jnp.stack([high, second - high]).astype(jnp.bfloat16)
+    first_parts = second_parts = ()
+    for first_mask, second_mask in zip(first_masks, second_masks):
+        first_parts = [first, exchanged(first, first_mask)]
+        first = jnp.concatenate(first_parts)
+        if second_mask == tp_count:
+            second_parts = [second, exchanged(second[0], second_mask)]
+        else:
+            second = jnp.concatenate([second, exchanged(second, second_mask)], 1)
     first_parts += [exchanged(part, 1) for part in first_parts]
     second_parts += [exchanged(part, 1) for part in second_parts]
-    early = first_stage(first_masks, tp_count, stripe, block_rows, factor)
-    late = second_stage(second_masks, tp_count, stripe, block_rows, factor)
-    known = early(*first_parts, hamiltonian, interaction)
-    return late(*second_parts, hamiltonian, interaction, *known)[:, :, None]
+    sizes = (tp_count, stripe, block_rows, factor)
+    known = second_group([mask] + second_masks[:-1], *sizes)(
+        *second_parts, hamiltonian, interaction
+    )
+    result = both_groups([mask] + first_masks, *sizes)(
+        *first_parts, hamiltonian, interaction, *known
+    )
+    return result[:, :, None]
 
 
 def solution(mesh):
@@ -393,7 +390,7 @@
 
     def shards(green, hamiltonian, interaction):
         whole_bytes = green.size * green.dtype.itemsize * ta_count * tp_count
-        covered = ta_count == 2 and green.shape[1] == 2 and tp_count >= 8
+        covered = ta_count == 2 and green.shape[1] == 2 and tp_count >= 16
         if covered and tp_count & (tp_count - 1) == 0 and whole_bytes <= 1 << 22:
             return replicated(green, hamiltonian, interaction)
         return windowed(green, hamiltonian, interaction)

time: 30.4 us -> 30.2 us (level)
  waiting for transfers between devices: 8.24 us -> 8.76 us
  starting transfers between devices: 16.5 us -> 16 us
  Pallas kernels: 4.5 us -> 4.17 us
    ppermute x12 -> x11, waiting for transfers between devices: 8.24 us -> 8.76 us  [exchanged(): lax.ppermute(block, ('ta', 'tp'), [(i, i ^ mask) for i in range(count)])]
    ppermute x12 -> x11, starting transfers between devices: 16.5 us -> 16 us  [exchanged(): lax.ppermute(block, ('ta', 'tp'), [(i, i ^ mask) for i in range(count)])]
    pallas_call x2, Pallas kernels: 4.5 us -> 4.17 us  [the longest x1 3.18 us: replicated(): both_groups([mask] + first_masks, *sizes)]
    another operation x1 -> x2, local copies, waits for them, and re-layouts: 0.83 us -> 0.8 us  [replicated(): second = jnp.stack([green[:, 1, 0], arriving[:, 1, 0]])]
  transfers between devices with their start and end apart: 12 -> 11, of which waited for: 8 -> 8; matrix products, arithmetic and copies ran while one was open for 0% -> 3% of each run, Pallas kernels for 4% -> 3%
where the time goes in v7:
time: 30.2 us; the launch traced here: 29.9 us
  starting transfers between devices  16 us (53%)
  waiting for transfers between devices  8.76 us (29%)
  Pallas kernels  4.17 us (14%)
  local copies, waits for them, and re-layouts  0.83 us (3%)
    ppermute x11, starting transfers between devices, exchanged(): lax.ppermute(block, ('ta', 'tp'), [(i, i ^ mask) for i in range(count)])  16 us
    ppermute x11, waiting for transfers between devices, exchanged(): lax.ppermute(block, ('ta', 'tp'), [(i, i ^ mask) for i in range(count)])  8.76 us
    pallas_call x1, Pallas kernels, replicated(): both_groups([mask] + first_masks, *sizes)  3.18 us
    pallas_call x1, Pallas kernels, replicated(): second_group([mask] + second_masks[:-1], *sizes)  0.98 us
    another operation x2, local copies, waits for them, and re-layouts, replicated(): second = jnp.stack([green[:, 1, 0], arriving[:, 1, 0]])  0.8 us
  transfers between devices with their start and end apart: 11, of which 8 were waited for; matrix products, arithmetic and copies ran while one was open for 3% of the time, Pallas kernels for 3%

profile of v7, /device:TPU:0, one launch (start us, length us, event | category | flops | bytes accessed | tf_op | source)
XLA Modules:
  0.0 29.9 jit_solution(10104690962598860852)
XLA Ops:
  0.0 3.0 %collective-permute-start = (f32[64,256]{1,0:T(8,128)}, f32[64,256]{1,0:T(8,128)S(1)}, u32[]{:S(2)}, u32[]{:S(2)}) collective-permute-start(f32[64,256]{1,0:T(8,128)} %bitcast.23), channel_id=1, source_target_pairs={{0,2},{1,3},{2,0},{3,1},{4,6},{5,7},{6,4},{7,5},{8,10},{9,11},{10,... | collective-permute-start | bytes 196616 | tf_op jit(solution)/shard_map/ppermute | solution.py:358
  3.0 0.8 %slice_bitcast_fusion.3 = (f32[1,1,2,16,256]{4,3,2,1,0:T(8,128)S(1)}, f32[1,2,16,256]{3,2,1,0:T(8,128)S(1)}) fusion(f32[2,2,1,16,256]{4,3,2,1,0:T(8,128)} %param.3), kind=kLoop, calls=%fused_computation.13 | loop fusion | bytes 131072 | tf_op jit(solution)/shard_map/stack | solution.py:362
  3.8 1.7 %collective-permute-done = f32[64,256]{1,0:T(8,128)S(1)} collective-permute-done((f32[64,256]{1,0:T(8,128)}, f32[64,256]{1,0:T(8,128)S(1)}, u32[]{:S(2)}, u32[]{:S(2)}) %collective-permute-start) | collective-permute-done | bytes 65568 | tf_op jit(solution)/shard_map/ppermute | solution.py:358
  5.5 3.2 %collective-permute-start.1 = (f32[2,2,16,256]{3,2,1,0:T(8,128)S(1)}, f32[2,2,16,256]{3,2,1,0:T(8,128)S(1)}, u32[]{:S(2)}, u32[]{:S(2)}) collective-permute-start(f32[2,2,16,256]{3,2,1,0:T(8,128)S(1)} %pad_maximum_fusion.4), channel_id=1, source_target_pairs={{0,8},{1,9},{2,10},{3,11},{4,12},{5,13},{6,14},{7,15},{8,0},{9,1},... | collective-permute-start | bytes 196616 | tf_op jit(solution)/shard_map/ppermute | solution.py:358
  8.7 1.6 %collective-permute-start.6 = (bf16[2,2,2,16,256]{4,3,2,1,0:T(8,128)(2,1)S(1)}, bf16[2,2,2,16,256]{4,3,2,1,0:T(8,128)(2,1)S(1)}, u32[]{:S(2)}, u32[]{:S(2)}) collective-permute-start(bf16[2,2,2,16,256]{4,3,2,1,0:T(8,128)(2,1)S(1)} %pad_maximum_fusion.6), channel_id=1, source_target_pairs={{0,4},{1,5},{2,6},{3,7},{4,0},{5,1},{6,2},{7,3},{8,12},{9,13},{10,... | collective-permute-start | bytes 196616 | tf_op jit(solution)/shard_map/ppermute | solution.py:358
  10.3 0.7 %collective-permute-done.1 = f32[2,2,16,256]{3,2,1,0:T(8,128)S(1)} collective-permute-done((f32[2,2,16,256]{3,2,1,0:T(8,128)S(1)}, f32[2,2,16,256]{3,2,1,0:T(8,128)S(1)}, u32[]{:S(2)}, u32[]{:S(2)}) %collective-permute-start.1) | collective-permute-done | bytes 65568 | tf_op jit(solution)/shard_map/ppermute | solution.py:358
  11.0 1.8 %collective-permute-start.2 = (f32[4,2,16,256]{3,2,1,0:T(8,128)S(1)}, f32[4,2,16,256]{3,2,1,0:T(8,128)S(1)}, u32[]{:S(2)}, u32[]{:S(2)}) collective-permute-start(f32[4,2,16,256]{3,2,1,0:T(8,128)S(1)} %pad_maximum_fusion.2), channel_id=1, source_target_pairs={{0,16},{1,17},{2,18},{3,19},{4,20},{5,21},{6,22},{7,23},{8,24},{9,... | collective-permute-start | bytes 393224 | tf_op jit(solution)/shard_map/ppermute | solution.py:358
  12.8 0.2 collective-permute-done.6
  13.0 2.5 %collective-permute-start.7 = (bf16[2,4,2,16,256]{4,3,2,1,0:T(8,128)(2,1)S(1)}, bf16[2,4,2,16,256]{4,3,2,1,0:T(8,128)(2,1)S(1)}, u32[]{:S(2)}, u32[]{:S(2)}) collective-permute-start(bf16[2,4,2,16,256]{4,3,2,1,0:T(8,128)(2,1)S(1)} %pad_maximum_fusion.3), channel_id=1, source_target_pairs={{0,8},{1,9},{2,10},{3,11},{4,12},{5,13},{6,14},{7,15},{8,0},{9,1},... | collective-permute-start | bytes 393224 | tf_op jit(solution)/shard_map/ppermute | solution.py:358
  15.5 0.5 %collective-permute-done.2 = f32[4,2,16,256]{3,2,1,0:T(8,128)S(1)} collective-permute-done((f32[4,2,16,256]{3,2,1,0:T(8,128)S(1)}, f32[4,2,16,256]{3,2,1,0:T(8,128)S(1)}, u32[]{:S(2)}, u32[]{:S(2)}) %collective-permute-start.2) | collective-permute-done | bytes 131104 | tf_op jit(solution)/shard_map/ppermute | solution.py:358
  16.0 1.9 %collective-permute-start.3 = (f32[8,2,16,256]{3,2,1,0:T(8,128)S(1)}, f32[8,2,16,256]{3,2,1,0:T(8,128)S(1)}, u32[]{:S(2)}, u32[]{:S(2)}) collective-permute-start(f32[8,2,16,256]{3,2,1,0:T(8,128)S(1)} %pad_maximum_fusion.refs_0_), channel_id=1, source_target_pairs={{0,4},{1,5},{2,6},{3,7},{4,0},{5,1},{6,2},{7,3},{8,12},{9,13},{10,... | collective-permute-start | bytes 786440 | tf_op jit(solution)/shard_map/ppermute | solution.py:358
  17.9 1.4 %collective-permute-done.7 = bf16[2,4,2,16,256]{4,3,2,1,0:T(8,128)(2,1)S(1)} collective-permute-done((bf16[2,4,2,16,256]{4,3,2,1,0:T(8,128)(2,1)S(1)}, bf16[2,4,2,16,256]{4,3,2,1,0:T(8,128)(2,1)S(1)}, u32[]{:S(2)}, u32[]{:S(2)}) %collective-permute-start.7) | collective-permute-done | bytes 131104 | tf_op jit(solution)/shard_map/ppermute | solution.py:358
  19.3 0.0 copy-start
  19.3 0.0 copy-start.1
  19.4 1.5 %collective-permute-start.8 = (bf16[8,2,16,256]{3,2,1,0:T(8,128)(2,1)S(1)}, bf16[8,2,16,256]{3,2,1,0:T(8,128)(2,1)S(1)}, u32[]{:S(2)}, u32[]{:S(2)}) collective-permute-start(bf16[8,2,16,256]{3,2,1,0:T(8,128)(2,1)S(1)} %slice_bitcast_fusion), channel_id=1, source_target_pairs={{0,16},{1,17},{2,18},{3,19},{4,20},{5,21},{6,22},{7,23},{8,24},{9,... | collective-permute-start | bytes 393224 | tf_op jit(solution)/shard_map/ppermute | solution.py:358
  20.9 0.0 collective-permute-start.9
  20.9 0.5 %collective-permute-start.4 = (f32[8,2,16,256]{3,2,1,0:T(8,128)S(1)}, f32[8,2,16,256]{3,2,1,0:T(8,128)S(1)}, u32[]{:S(2)}, u32[]{:S(2)}) collective-permute-start(f32[8,2,16,256]{3,2,1,0:T(8,128)S(1)} %pad_maximum_fusion.refs_0_), channel_id=1, source_target_pairs={{0,1},{1,0},{2,3},{3,2},{4,5},{5,4},{6,7},{7,6},{8,9},{9,8},{10,11... | collective-permute-start | bytes 786440 | tf_op jit(solution)/shard_map/ppermute | solution.py:358
  21.4 1.9 %collective-permute-done.3.refs_1_ = f32[8,2,16,256]{3,2,1,0:T(8,128)S(1)} collective-permute-done((f32[8,2,16,256]{3,2,1,0:T(8,128)S(1)}, f32[8,2,16,256]{3,2,1,0:T(8,128)S(1)}, u32[]{:S(2)}, u32[]{:S(2)}) %collective-permute-start.3) | collective-permute-done | bytes 262176 | tf_op jit(solution)/shard_map/ppermute | solution.py:358
  23.3 0.0 collective-permute-start.5
  23.3 1.1 %collective-permute-done.8.refs_1_ = bf16[8,2,16,256]{3,2,1,0:T(8,128)(2,1)S(1)} collective-permute-done((bf16[8,2,16,256]{3,2,1,0:T(8,128)(2,1)S(1)}, bf16[8,2,16,256]{3,2,1,0:T(8,128)(2,1)S(1)}, u32[]{:S(2)}, u32[]{:S(2)}) %collective-permute-start.8) | collective-permute-done | bytes 131104 | tf_op jit(solution)/shard_map/ppermute | solution.py:358
  24.4 0.0 collective-permute-start.10
  24.4 1.3 %collective-permute-done.10.refs_3_ = bf16[8,2,16,256]{3,2,1,0:T(8,128)(2,1)S(1)} collective-permute-done((bf16[8,2,16,256]{3,2,1,0:T(8,128)(2,1)S(1)}, bf16[8,2,16,256]{3,2,1,0:T(8,128)(2,1)S(1)}, u32[]{:S(2)}, u32[]{:S(2)}) %collective-permute-start.10) | collective-permute-done | bytes 131104 | tf_op jit(solution)/shard_map/ppermute | solution.py:358
  25.7 0.0 collective-permute-done.9.refs_2_
  25.7 0.0 copy-done
  25.7 0.0 copy-done.1
  25.7 1.0 %second_group.1 = (bf16[2,32,16,256]{3,2,1,0:T(8,128)(2,1)S(1)}, f32[2,2,256,256]{3,2,1,0:T(8,128)S(1)}, bf16[2,256,256]{2,1,0:T(8,128)(2,1)S(1)}, f32[2,256,256]{2,1,0:T(8,128)S(1)}) custom-call(bf16[2,8,2,16,256]{4,3,2,1,0:T(8,128)(2,1)S(1)} %pad_maximum_fusion.1.refs_0_, bf16[8,2,16,256]{3,2,1,0:T(8,128)(2,1)S(1)} %collective-permute-done.8.refs_1_, ...), custom_call_target="tpu_custom_call" | custom-call | tf_op jit(solution)/shard_map/second_group/pallas_call | solution.py:376
  26.7 0.0 collective-permute-done.4.refs_2_
  26.7 0.0 collective-permute-done.5.refs_3_
  26.8 3.2 %both_groups.1 = f32[2,2,16,256]{3,2,1,0:T(8,128)} custom-call(f32[8,2,16,256]{3,2,1,0:T(8,128)S(1)} %pad_maximum_fusion.refs_0_, f32[8,2,16,256]{3,2,1,0:T(8,128)S(1)} %collective-permute-done.3.refs_1_, f32[8,2,16,256]{3,2,1,0:T(8,128)S(1)} %collective-permute-done.4.refs_2_, f32[8,2,16,256]{3,2,1,0:T(8,128)S(1)} %collective-permute-done.5.refs_3_, ...), custom_call_target="tpu_custom_call" | custom-call | tf_op jit(solution)/shard_map/both_groups/pallas_call | solution.py:379
  (9 shorter events, 0.1 us)
Async XLA Ops:
  0.0 5.4 %collective-permute-start = (f32[64,256]{1,0:T(8,128)}, f32[64,256]{1,0:T(8,128)S(1)}, u32[]{:S(2)}, u32[]{:S(2)}) collective-permute-start(f32[64,256]{1,0:T(8,128)} %bitcast.23), channel_id=1, source_target_pairs={{0,2},{1,3},{2,0},{3,1},{4,6},{5,7},{6,4},{7,5},{8,10},{9,11},{10,... | collective-permute-start | bytes 196616 | tf_op jit(solution)/shard_map/ppermute | solution.py:358
  5.5 5.5 %collective-permute-start.1 = (f32[2,2,16,256]{3,2,1,0:T(8,128)S(1)}, f32[2,2,16,256]{3,2,1,0:T(8,128)S(1)}, u32[]{:S(2)}, u32[]{:S(2)}) collective-permute-start(f32[2,2,16,256]{3,2,1,0:T(8,128)S(1)} %pad_maximum_fusion.4), channel_id=1, source_target_pairs={{0,8},{1,9},{2,10},{3,11},{4,12},{5,13},{6,14},{7,15},{8,0},{9,1},... | collective-permute-start | bytes 196616 | tf_op jit(solution)/shard_map/ppermute | solution.py:358
  8.7 4.3 %collective-permute-start.6 = (bf16[2,2,2,16,256]{4,3,2,1,0:T(8,128)(2,1)S(1)}, bf16[2,2,2,16,256]{4,3,2,1,0:T(8,128)(2,1)S(1)}, u32[]{:S(2)}, u32[]{:S(2)}) collective-permute-start(bf16[2,2,2,16,256]{4,3,2,1,0:T(8,128)(2,1)S(1)} %pad_maximum_fusion.6), channel_id=1, source_target_pairs={{0,4},{1,5},{2,6},{3,7},{4,0},{5,1},{6,2},{7,3},{8,12},{9,13},{10,... | collective-permute-start | bytes 196616 | tf_op jit(solution)/shard_map/ppermute | solution.py:358
  11.0 5.0 %collective-permute-start.2 = (f32[4,2,16,256]{3,2,1,0:T(8,128)S(1)}, f32[4,2,16,256]{3,2,1,0:T(8,128)S(1)}, u32[]{:S(2)}, u32[]{:S(2)}) collective-permute-start(f32[4,2,16,256]{3,2,1,0:T(8,128)S(1)} %pad_maximum_fusion.2), channel_id=1, source_target_pairs={{0,16},{1,17},{2,18},{3,19},{4,20},{5,21},{6,22},{7,23},{8,24},{9,... | collective-permute-start | bytes 393224 | tf_op jit(solution)/shard_map/ppermute | solution.py:358
  13.0 6.3 %collective-permute-start.7 = (bf16[2,4,2,16,256]{4,3,2,1,0:T(8,128)(2,1)S(1)}, bf16[2,4,2,16,256]{4,3,2,1,0:T(8,128)(2,1)S(1)}, u32[]{:S(2)}, u32[]{:S(2)}) collective-permute-start(bf16[2,4,2,16,256]{4,3,2,1,0:T(8,128)(2,1)S(1)} %pad_maximum_fusion.3), channel_id=1, source_target_pairs={{0,8},{1,9},{2,10},{3,11},{4,12},{5,13},{6,14},{7,15},{8,0},{9,1},... | collective-permute-start | bytes 393224 | tf_op jit(solution)/shard_map/ppermute | solution.py:358
  16.0 7.2 %collective-permute-start.3 = (f32[8,2,16,256]{3,2,1,0:T(8,128)S(1)}, f32[8,2,16,256]{3,2,1,0:T(8,128)S(1)}, u32[]{:S(2)}, u32[]{:S(2)}) collective-permute-start(f32[8,2,16,256]{3,2,1,0:T(8,128)S(1)} %pad_maximum_fusion.refs_0_), channel_id=1, source_target_pairs={{0,4},{1,5},{2,6},{3,7},{4,0},{5,1},{6,2},{7,3},{8,12},{9,13},{10,... | collective-permute-start | bytes 786440 | tf_op jit(solution)/shard_map/ppermute | solution.py:358
  19.3 6.4 %copy-start = (f32[32,32]{1,0:T(8,128)S(1)}, f32[32,32]{1,0:T(8,128)}, u32[]{:S(2)}) copy-start(f32[32,32]{1,0:T(8,128)} %refs_4_.3) | copy-start | bytes 12292
  19.3 6.4 %copy-start.1 = (f32[32,32]{1,0:T(8,128)S(1)}, f32[32,32]{1,0:T(8,128)}, u32[]{:S(2)}) copy-start(f32[32,32]{1,0:T(8,128)} %refs_5_.3) | copy-start | bytes 12292
  19.4 5.0 %collective-permute-start.8 = (bf16[8,2,16,256]{3,2,1,0:T(8,128)(2,1)S(1)}, bf16[8,2,16,256]{3,2,1,0:T(8,128)(2,1)S(1)}, u32[]{:S(2)}, u32[]{:S(2)}) collective-permute-start(bf16[8,2,16,256]{3,2,1,0:T(8,128)(2,1)S(1)} %slice_bitcast_fusion), channel_id=1, source_target_pairs={{0,16},{1,17},{2,18},{3,19},{4,20},{5,21},{6,22},{7,23},{8,24},{9,... | collective-permute-start | bytes 393224 | tf_op jit(solution)/shard_map/ppermute | solution.py:358
  20.9 4.9 %collective-permute-start.9 = (bf16[2,8,2,16,256]{4,3,2,1,0:T(8,128)(2,1)S(1)}, bf16[2,8,2,16,256]{4,3,2,1,0:T(8,128)(2,1)S(1)}, u32[]{:S(2)}, u32[]{:S(2)}) collective-permute-start(bf16[2,8,2,16,256]{4,3,2,1,0:T(8,128)(2,1)S(1)} %pad_maximum_fusion.1.refs_0_), channel_id=1, source_target_pairs={{0,1},{1,0},{2,3},{3,2},{4,5},{5,4},{6,7},{7,6},{8,9},{9,8},{10,11... | collective-permute-start | bytes 786440 | tf_op jit(solution)/shard_map/ppermute | solution.py:358
  20.9 5.9 %collective-permute-start.4 = (f32[8,2,16,256]{3,2,1,0:T(8,128)S(1)}, f32[8,2,16,256]{3,2,1,0:T(8,128)S(1)}, u32[]{:S(2)}, u32[]{:S(2)}) collective-permute-start(f32[8,2,16,256]{3,2,1,0:T(8,128)S(1)} %pad_maximum_fusion.refs_0_), channel_id=1, source_target_pairs={{0,1},{1,0},{2,3},{3,2},{4,5},{5,4},{6,7},{7,6},{8,9},{9,8},{10,11... | collective-permute-start | bytes 786440 | tf_op jit(solution)/shard_map/ppermute | solution.py:358
  23.3 3.5 %collective-permute-start.5 = (f32[8,2,16,256]{3,2,1,0:T(8,128)S(1)}, f32[8,2,16,256]{3,2,1,0:T(8,128)S(1)}, u32[]{:S(2)}, u32[]{:S(2)}) collective-permute-start(f32[8,2,16,256]{3,2,1,0:T(8,128)S(1)} %collective-permute-done.3.refs_1_), channel_id=1, source_target_pairs={{0,1},{1,0},{2,3},{3,2},{4,5},{5,4},{6,7},{7,6},{8,9},{9,8},{10,11... | collective-permute-start | bytes 786440 | tf_op jit(solution)/shard_map/ppermute | solution.py:358
  24.4 1.3 %collective-permute-start.10 = (bf16[8,2,16,256]{3,2,1,0:T(8,128)(2,1)S(1)}, bf16[8,2,16,256]{3,2,1,0:T(8,128)(2,1)S(1)}, u32[]{:S(2)}, u32[]{:S(2)}) collective-permute-start(bf16[8,2,16,256]{3,2,1,0:T(8,128)(2,1)S(1)} %collective-permute-done.8.refs_1_), channel_id=1, source_target_pairs={{0,1},{1,0},{2,3},{3,2},{4,5},{5,4},{6,7},{7,6},{8,9},{9,8},{10,11... | collective-permute-start | bytes 393224 | tf_op jit(solution)/shard_map/ppermute | solution.py:358

commit v8 on v6

--- a/solution.py
+++ b/solution.py
@@ -123,11 +123,11 @@
     return current.reshape(2, groups, 1, stripe, block_rows)
 
 
-def exchange_masks(ta_count, tp_count):
+def exchange_masks(tp_count):
     bits = [1 << bit for bit in reversed(range(1, tp_count.bit_length() - 1))]
-    first, middle, last = bits[0], bits[1:-1], bits[-1:]
-    ta_bit = [ta_count * tp_count // 2]
-    return first, middle + last + ta_bit, last + ta_bit + middle
+    middle, low, ta_bit = bits[1:-1], bits[-1:], [tp_count]
+    even, odd = ta_bit + middle + low, low + middle + ta_bit
+    return bits[0], (even, odd), ta_bit + low + middle
 
 
 def offsets_of(masks):
@@ -199,16 +199,17 @@
 
 
 def first_stage(masks, tp_count, stripe, block_rows, factor):
-    offsets = offsets_of(masks)
-    half_count = len(offsets) // 2
+    offsets = [offsets_of(each) for each in masks]
+    half_count = len(offsets[0]) // 2
 
     def kernel(*refs):
         sources = refs[:4]
         hamiltonian, interaction, values, lows, bases, window = refs[4:]
         me = lax.axis_index("ta") * tp_count + lax.axis_index("tp")
         for flip in range(2):
-            for index, mask in enumerate(offsets):
+            for index in range(2 * half_count):
                 late, slot = divmod(index, half_count)
+                mask = jnp.where(me % 2 == flip, offsets[0][index], offsets[1][index])
                 device = me ^ (flip ^ mask)
                 for part in range(2):
                     values[part, device] = sources[2 * flip + late][slot, part]
@@ -363,10 +364,11 @@
     stripe = green.shape[3]
     block_rows = green.shape[4]
     factor = 1.0 / math.sqrt(2 * block_rows)
-    mask, first_masks, second_masks = exchange_masks(2, tp_count)
+    mask, first_masks, second_masks = exchange_masks(tp_count)
 
     def exchanged(block, mask):
-        return lax.ppermute(block, ("ta", "tp"), [(i, i ^ mask) for i in range(count)])
+        masks = (mask, mask) if isinstance(mask, int) else mask
+        return lax.ppermute(block, ("ta", "tp"), [(i, i ^ masks[i % 2]) for i in range(count)])
 
     arriving = exchanged(green.reshape(-1, block_rows), mask).reshape(green.shape)
     first = jnp.stack([green[:, 0, 0], arriving[:, 0, 0]])
@@ -374,7 +376,7 @@
     high = lax.reduce_precision(second, 8, 7)
     second = jnp.stack([high, second - high], 1).astype(jnp.bfloat16)
     first_parts = second_parts = ()
-    for first_mask, second_mask in zip(first_masks, second_masks):
+    for first_mask, second_mask in zip(zip(*first_masks), second_masks):
         first_parts = [first, exchanged(first, first_mask)]
         first = jnp.concatenate(first_parts)
         if second_mask == tp_count:
@@ -385,7 +387,7 @@
             second = jnp.concatenate(second_parts)
     first_parts += [exchanged(part, 1) for part in first_parts]
     second_parts += [exchanged(part, 1) for part in second_parts]
-    first_masks = [mask] + first_masks
+    first_masks = [[mask] + each for each in first_masks]
     second_masks = [mask] + [later for later in second_masks if later != tp_count]
     early = first_stage(first_masks, tp_count, stripe, block_rows, factor)
     late = second_stage(second_masks, tp_count, stripe, block_rows, factor)

time: 29.9 us -> 29.9 us (level)
  starting transfers between devices: 12.8 us -> 11.6 us
  waiting for transfers between devices: 11.6 us -> 12.8 us
    ppermute x11, waiting for transfers between devices: 11.6 us -> 12.8 us  [exchanged(): lax.ppermute(block, ('ta', 'tp'), [(i, i ^ masks[i % 2]) for i in range(c...]
    ppermute x11, starting transfers between devices: 12.8 us -> 11.6 us  [exchanged(): lax.ppermute(block, ('ta', 'tp'), [(i, i ^ masks[i % 2]) for i in range(c...]
  transfers between devices with their start and end apart: 11 -> 11, of which waited for: 6 -> 7; matrix products, arithmetic and copies ran while one was open for 3% -> 3% of each run, Pallas kernels for 3% -> 3%
where the time goes in v8:
time: 29.9 us; the launch traced here: 29.7 us
  waiting for transfers between devices  12.8 us (43%)
  starting transfers between devices  11.6 us (39%)
  Pallas kernels  4.33 us (14%)
  local copies, waits for them, and re-layouts  0.82 us (3%)
    ppermute x11, waiting for transfers between devices, exchanged(): lax.ppermute(block, ('ta', 'tp'), [(i, i ^ masks[i % 2]) for i in range(c...  12.8 us
    ppermute x11, starting transfers between devices, exchanged(): lax.ppermute(block, ('ta', 'tp'), [(i, i ^ masks[i % 2]) for i in range(c...  11.6 us
    pallas_call x1, Pallas kernels, replicated(): return late(*second_parts, hamiltonian, interaction, *known)[:, :, None]  3.3 us
    pallas_call x1, Pallas kernels, replicated(): known = early(*first_parts, hamiltonian, interaction)  1.03 us
    another operation x2, local copies, waits for them, and re-layouts, replicated(): first = jnp.stack([green[:, 0, 0], arriving[:, 0, 0]])  0.8 us
  transfers between devices with their start and end apart: 11, of which 7 were waited for; matrix products, arithmetic and copies ran while one was open for 3% of the time, Pallas kernels for 3%

profile of v8, /device:TPU:0, one launch (start us, length us, event | category | flops | bytes accessed | tf_op | source)
XLA Modules:
  0.0 29.7 jit_solution(17159404065416059238)
XLA Ops:
  0.0 4.1 %collective-permute-start = (f32[64,256]{1,0:T(8,128)}, f32[64,256]{1,0:T(8,128)S(1)}, u32[]{:S(2)}, u32[]{:S(2)}) collective-permute-start(f32[64,256]{1,0:T(8,128)} %bitcast.28), channel_id=1, source_target_pairs={{0,8},{1,9},{2,10},{3,11},{4,12},{5,13},{6,14},{7,15},{8,0},{9,1},... | collective-permute-start | bytes 196616 | tf_op jit(solution)/shard_map/ppermute | solution.py:371
  4.1 0.8 %slice_bitcast_fusion.2 = (f32[1,2,16,256]{3,2,1,0:T(8,128)S(1)}, f32[1,1,2,16,256]{4,3,2,1,0:T(8,128)S(1)}) fusion(f32[2,2,1,16,256]{4,3,2,1,0:T(8,128)} %param.3), kind=kLoop, calls=%fused_computation.11 | loop fusion | bytes 131072 | tf_op jit(solution)/shard_map/stack;squeeze | solution.py:374
  4.9 3.1 %collective-permute-done = f32[64,256]{1,0:T(8,128)S(1)} collective-permute-done((f32[64,256]{1,0:T(8,128)}, f32[64,256]{1,0:T(8,128)S(1)}, u32[]{:S(2)}, u32[]{:S(2)}) %collective-permute-start) | collective-permute-done | bytes 65568 | tf_op jit(solution)/shard_map/ppermute | solution.py:371
  7.9 1.8 %collective-permute-start.6 = (f32[2,2,16,256]{3,2,1,0:T(8,128)S(1)}, f32[2,2,16,256]{3,2,1,0:T(8,128)S(1)}, u32[]{:S(2)}, u32[]{:S(2)}) collective-permute-start(f32[2,2,16,256]{3,2,1,0:T(8,128)S(1)} %pad_maximum_fusion.5), channel_id=1, source_target_pairs={{0,16},{1,3},{2,18},{3,1},{4,20},{5,7},{6,22},{7,5},{8,24},{9,11},... | collective-permute-start | bytes 196616 | tf_op jit(solution)/shard_map/ppermute | solution.py:371
  9.7 0.4 %collective-permute-start.1 = (bf16[2,2,16,256]{3,2,1,0:T(8,128)(2,1)S(1)}, bf16[2,2,16,256]{3,2,1,0:T(8,128)(2,1)S(1)}, u32[]{:S(2)}, u32[]{:S(2)}) collective-permute-start(bf16[2,2,16,256]{3,2,1,0:T(8,128)(2,1)S(1)} %bitcast.25), channel_id=1, source_target_pairs={{0,16},{1,17},{2,18},{3,19},{4,20},{5,21},{6,22},{7,23},{8,24},{9,... | collective-permute-start | bytes 98312 | tf_op jit(solution)/shard_map/ppermute | solution.py:371
  10.1 2.2 %collective-permute-done.6 = f32[2,2,16,256]{3,2,1,0:T(8,128)S(1)} collective-permute-done((f32[2,2,16,256]{3,2,1,0:T(8,128)S(1)}, f32[2,2,16,256]{3,2,1,0:T(8,128)S(1)}, u32[]{:S(2)}, u32[]{:S(2)}) %collective-permute-start.6) | collective-permute-done | bytes 65568 | tf_op jit(solution)/shard_map/ppermute | solution.py:371
  12.3 1.0 %collective-permute-start.7 = (f32[4,2,16,256]{3,2,1,0:T(8,128)S(1)}, f32[4,2,16,256]{3,2,1,0:T(8,128)S(1)}, u32[]{:S(2)}, u32[]{:S(2)}) collective-permute-start(f32[4,2,16,256]{3,2,1,0:T(8,128)S(1)} %pad_maximum_fusion.2), channel_id=1, source_target_pairs={{0,4},{1,5},{2,6},{3,7},{4,0},{5,1},{6,2},{7,3},{8,12},{9,13},{10,... | collective-permute-start | bytes 393224 | tf_op jit(solution)/shard_map/ppermute | solution.py:371
  13.3 0.4 %collective-permute-done.1 = bf16[2,2,16,256]{3,2,1,0:T(8,128)(2,1)S(1)} collective-permute-done((bf16[2,2,16,256]{3,2,1,0:T(8,128)(2,1)S(1)}, bf16[2,2,16,256]{3,2,1,0:T(8,128)(2,1)S(1)}, u32[]{:S(2)}, u32[]{:S(2)}) %collective-permute-start.1) | collective-permute-done | bytes 32800 | tf_op jit(solution)/shard_map/ppermute | solution.py:371
  13.7 1.6 %collective-permute-start.2 = (bf16[2,3,2,16,256]{4,3,2,1,0:T(8,128)(2,1)S(1)}, bf16[2,3,2,16,256]{4,3,2,1,0:T(8,128)(2,1)S(1)}, u32[]{:S(2)}, u32[]{:S(2)}) collective-permute-start(bf16[2,3,2,16,256]{4,3,2,1,0:T(8,128)(2,1)S(1)} %pad_maximum_fusion.3), channel_id=1, source_target_pairs={{0,2},{1,3},{2,0},{3,1},{4,6},{5,7},{6,4},{7,5},{8,10},{9,11},{10,... | collective-permute-start | bytes 294920 | tf_op jit(solution)/shard_map/ppermute | solution.py:371
  15.3 2.0 %collective-permute-done.7 = f32[4,2,16,256]{3,2,1,0:T(8,128)S(1)} collective-permute-done((f32[4,2,16,256]{3,2,1,0:T(8,128)S(1)}, f32[4,2,16,256]{3,2,1,0:T(8,128)S(1)}, u32[]{:S(2)}, u32[]{:S(2)}) %collective-permute-start.7) | collective-permute-done | bytes 131104 | tf_op jit(solution)/shard_map/ppermute | solution.py:371
  17.3 0.0 copy-start
  17.4 0.0 copy-start.1
  17.4 1.8 %collective-permute-start.8 = (f32[8,2,16,256]{3,2,1,0:T(8,128)S(1)}, f32[8,2,16,256]{3,2,1,0:T(8,128)S(1)}, u32[]{:S(2)}, u32[]{:S(2)}) collective-permute-start(f32[8,2,16,256]{3,2,1,0:T(8,128)S(1)} %pad_maximum_fusion.refs_0_), channel_id=1, source_target_pairs={{0,2},{1,17},{2,0},{3,19},{4,6},{5,21},{6,4},{7,23},{8,10},{9,25},... | collective-permute-start | bytes 786440 | tf_op jit(solution)/shard_map/ppermute | solution.py:371
  19.2 0.0 collective-permute-done.2
  19.2 0.5 %collective-permute-start.3 = (bf16[4,3,2,16,256]{4,3,2,1,0:T(8,128)(2,1)S(1)}, bf16[4,3,2,16,256]{4,3,2,1,0:T(8,128)(2,1)S(1)}, u32[]{:S(2)}, u32[]{:S(2)}) collective-permute-start(bf16[4,3,2,16,256]{4,3,2,1,0:T(8,128)(2,1)S(1)} %pad_maximum_fusion.1.refs_0_), channel_id=1, source_target_pairs={{0,4},{1,5},{2,6},{3,7},{4,0},{5,1},{6,2},{7,3},{8,12},{9,13},{10,... | collective-permute-start | bytes 589832 | tf_op jit(solution)/shard_map/ppermute | solution.py:371
  19.7 0.0 collective-permute-start.9
  19.7 4.1 %collective-permute-done.8.refs_1_ = f32[8,2,16,256]{3,2,1,0:T(8,128)S(1)} collective-permute-done((f32[8,2,16,256]{3,2,1,0:T(8,128)S(1)}, f32[8,2,16,256]{3,2,1,0:T(8,128)S(1)}, u32[]{:S(2)}, u32[]{:S(2)}) %collective-permute-start.8) | collective-permute-done | bytes 262176 | tf_op jit(solution)/shard_map/ppermute | solution.py:371
  23.8 0.0 collective-permute-start.10
  23.8 0.5 %collective-permute-start.4 = (bf16[4,3,2,16,256]{4,3,2,1,0:T(8,128)(2,1)S(1)}, bf16[4,3,2,16,256]{4,3,2,1,0:T(8,128)(2,1)S(1)}, u32[]{:S(2)}, u32[]{:S(2)}) collective-permute-start(bf16[4,3,2,16,256]{4,3,2,1,0:T(8,128)(2,1)S(1)} %pad_maximum_fusion.1.refs_0_), channel_id=1, source_target_pairs={{0,1},{1,0},{2,3},{3,2},{4,5},{5,4},{6,7},{7,6},{8,9},{9,8},{10,11... | collective-permute-start | bytes 589832 | tf_op jit(solution)/shard_map/ppermute | solution.py:371
  24.3 0.6 %collective-permute-done.3.refs_1_ = bf16[4,3,2,16,256]{4,3,2,1,0:T(8,128)(2,1)S(1)} collective-permute-done((bf16[4,3,2,16,256]{4,3,2,1,0:T(8,128)(2,1)S(1)}, bf16[4,3,2,16,256]{4,3,2,1,0:T(8,128)(2,1)S(1)}, u32[]{:S(2)}, u32[]{:S(2)}) %collective-permute-start.3) | collective-permute-done | bytes 196640 | tf_op jit(solution)/shard_map/ppermute | solution.py:371
  24.9 0.0 collective-permute-start.5
  24.9 0.0 collective-permute-done.9.refs_2_
  24.9 0.4 %collective-permute-done.10.refs_3_ = f32[8,2,16,256]{3,2,1,0:T(8,128)S(1)} collective-permute-done((f32[8,2,16,256]{3,2,1,0:T(8,128)S(1)}, f32[8,2,16,256]{3,2,1,0:T(8,128)S(1)}, u32[]{:S(2)}, u32[]{:S(2)}) %collective-permute-start.10) | collective-permute-done | bytes 262176 | tf_op jit(solution)/shard_map/ppermute | solution.py:371
  25.3 0.0 copy-done
  25.3 0.0 copy-done.1
  25.3 1.0 %first_stage.1 = (f32[2,32,16,256]{3,2,1,0:T(8,128)S(1)}, bf16[2,256,512]{2,1,0:T(8,128)(2,1)S(1)}, f32[2,2,256,256]{3,2,1,0:T(8,128)S(1)}, bf16[2,256,256]{2,1,0:T(8,128)(2,1)S(1)}) custom-call(f32[8,2,16,256]{3,2,1,0:T(8,128)S(1)} %pad_maximum_fusion.refs_0_, f32[8,2,16,256]{3,2,1,0:T(8,128)S(1)} %collective-permute-done.8.refs_1_, ...), custom_call_target="tpu_custom_call" | custom-call | tf_op jit(solution)/shard_map/first_stage/pallas_call | solution.py:394
  26.4 0.0 collective-permute-done.4.refs_2_
  26.4 0.0 collective-permute-done.5.refs_3_
  26.4 3.3 %second_stage.1 = f32[2,2,16,256]{3,2,1,0:T(8,128)} custom-call(bf16[4,3,2,16,256]{4,3,2,1,0:T(8,128)(2,1)S(1)} %pad_maximum_fusion.1.refs_0_, bf16[4,3,2,16,256]{4,3,2,1,0:T(8,128)(2,1)S(1)} %collective-permute-done.3.refs_1_, bf16[4,3,2,16,256]{4,3,2,1,0:T(8,128)(2,1)S(1)} %collective-permute-done.4.refs_2_, ...), custom_call_target="tpu_custom_call" | custom-call | tf_op jit(solution)/shard_map/second_stage/pallas_call | solution.py:395
  (7 shorter events, 0.1 us)
Async XLA Ops:
  0.0 7.9 %collective-permute-start = (f32[64,256]{1,0:T(8,128)}, f32[64,256]{1,0:T(8,128)S(1)}, u32[]{:S(2)}, u32[]{:S(2)}) collective-permute-start(f32[64,256]{1,0:T(8,128)} %bitcast.28), channel_id=1, source_target_pairs={{0,8},{1,9},{2,10},{3,11},{4,12},{5,13},{6,14},{7,15},{8,0},{9,1},... | collective-permute-start | bytes 196616 | tf_op jit(solution)/shard_map/ppermute | solution.py:371
  7.9 4.3 %collective-permute-start.6 = (f32[2,2,16,256]{3,2,1,0:T(8,128)S(1)}, f32[2,2,16,256]{3,2,1,0:T(8,128)S(1)}, u32[]{:S(2)}, u32[]{:S(2)}) collective-permute-start(f32[2,2,16,256]{3,2,1,0:T(8,128)S(1)} %pad_maximum_fusion.5), channel_id=1, source_target_pairs={{0,16},{1,3},{2,18},{3,1},{4,20},{5,7},{6,22},{7,5},{8,24},{9,11},... | collective-permute-start | bytes 196616 | tf_op jit(solution)/shard_map/ppermute | solution.py:371
  9.7 4.0 %collective-permute-start.1 = (bf16[2,2,16,256]{3,2,1,0:T(8,128)(2,1)S(1)}, bf16[2,2,16,256]{3,2,1,0:T(8,128)(2,1)S(1)}, u32[]{:S(2)}, u32[]{:S(2)}) collective-permute-start(bf16[2,2,16,256]{3,2,1,0:T(8,128)(2,1)S(1)} %bitcast.25), channel_id=1, source_target_pairs={{0,16},{1,17},{2,18},{3,19},{4,20},{5,21},{6,22},{7,23},{8,24},{9,... | collective-permute-start | bytes 98312 | tf_op jit(solution)/shard_map/ppermute | solution.py:371
  12.3 5.0 %collective-permute-start.7 = (f32[4,2,16,256]{3,2,1,0:T(8,128)S(1)}, f32[4,2,16,256]{3,2,1,0:T(8,128)S(1)}, u32[]{:S(2)}, u32[]{:S(2)}) collective-permute-start(f32[4,2,16,256]{3,2,1,0:T(8,128)S(1)} %pad_maximum_fusion.2), channel_id=1, source_target_pairs={{0,4},{1,5},{2,6},{3,7},{4,0},{5,1},{6,2},{7,3},{8,12},{9,13},{10,... | collective-permute-start | bytes 393224 | tf_op jit(solution)/shard_map/ppermute | solution.py:371
  13.7 5.5 %collective-permute-start.2 = (bf16[2,3,2,16,256]{4,3,2,1,0:T(8,128)(2,1)S(1)}, bf16[2,3,2,16,256]{4,3,2,1,0:T(8,128)(2,1)S(1)}, u32[]{:S(2)}, u32[]{:S(2)}) collective-permute-start(bf16[2,3,2,16,256]{4,3,2,1,0:T(8,128)(2,1)S(1)} %pad_maximum_fusion.3), channel_id=1, source_target_pairs={{0,2},{1,3},{2,0},{3,1},{4,6},{5,7},{6,4},{7,5},{8,10},{9,11},{10,... | collective-permute-start | bytes 294920 | tf_op jit(solution)/shard_map/ppermute | solution.py:371
  17.3 8.0 %copy-start = (f32[32,32]{1,0:T(8,128)S(1)}, f32[32,32]{1,0:T(8,128)}, u32[]{:S(2)}) copy-start(f32[32,32]{1,0:T(8,128)} %refs_4_.3) | copy-start | bytes 12292
  17.4 8.0 %copy-start.1 = (f32[32,32]{1,0:T(8,128)S(1)}, f32[32,32]{1,0:T(8,128)}, u32[]{:S(2)}) copy-start(f32[32,32]{1,0:T(8,128)} %refs_5_.3) | copy-start | bytes 12292
  17.4 6.4 %collective-permute-start.8 = (f32[8,2,16,256]{3,2,1,0:T(8,128)S(1)}, f32[8,2,16,256]{3,2,1,0:T(8,128)S(1)}, u32[]{:S(2)}, u32[]{:S(2)}) collective-permute-start(f32[8,2,16,256]{3,2,1,0:T(8,128)S(1)} %pad_maximum_fusion.refs_0_), channel_id=1, source_target_pairs={{0,2},{1,17},{2,0},{3,19},{4,6},{5,21},{6,4},{7,23},{8,10},{9,25},... | collective-permute-start | bytes 786440 | tf_op jit(solution)/shard_map/ppermute | solution.py:371
  19.2 5.7 %collective-permute-start.3 = (bf16[4,3,2,16,256]{4,3,2,1,0:T(8,128)(2,1)S(1)}, bf16[4,3,2,16,256]{4,3,2,1,0:T(8,128)(2,1)S(1)}, u32[]{:S(2)}, u32[]{:S(2)}) collective-permute-start(bf16[4,3,2,16,256]{4,3,2,1,0:T(8,128)(2,1)S(1)} %pad_maximum_fusion.1.refs_0_), channel_id=1, source_target_pairs={{0,4},{1,5},{2,6},{3,7},{4,0},{5,1},{6,2},{7,3},{8,12},{9,13},{10,... | collective-permute-start | bytes 589832 | tf_op jit(solution)/shard_map/ppermute | solution.py:371
  19.7 5.2 %collective-permute-start.9 = (f32[8,2,16,256]{3,2,1,0:T(8,128)S(1)}, f32[8,2,16,256]{3,2,1,0:T(8,128)S(1)}, u32[]{:S(2)}, u32[]{:S(2)}) collective-permute-start(f32[8,2,16,256]{3,2,1,0:T(8,128)S(1)} %pad_maximum_fusion.refs_0_), channel_id=1, source_target_pairs={{0,1},{1,0},{2,3},{3,2},{4,5},{5,4},{6,7},{7,6},{8,9},{9,8},{10,11... | collective-permute-start | bytes 786440 | tf_op jit(solution)/shard_map/ppermute | solution.py:371
  23.8 1.5 %collective-permute-start.10 = (f32[8,2,16,256]{3,2,1,0:T(8,128)S(1)}, f32[8,2,16,256]{3,2,1,0:T(8,128)S(1)}, u32[]{:S(2)}, u32[]{:S(2)}) collective-permute-start(f32[8,2,16,256]{3,2,1,0:T(8,128)S(1)} %collective-permute-done.8.refs_1_), channel_id=1, source_target_pairs={{0,1},{1,0},{2,3},{3,2},{4,5},{5,4},{6,7},{7,6},{8,9},{9,8},{10,11... | collective-permute-start | bytes 786440 | tf_op jit(solution)/shard_map/ppermute | solution.py:371
  23.8 2.6 %collective-permute-start.4 = (bf16[4,3,2,16,256]{4,3,2,1,0:T(8,128)(2,1)S(1)}, bf16[4,3,2,16,256]{4,3,2,1,0:T(8,128)(2,1)S(1)}, u32[]{:S(2)}, u32[]{:S(2)}) collective-permute-start(bf16[4,3,2,16,256]{4,3,2,1,0:T(8,128)(2,1)S(1)} %pad_maximum_fusion.1.refs_0_), channel_id=1, source_target_pairs={{0,1},{1,0},{2,3},{3,2},{4,5},{5,4},{6,7},{7,6},{8,9},{9,8},{10,11... | collective-permute-start | bytes 589832 | tf_op jit(solution)/shard_map/ppermute | solution.py:371
  24.9 1.4 %collective-permute-start.5 = (bf16[4,3,2,16,256]{4,3,2,1,0:T(8,128)(2,1)S(1)}, bf16[4,3,2,16,256]{4,3,2,1,0:T(8,128)(2,1)S(1)}, u32[]{:S(2)}, u32[]{:S(2)}) collective-permute-start(bf16[4,3,2,16,256]{4,3,2,1,0:T(8,128)(2,1)S(1)} %collective-permute-done.3.refs_1_), channel_id=1, source_target_pairs={{0,1},{1,0},{2,3},{3,2},{4,5},{5,4},{6,7},{7,6},{8,9},{9,8},{10,11... | collective-permute-start | bytes 589832 | tf_op jit(solution)/shard_map/ppermute | solution.py:371

commit v9 on v8

--- a/solution.py
+++ b/solution.py
@@ -64,7 +64,7 @@
     block_width = math.gcd(block_rows, 128)
     blocked = jnp.kron(jnp.eye(block_width // NO, dtype=jnp.float32), hamiltonian.T)
     zero_half = jnp.zeros((), jnp.bfloat16)
-    for iteration in range(ITERS):
+    for _ in range(ITERS):
         rounded = current.astype(jnp.bfloat16)
         outgoing = rounded.reshape(2, groups, stripe, tp_count, stripe)
         previous = shifted(rounded, "ta", 1)
@@ -188,65 +188,133 @@
     return weights, halves(jnp.where(same_time, table, 0.0))
 
 
-def one_body(values, high, low, table):
-    turned = [
-        bf16_dot(high[part], table[0])
-        + bf16_dot(low[part], table[0])
-        + bf16_dot(high[part], table[1])
+def turned_by(table, high, low=None):
+    result = bf16_dot(high, table[0]) + bf16_dot(high, table[1])
+    return result if low is None else result + bf16_dot(low, table[0])
+
+
+def started(values, turned):
+    return values[0] + 0.5 * turned[1], values[1] - 0.5 * turned[0]
+
+
+def rows_of(pieces):
+    return pieces.reshape(pieces.shape[0] * pieces.shape[1], pieces.shape[2])
+
+
+def whole(source, block):
+    tp_count, stripe, block_rows = source.shape[1] // 2, source.shape[2], source.shape[3]
+    return [
+        source[part, block * tp_count : (block + 1) * tp_count].reshape(
+            tp_count * stripe, block_rows
+        )
         for part in range(2)
     ]
-    return values[0] + 0.5 * turned[1], values[1] - 0.5 * turned[0]
+
+
+def put(device, targets, results, index, stripe):
+    for target, result in zip(targets, results):
+        for part in range(2):
+            target[part, device] = result[part][index * stripe : (index + 1) * stripe]
+
+
+def take_first(sources, late, me, offsets, stripe, table, targets):
+    count = len(offsets[0]) // 2
+    for flip in range(2):
+        values = [rows_of(sources[flip][:, part]) for part in range(2)]
+        split = [halves(part) for part in values]
+        base = started(values, [turned_by(table, high, low) for high, low in split])
+        highs = [high for high, _ in split]
+        for index in range(count):
+            place = late * count + index
+            mask = jnp.where(me % 2 == flip, offsets[0][place], offsets[1][place])
+            put(me ^ (flip ^ mask), targets, (values, highs, base), index, stripe)
+
+
+def take_second(sources, late, me, offsets, tp_count, stripe, table, targets):
+    count = len(offsets) // 2
+    for flip in range(2):
+        for plane in range(2):
+            highs = [rows_of(sources[flip][:, plane, part]) for part in range(2)]
+            values = [high.astype(jnp.float32) for high in highs]
+            if plane == 0:
+                lows = [rows_of(sources[flip][:, 2, part]) for part in range(2)]
+                values = [values[part] + lows[part].astype(jnp.float32) for part in range(2)]
+                turned = [turned_by(table, highs[part], lows[part]) for part in range(2)]
+            else:
+                turned = [turned_by(table, high) for high in highs]
+            base = started(values, turned)
+            for index in range(count):
+                device = me ^ (flip ^ offsets[late * count + index] ^ (plane * tp_count))
+                put(device, targets, (values, highs, base), index, stripe)
+
+
+def own_place(tp_count):
+    return lax.axis_index("ta") * tp_count + lax.axis_index("tp")
+
+
+def kept_shapes(tp_count, stripe, block_rows):
+    pieces = (2, 2 * tp_count, stripe, block_rows)
+    return [jax.ShapeDtypeStruct(pieces, each) for each in (jnp.float32, jnp.bfloat16, jnp.float32)]
+
+
+def in_vmem(count):
+    return [pl.BlockSpec(memory_space=pltpu.VMEM)] * count
+
+
+def early_stage(first_masks, second_masks, tp_count, stripe, block_rows, factor):
+    first_offsets = [offsets_of(each) for each in first_masks]
+    second_offsets = offsets_of(second_masks)
+
+    def kernel(*refs):
+        hamiltonian, interaction, weights_out, table_out = refs[4:6] + refs[12:]
+        me = own_place(tp_count)
+        weights, table = tables_of(hamiltonian, interaction, block_rows)
+        weights_out[...] = weights
+        table_out[0] = table[0]
+        table_out[1] = table[1]
+        take_first(refs[:2], 0, me, first_offsets, stripe, table, refs[6:9])
+        take_second(refs[2:4], 0, me, second_offsets, tp_count, stripe, table, refs[9:12])
+
+    shapes = kept_shapes(tp_count, stripe, block_rows)
+    tables = [
+        jax.ShapeDtypeStruct((NO, block_rows), jnp.float32),
+        jax.ShapeDtypeStruct((2, block_rows, block_rows), jnp.bfloat16),
+    ]
+    return pl.pallas_call(
+        kernel,
+        out_shape=shapes + shapes + tables,
+        in_specs=in_vmem(6),
+        out_specs=in_vmem(8),
+        compiler_params=pltpu.CompilerParams(vmem_limit_bytes=16 << 20),
+        name="early_stage",
+    )
 
 
 def first_stage(masks, tp_count, stripe, block_rows, factor):
     offsets = [offsets_of(each) for each in masks]
-    half_count = len(offsets[0]) // 2
+    scale = 0.5 * factor
 
     def kernel(*refs):
-        sources = refs[:4]
-        hamiltonian, interaction, values, lows, bases, window = refs[4:]
-        me = lax.axis_index("ta") * tp_count + lax.axis_index("tp")
-        for flip in range(2):
-            for index in range(2 * half_count):
-                late, slot = divmod(index, half_count)
-                mask = jnp.where(me % 2 == flip, offsets[0][index], offsets[1][index])
-                device = me ^ (flip ^ mask)
-                for part in range(2):
-                    values[part, device] = sources[2 * flip + late][slot, part]
-        weights, table = tables_of(hamiltonian, interaction, block_rows)
-        for block in range(2):
-            current = [
-                values[part, block * tp_count : (block + 1) * tp_count].reshape(
-                    block_rows, block_rows
-                )
-                for part in range(2)
-            ]
-            split = [halves(part) for part in current]
-            high = [part[0] for part in split]
-            base = one_body(current, high, [part[1] for part in split], table)
-            for part in range(2):
-                lows[part, :, block * block_rows : (block + 1) * block_rows] = high[part]
-            if block == 0:
-                made = window_of(current, mirrored(high), weights, 0)
-                memory = products(high, made)
-                scale = 0.5 * factor
-                base = (base[0] + scale * memory[1], base[1] - scale * memory[0])
-                window[0] = made[0]
-                window[1] = made[1]
-            bases[0, block] = base[0]
-            bases[1, block] = base[1]
-
-    block = jax.ShapeDtypeStruct((2, 2, block_rows, block_rows), jnp.float32)
+        weights, table = refs[2], (refs[3][0], refs[3][1])
+        targets, window = refs[7:10], refs[10]
+        take_first(refs[:2], 1, own_place(tp_count), offsets, stripe, table, targets)
+        values, highs, bases = targets
+        high = whole(highs, 0)
+        made = window_of(whole(values, 0), mirrored(high), weights[...], 0)
+        memory = products(high, made)
+        window[0] = made[0]
+        window[1] = made[1]
+        half = (tp_count, stripe, block_rows)
+        bases[0, :tp_count] = bases[0, :tp_count] + scale * memory[1].reshape(half)
+        bases[1, :tp_count] = bases[1, :tp_count] - scale * memory[0].reshape(half)
+
+    square = jax.ShapeDtypeStruct((2, block_rows, block_rows), jnp.bfloat16)
     return pl.pallas_call(
         kernel,
-        out_shape=[
-            jax.ShapeDtypeStruct((2, 2 * tp_count, stripe, block_rows), jnp.float32),
-            jax.ShapeDtypeStruct((2, block_rows, 2 * block_rows), jnp.bfloat16),
-            block,
-            jax.ShapeDtypeStruct((2, block_rows, block_rows), jnp.bfloat16),
-        ],
-        in_specs=[pl.BlockSpec(memory_space=pltpu.VMEM)] * 6,
-        out_specs=[pl.BlockSpec(memory_space=pltpu.VMEM)] * 4,
+        out_shape=kept_shapes(tp_count, stripe, block_rows) + [square],
+        in_specs=in_vmem(7),
+        out_specs=in_vmem(4),
+        input_output_aliases={4: 0, 5: 1, 6: 2},
         compiler_params=pltpu.CompilerParams(vmem_limit_bytes=16 << 20),
         name="first_stage",
     )
@@ -254,49 +322,20 @@
 
 def second_stage(masks, tp_count, stripe, block_rows, factor):
     offsets = offsets_of(masks)
-    half_count = len(offsets) // 2
     order_size = 2 * block_rows
     scale = 0.5 * factor
 
     def kernel(*refs):
-        sources = refs[:4]
-        hamiltonian, interaction, values, lows, bases, window = refs[4:10]
-        out, highs, rests, nexts, low_next = refs[10:]
+        weights, table = refs[2][...], (refs[3][0], refs[3][1])
+        values, lows, bases, window = refs[4:8]
+        out, targets, nexts, low_next = refs[11], refs[12:15], refs[15], refs[16]
         ta_place = lax.axis_index("ta")
         tp_place = lax.axis_index("tp")
-        me = ta_place * tp_count + tp_place
-        blank = jnp.zeros((stripe, block_rows), jnp.bfloat16)
-        for flip in range(2):
-            for index, mask in enumerate(offsets):
-                late, slot = divmod(index, half_count)
-                device = me ^ (flip ^ mask)
-                other = device ^ tp_count
-                source = sources[2 * flip + late]
-                for part in range(2):
-                    highs[part, device] = source[slot, 0, part]
-                    highs[part, other] = source[slot, 1, part]
-                    rests[part, device] = source[slot, 2, part]
-                    rests[part, other] = blank
-        weights, table = tables_of(hamiltonian, interaction, block_rows)
-
-        def whole(source, block):
-            return [
-                source[part, block * tp_count : (block + 1) * tp_count].reshape(
-                    block_rows, block_rows
-                )
-                for part in range(2)
-            ]
-
-        high = [whole(highs, block) for block in range(2)]
-        rest = [whole(rests, block) for block in range(2)]
-        full = [
-            [
-                high[block][part].astype(jnp.float32) + rest[block][part].astype(jnp.float32)
-                for part in range(2)
-            ]
-            for block in range(2)
-        ]
-        base = [one_body(full[block], high[block], rest[block], table) for block in range(2)]
+        take_second(
+            refs[:2], 1, own_place(tp_count), offsets, tp_count, stripe, table, targets
+        )
+        second_values, second_highs, second_bases = targets
+        high = [whole(second_highs, block) for block in range(2)]
 
         def stored(block, group, real, imag):
             for part, result in ((0, real), (1, imag)):
@@ -305,19 +344,19 @@
                     result.astype(jnp.bfloat16)
                 )
 
-        stored(0, 0, bases[0, 0], bases[1, 0])
+        stored(0, 0, *whole(bases, 0))
         memory = products(high[0], (window[0], window[1]))
-        stored(0, 1, base[0][0] + scale * memory[1], base[0][1] - scale * memory[0])
+        base = whole(second_bases, 0)
+        stored(0, 1, base[0] + scale * memory[1], base[1] - scale * memory[0])
         later = [
             window_of(whole(values, 1), mirrored(high[0]), weights, block_rows // NO),
-            window_of(full[1], mirrored(high[1]), weights, 0),
+            window_of(whole(second_values, 1), mirrored(high[1]), weights, 0),
         ]
-        rows = [[lows[part, :, :block_rows] for part in range(2)]]
-        rows.append([lows[part, :, block_rows:] for part in range(2)])
+        rows = [whole(lows, block) for block in range(2)]
         early_memory = [products(rows[0], later[0]), products(high[0], later[0])]
         late_memory = [products(rows[1], later[1]), products(high[1], later[1])]
         for group in range(2):
-            start = (bases[0, 1], bases[1, 1]) if group == 0 else base[1]
+            start = whole(bases if group == 0 else second_bases, 1)
             real = early_memory[group][0] + late_memory[group][0]
             imag = early_memory[group][1] + late_memory[group][1]
             stored(1, group, start[0] + scale * imag, start[1] - scale * real)
@@ -335,22 +374,20 @@
             for part in range(2)
         ]
         memory = products(own_rounded, last)
-        split = [halves(part) for part in own]
-        real, imag = one_body(own, [part[0] for part in split], [part[1] for part in split], table)
+        real, imag = started(own, [turned_by(table, *halves(part)) for part in own])
         shape = (2, stripe, block_rows)
         out[0] = (real + scale * memory[1]).reshape(shape)
         out[1] = (imag - scale * memory[0]).reshape(shape)
 
-    square = (2, 2, block_rows, block_rows)
     return pl.pallas_call(
         kernel,
-        out_shape=jax.ShapeDtypeStruct((2, 2, stripe, block_rows), jnp.float32),
-        in_specs=[pl.BlockSpec(memory_space=pltpu.VMEM)] * 10,
-        out_specs=pl.BlockSpec(memory_space=pltpu.VMEM),
+        out_shape=[jax.ShapeDtypeStruct((2, 2, stripe, block_rows), jnp.float32)]
+        + kept_shapes(tp_count, stripe, block_rows),
+        in_specs=in_vmem(11),
+        out_specs=in_vmem(4),
+        input_output_aliases={8: 1, 9: 2, 10: 3},
         scratch_shapes=[
-            pltpu.VMEM((2, 2 * tp_count, stripe, block_rows), jnp.bfloat16),
-            pltpu.VMEM((2, 2 * tp_count, stripe, block_rows), jnp.bfloat16),
-            pltpu.VMEM((2,) + square, jnp.float32),
+            pltpu.VMEM((2, 2, 2, block_rows, block_rows), jnp.float32),
             pltpu.VMEM((2, 2, block_rows, order_size), jnp.bfloat16),
         ],
         compiler_params=pltpu.CompilerParams(vmem_limit_bytes=24 << 20),
@@ -389,10 +426,15 @@
     second_parts += [exchanged(part, 1) for part in second_parts]
     first_masks = [[mask] + each for each in first_masks]
     second_masks = [mask] + [later for later in second_masks if later != tp_count]
-    early = first_stage(first_masks, tp_count, stripe, block_rows, factor)
-    late = second_stage(second_masks, tp_count, stripe, block_rows, factor)
-    known = early(*first_parts, hamiltonian, interaction)
-    return late(*second_parts, hamiltonian, interaction, *known)[:, :, None]
+    sizes = (tp_count, stripe, block_rows, factor)
+    *kept, weights, table = early_stage(first_masks, second_masks, *sizes)(
+        *first_parts[::2], *second_parts[::2], hamiltonian, interaction
+    )
+    known = first_stage(first_masks, *sizes)(*first_parts[1::2], weights, table, *kept[:3])
+    result = second_stage(second_masks, *sizes)(
+        *second_parts[1::2], weights, table, *known, *kept[3:]
+    )
+    return result[0][:, :, None]
 
 
 def solution(mesh):

time: 29.9 us -> 30.6 us (1.023)
  Pallas kernels: 4.33 us -> 4.74 us
    pallas_call x2 -> x3, Pallas kernels: 4.33 us -> 4.74 us  [the longest x1 3.02 us: replicated(): second_stage(second_masks, *sizes)]
  transfers between devices with their start and end apart: 11 -> 11, of which waited for: 7 -> 7; matrix products, arithmetic and copies ran while one was open for 3% -> 3% of each run, Pallas kernels for 3% -> 6%
where the time goes in v9:
time: 30.6 us; the launch traced here: 30.4 us
  waiting for transfers between devices  13.1 us (43%)
  starting transfers between devices  11.6 us (38%)
  Pallas kernels  4.74 us (15%)
  local copies, waits for them, and re-layouts  0.82 us (3%)
    ppermute x11, waiting for transfers between devices, exchanged(): lax.ppermute(block, ('ta', 'tp'), [(i, i ^ masks[i % 2]) for i in range(c...  13.1 us
    ppermute x11, starting transfers between devices, exchanged(): lax.ppermute(block, ('ta', 'tp'), [(i, i ^ masks[i % 2]) for i in range(c...  11.6 us
    pallas_call x1, Pallas kernels, replicated(): second_stage(second_masks, *sizes)  3.02 us
    pallas_call x1, Pallas kernels, replicated(): early_stage(first_masks, second_masks, *sizes)  1.03 us
    another operation x2, local copies, waits for them, and re-layouts, replicated(): first = jnp.stack([green[:, 0, 0], arriving[:, 0, 0]])  0.8 us
    pallas_call x1, Pallas kernels, replicated(): first_stage(first_masks, *sizes)  0.69 us
  transfers between devices with their start and end apart: 11, of which 7 were waited for; matrix products, arithmetic and copies ran while one was open for 3% of the time, Pallas kernels for 6%

profile of v9, /device:TPU:0, one launch (start us, length us, event | category | flops | bytes accessed | tf_op | source)
XLA Modules:
  0.0 30.4 jit_solution(15021343186461979014)
XLA Ops:
  0.0 4.1 %collective-permute-start = (f32[64,256]{1,0:T(8,128)}, f32[64,256]{1,0:T(8,128)S(1)}, u32[]{:S(2)}, u32[]{:S(2)}) collective-permute-start(f32[64,256]{1,0:T(8,128)} %bitcast.28), channel_id=1, source_target_pairs={{0,8},{1,9},{2,10},{3,11},{4,12},{5,13},{6,14},{7,15},{8,0},{9,1},... | collective-permute-start | bytes 196616 | tf_op jit(solution)/shard_map/ppermute | solution.py:408
  4.1 0.8 %slice_bitcast_fusion.2 = (f32[1,2,16,256]{3,2,1,0:T(8,128)S(1)}, f32[1,1,2,16,256]{4,3,2,1,0:T(8,128)S(1)}) fusion(f32[2,2,1,16,256]{4,3,2,1,0:T(8,128)} %param.3), kind=kLoop, calls=%fused_computation.11 | loop fusion | bytes 131072 | tf_op jit(solution)/shard_map/stack;squeeze | solution.py:411
  4.9 3.1 %collective-permute-done = f32[64,256]{1,0:T(8,128)S(1)} collective-permute-done((f32[64,256]{1,0:T(8,128)}, f32[64,256]{1,0:T(8,128)S(1)}, u32[]{:S(2)}, u32[]{:S(2)}) %collective-permute-start) | collective-permute-done | bytes 65568 | tf_op jit(solution)/shard_map/ppermute | solution.py:408
  7.9 1.8 %collective-permute-start.5 = (f32[2,2,16,256]{3,2,1,0:T(8,128)S(1)}, f32[2,2,16,256]{3,2,1,0:T(8,128)S(1)}, u32[]{:S(2)}, u32[]{:S(2)}) collective-permute-start(f32[2,2,16,256]{3,2,1,0:T(8,128)S(1)} %pad_maximum_fusion.5), channel_id=1, source_target_pairs={{0,16},{1,3},{2,18},{3,1},{4,20},{5,7},{6,22},{7,5},{8,24},{9,11},... | collective-permute-start | bytes 196616 | tf_op jit(solution)/shard_map/ppermute | solution.py:408
  9.7 0.4 %collective-permute-start.1 = (bf16[2,2,16,256]{3,2,1,0:T(8,128)(2,1)S(1)}, bf16[2,2,16,256]{3,2,1,0:T(8,128)(2,1)S(1)}, u32[]{:S(2)}, u32[]{:S(2)}) collective-permute-start(bf16[2,2,16,256]{3,2,1,0:T(8,128)(2,1)S(1)} %bitcast.25), channel_id=1, source_target_pairs={{0,16},{1,17},{2,18},{3,19},{4,20},{5,21},{6,22},{7,23},{8,24},{9,... | collective-permute-start | bytes 98312 | tf_op jit(solution)/shard_map/ppermute | solution.py:408
  10.1 2.2 %collective-permute-done.5 = f32[2,2,16,256]{3,2,1,0:T(8,128)S(1)} collective-permute-done((f32[2,2,16,256]{3,2,1,0:T(8,128)S(1)}, f32[2,2,16,256]{3,2,1,0:T(8,128)S(1)}, u32[]{:S(2)}, u32[]{:S(2)}) %collective-permute-start.5) | collective-permute-done | bytes 65568 | tf_op jit(solution)/shard_map/ppermute | solution.py:408
  12.3 1.0 %collective-permute-start.6 = (f32[4,2,16,256]{3,2,1,0:T(8,128)S(1)}, f32[4,2,16,256]{3,2,1,0:T(8,128)S(1)}, u32[]{:S(2)}, u32[]{:S(2)}) collective-permute-start(f32[4,2,16,256]{3,2,1,0:T(8,128)S(1)} %pad_maximum_fusion.2), channel_id=1, source_target_pairs={{0,4},{1,5},{2,6},{3,7},{4,0},{5,1},{6,2},{7,3},{8,12},{9,13},{10,... | collective-permute-start | bytes 393224 | tf_op jit(solution)/shard_map/ppermute | solution.py:408
  13.3 0.4 %collective-permute-done.1 = bf16[2,2,16,256]{3,2,1,0:T(8,128)(2,1)S(1)} collective-permute-done((bf16[2,2,16,256]{3,2,1,0:T(8,128)(2,1)S(1)}, bf16[2,2,16,256]{3,2,1,0:T(8,128)(2,1)S(1)}, u32[]{:S(2)}, u32[]{:S(2)}) %collective-permute-start.1) | collective-permute-done | bytes 32800 | tf_op jit(solution)/shard_map/ppermute | solution.py:408
  13.7 1.6 %collective-permute-start.2 = (bf16[2,3,2,16,256]{4,3,2,1,0:T(8,128)(2,1)S(1)}, bf16[2,3,2,16,256]{4,3,2,1,0:T(8,128)(2,1)S(1)}, u32[]{:S(2)}, u32[]{:S(2)}) collective-permute-start(bf16[2,3,2,16,256]{4,3,2,1,0:T(8,128)(2,1)S(1)} %pad_maximum_fusion.3), channel_id=1, source_target_pairs={{0,2},{1,3},{2,0},{3,1},{4,6},{5,7},{6,4},{7,5},{8,10},{9,11},{10,... | collective-permute-start | bytes 294920 | tf_op jit(solution)/shard_map/ppermute | solution.py:408
  15.3 2.0 %collective-permute-done.6 = f32[4,2,16,256]{3,2,1,0:T(8,128)S(1)} collective-permute-done((f32[4,2,16,256]{3,2,1,0:T(8,128)S(1)}, f32[4,2,16,256]{3,2,1,0:T(8,128)S(1)}, u32[]{:S(2)}, u32[]{:S(2)}) %collective-permute-start.6) | collective-permute-done | bytes 131104 | tf_op jit(solution)/shard_map/ppermute | solution.py:408
  17.3 0.0 copy-start
  17.4 0.0 copy-start.1
  17.4 1.8 %collective-permute-start.9 = (f32[8,2,16,256]{3,2,1,0:T(8,128)S(1)}, f32[8,2,16,256]{3,2,1,0:T(8,128)S(1)}, u32[]{:S(2)}, u32[]{:S(2)}) collective-permute-start(f32[8,2,16,256]{3,2,1,0:T(8,128)S(1)} %pad_maximum_fusion.refs_0_), channel_id=1, source_target_pairs={{0,2},{1,17},{2,0},{3,19},{4,6},{5,21},{6,4},{7,23},{8,10},{9,25},... | collective-permute-start | bytes 786440 | tf_op jit(solution)/shard_map/ppermute | solution.py:408
  19.2 0.0 collective-permute-done.2
  19.2 0.5 %collective-permute-start.3 = (bf16[4,3,2,16,256]{4,3,2,1,0:T(8,128)(2,1)S(1)}, bf16[4,3,2,16,256]{4,3,2,1,0:T(8,128)(2,1)S(1)}, u32[]{:S(2)}, u32[]{:S(2)}) collective-permute-start(bf16[4,3,2,16,256]{4,3,2,1,0:T(8,128)(2,1)S(1)} %pad_maximum_fusion.1.refs_2_), channel_id=1, source_target_pairs={{0,4},{1,5},{2,6},{3,7},{4,0},{5,1},{6,2},{7,3},{8,12},{9,13},{10,... | collective-permute-start | bytes 589832 | tf_op jit(solution)/shard_map/ppermute | solution.py:408
  19.7 0.0 collective-permute-start.7
  19.7 4.1 %collective-permute-done.9.refs_0_ = f32[8,2,16,256]{3,2,1,0:T(8,128)S(1)} collective-permute-done((f32[8,2,16,256]{3,2,1,0:T(8,128)S(1)}, f32[8,2,16,256]{3,2,1,0:T(8,128)S(1)}, u32[]{:S(2)}, u32[]{:S(2)}) %collective-permute-start.9) | collective-permute-done | bytes 262176 | tf_op jit(solution)/shard_map/ppermute | solution.py:408
  23.8 0.0 collective-permute-start.10
  23.8 0.5 %collective-permute-start.8 = (bf16[4,3,2,16,256]{4,3,2,1,0:T(8,128)(2,1)S(1)}, bf16[4,3,2,16,256]{4,3,2,1,0:T(8,128)(2,1)S(1)}, u32[]{:S(2)}, u32[]{:S(2)}) collective-permute-start(bf16[4,3,2,16,256]{4,3,2,1,0:T(8,128)(2,1)S(1)} %pad_maximum_fusion.1.refs_2_), channel_id=1, source_target_pairs={{0,1},{1,0},{2,3},{3,2},{4,5},{5,4},{6,7},{7,6},{8,9},{9,8},{10,11... | collective-permute-start | bytes 589832 | tf_op jit(solution)/shard_map/ppermute | solution.py:408
  24.3 0.6 %collective-permute-done.3.refs_0_ = bf16[4,3,2,16,256]{4,3,2,1,0:T(8,128)(2,1)S(1)} collective-permute-done((bf16[4,3,2,16,256]{4,3,2,1,0:T(8,128)(2,1)S(1)}, bf16[4,3,2,16,256]{4,3,2,1,0:T(8,128)(2,1)S(1)}, u32[]{:S(2)}, u32[]{:S(2)}) %collective-permute-start.3) | collective-permute-done | bytes 196640 | tf_op jit(solution)/shard_map/ppermute | solution.py:408
  24.9 0.0 collective-permute-start.4
  24.9 0.7 %collective-permute-done.8.refs_3_ = bf16[4,3,2,16,256]{4,3,2,1,0:T(8,128)(2,1)S(1)} collective-permute-done((bf16[4,3,2,16,256]{4,3,2,1,0:T(8,128)(2,1)S(1)}, bf16[4,3,2,16,256]{4,3,2,1,0:T(8,128)(2,1)S(1)}, u32[]{:S(2)}, u32[]{:S(2)}) %collective-permute-start.8) | collective-permute-done | bytes 196640 | tf_op jit(solution)/shard_map/ppermute | solution.py:408
  25.6 0.0 collective-permute-done.7.refs_1_
  25.6 0.0 copy-done
  25.6 0.0 copy-done.1
  25.6 1.0 %early_stage.1 = (f32[2,32,16,256]{3,2,1,0:T(8,128)S(1)}, bf16[2,32,16,256]{3,2,1,0:T(8,128)(2,1)S(1)}, f32[2,32,16,256]{3,2,1,0:T(8,128)S(1)}, f32[2,32,16,256]...) custom-call(f32[8,2,16,256]{3,2,1,0:T(8,128)S(1)} %pad_maximum_fusio, ...), custom_call_target="tpu_custom_call" | custom-call | tf_op jit(solution)/shard_map/early_stage/pallas_call | solution.py:430
  26.7 0.0 collective-permute-done.10.refs_1_
  26.7 0.7 %first_stage.1 = (f32[2,32,16,256]{3,2,1,0:T(8,128)S(1)}, bf16[2,32,16,256]{3,2,1,0:T(8,128)(2,1)S(1)}, f32[2,32,16,256]{3,2,1,0:T(8,128)S(1)}, bf16[2,256,256]{2,1,0:T(8,128)(2,1)S(1)}) custom-call(f32[8,2,16,256]{3,2,1,0:T(8,128)S(1)} %collective-permute-done.9.refs_0_, ...), custom_call_target="tpu_custom_call", output_to_operand_aliasing={{0}: (4, {}), {1}: (5, {}), {2}: (6, {})} | custom-call | tf_op jit(solution)/shard_map/first_stage/pallas_call | solution.py:433
  27.4 0.0 collective-permute-done.4.refs_1_
  27.4 3.0 %second_stage.1 = (f32[2,2,16,256]{3,2,1,0:T(8,128)}, f32[2,32,16,256]{3,2,1,0:T(8,128)S(1)}, bf16[2,32,16,256]{3,2,1,0:T(8,128)(2,1)S(1)}, f32[2,32,16,256]{3,2,1,0:T(8,128)S(1)}) custom-call(bf16[4,3,2,16,256]{4,3,2,1,0:T(8,128)(2,1)S(1)} %collective-permute-done.3.refs_0_, ...), custom_call_target="tpu_custom_call", output_to_operand_aliasing={{1}: (8, {}), {2}: (9, {}), {3}: (10, {})} | custom-call | tf_op jit(solution)/shard_map/second_stage/pallas_call | solution.py:434
  (7 shorter events, 0.1 us)
Async XLA Ops:
  0.0 7.9 %collective-permute-start = (f32[64,256]{1,0:T(8,128)}, f32[64,256]{1,0:T(8,128)S(1)}, u32[]{:S(2)}, u32[]{:S(2)}) collective-permute-start(f32[64,256]{1,0:T(8,128)} %bitcast.28), channel_id=1, source_target_pairs={{0,8},{1,9},{2,10},{3,11},{4,12},{5,13},{6,14},{7,15},{8,0},{9,1},... | collective-permute-start | bytes 196616 | tf_op jit(solution)/shard_map/ppermute | solution.py:408
  7.9 4.3 %collective-permute-start.5 = (f32[2,2,16,256]{3,2,1,0:T(8,128)S(1)}, f32[2,2,16,256]{3,2,1,0:T(8,128)S(1)}, u32[]{:S(2)}, u32[]{:S(2)}) collective-permute-start(f32[2,2,16,256]{3,2,1,0:T(8,128)S(1)} %pad_maximum_fusion.5), channel_id=1, source_target_pairs={{0,16},{1,3},{2,18},{3,1},{4,20},{5,7},{6,22},{7,5},{8,24},{9,11},... | collective-permute-start | bytes 196616 | tf_op jit(solution)/shard_map/ppermute | solution.py:408
  9.7 4.0 %collective-permute-start.1 = (bf16[2,2,16,256]{3,2,1,0:T(8,128)(2,1)S(1)}, bf16[2,2,16,256]{3,2,1,0:T(8,128)(2,1)S(1)}, u32[]{:S(2)}, u32[]{:S(2)}) collective-permute-start(bf16[2,2,16,256]{3,2,1,0:T(8,128)(2,1)S(1)} %bitcast.25), channel_id=1, source_target_pairs={{0,16},{1,17},{2,18},{3,19},{4,20},{5,21},{6,22},{7,23},{8,24},{9,... | collective-permute-start | bytes 98312 | tf_op jit(solution)/shard_map/ppermute | solution.py:408
  12.3 5.0 %collective-permute-start.6 = (f32[4,2,16,256]{3,2,1,0:T(8,128)S(1)}, f32[4,2,16,256]{3,2,1,0:T(8,128)S(1)}, u32[]{:S(2)}, u32[]{:S(2)}) collective-permute-start(f32[4,2,16,256]{3,2,1,0:T(8,128)S(1)} %pad_maximum_fusion.2), channel_id=1, source_target_pairs={{0,4},{1,5},{2,6},{3,7},{4,0},{5,1},{6,2},{7,3},{8,12},{9,13},{10,... | collective-permute-start | bytes 393224 | tf_op jit(solution)/shard_map/ppermute | solution.py:408
  13.7 5.5 %collective-permute-start.2 = (bf16[2,3,2,16,256]{4,3,2,1,0:T(8,128)(2,1)S(1)}, bf16[2,3,2,16,256]{4,3,2,1,0:T(8,128)(2,1)S(1)}, u32[]{:S(2)}, u32[]{:S(2)}) collective-permute-start(bf16[2,3,2,16,256]{4,3,2,1,0:T(8,128)(2,1)S(1)} %pad_maximum_fusion.3), channel_id=1, source_target_pairs={{0,2},{1,3},{2,0},{3,1},{4,6},{5,7},{6,4},{7,5},{8,10},{9,11},{10,... | collective-permute-start | bytes 294920 | tf_op jit(solution)/shard_map/ppermute | solution.py:408
  17.3 8.3 %copy-start = (f32[32,32]{1,0:T(8,128)S(1)}, f32[32,32]{1,0:T(8,128)}, u32[]{:S(2)}) copy-start(f32[32,32]{1,0:T(8,128)} %refs_4_.1) | copy-start | bytes 12292
  17.4 8.3 %copy-start.1 = (f32[32,32]{1,0:T(8,128)S(1)}, f32[32,32]{1,0:T(8,128)}, u32[]{:S(2)}) copy-start(f32[32,32]{1,0:T(8,128)} %refs_5_.1) | copy-start | bytes 12292
  17.4 6.4 %collective-permute-start.9 = (f32[8,2,16,256]{3,2,1,0:T(8,128)S(1)}, f32[8,2,16,256]{3,2,1,0:T(8,128)S(1)}, u32[]{:S(2)}, u32[]{:S(2)}) collective-permute-start(f32[8,2,16,256]{3,2,1,0:T(8,128)S(1)} %pad_maximum_fusion.refs_0_), channel_id=1, source_target_pairs={{0,2},{1,17},{2,0},{3,19},{4,6},{5,21},{6,4},{7,23},{8,10},{9,25},... | collective-permute-start | bytes 786440 | tf_op jit(solution)/shard_map/ppermute | solution.py:408
  19.2 5.7 %collective-permute-start.3 = (bf16[4,3,2,16,256]{4,3,2,1,0:T(8,128)(2,1)S(1)}, bf16[4,3,2,16,256]{4,3,2,1,0:T(8,128)(2,1)S(1)}, u32[]{:S(2)}, u32[]{:S(2)}) collective-permute-start(bf16[4,3,2,16,256]{4,3,2,1,0:T(8,128)(2,1)S(1)} %pad_maximum_fusion.1.refs_2_), channel_id=1, source_target_pairs={{0,4},{1,5},{2,6},{3,7},{4,0},{5,1},{6,2},{7,3},{8,12},{9,13},{10,... | collective-permute-start | bytes 589832 | tf_op jit(solution)/shard_map/ppermute | solution.py:408
  19.7 5.9 %collective-permute-start.7 = (f32[8,2,16,256]{3,2,1,0:T(8,128)S(1)}, f32[8,2,16,256]{3,2,1,0:T(8,128)S(1)}, u32[]{:S(2)}, u32[]{:S(2)}) collective-permute-start(f32[8,2,16,256]{3,2,1,0:T(8,128)S(1)} %pad_maximum_fusion.refs_0_), channel_id=1, source_target_pairs={{0,1},{1,0},{2,3},{3,2},{4,5},{5,4},{6,7},{7,6},{8,9},{9,8},{10,11... | collective-permute-start | bytes 786440 | tf_op jit(solution)/shard_map/ppermute | solution.py:408
  23.8 2.9 %collective-permute-start.10 = (f32[8,2,16,256]{3,2,1,0:T(8,128)S(1)}, f32[8,2,16,256]{3,2,1,0:T(8,128)S(1)}, u32[]{:S(2)}, u32[]{:S(2)}) collective-permute-start(f32[8,2,16,256]{3,2,1,0:T(8,128)S(1)} %collective-permute-done.9.refs_0_), channel_id=1, source_target_pairs={{0,1},{1,0},{2,3},{3,2},{4,5},{5,4},{6,7},{7,6},{8,9},{9,8},{10,11... | collective-permute-start | bytes 786440 | tf_op jit(solution)/shard_map/ppermute | solution.py:408
  23.8 1.8 %collective-permute-start.8 = (bf16[4,3,2,16,256]{4,3,2,1,0:T(8,128)(2,1)S(1)}, bf16[4,3,2,16,256]{4,3,2,1,0:T(8,128)(2,1)S(1)}, u32[]{:S(2)}, u32[]{:S(2)}) collective-permute-start(bf16[4,3,2,16,256]{4,3,2,1,0:T(8,128)(2,1)S(1)} %pad_maximum_fusion.1.refs_2_), channel_id=1, source_target_pairs={{0,1},{1,0},{2,3},{3,2},{4,5},{5,4},{6,7},{7,6},{8,9},{9,8},{10,11... | collective-permute-start | bytes 589832 | tf_op jit(solution)/shard_map/ppermute | solution.py:408
  24.9 2.4 %collective-permute-start.4 = (bf16[4,3,2,16,256]{4,3,2,1,0:T(8,128)(2,1)S(1)}, bf16[4,3,2,16,256]{4,3,2,1,0:T(8,128)(2,1)S(1)}, u32[]{:S(2)}, u32[]{:S(2)}) collective-permute-start(bf16[4,3,2,16,256]{4,3,2,1,0:T(8,128)(2,1)S(1)} %collective-permute-done.3.refs_0_), channel_id=1, source_target_pairs={{0,1},{1,0},{2,3},{3,2},{4,5},{5,4},{6,7},{7,6},{8,9},{9,8},{10,11... | collective-permute-start | bytes 589832 | tf_op jit(solution)/shard_map/ppermute | solution.py:408
